TPU v7x, 32 devices: a whole 2x2x4 slice. The times are simulated.
32 devices in a mesh: dp: 8 (over y, x, core), mp: 4 (over z).
Axes of the slice: x: 2, y: 2, z: 4, core: 2. Of those that a mesh axis runs over, the one named last changes fastest.
Arguments:
- tokens: bfloat16 [32, 512, 768], P('dp'), may hold values from -6 to 6
- doc_lengths: int32 [32, 4], P('dp'), may hold values from 1 to 256, 512 in all within a row
- w_query: bfloat16 [768, 768], P(None, 'mp'), may hold values from -0.21875 to 0.21875
- b_query: bfloat16 [768], P('mp'), may hold values from -3 to 3
- w_key: bfloat16 [768, 768], P(None, 'mp'), may hold values from -0.21875 to 0.21875
- w_value: bfloat16 [768, 768], P(None, 'mp'), may hold values from -0.21875 to 0.21875
- b_value: bfloat16 [768], P('mp'), may hold values from -3 to 3
- w_output: bfloat16 [768, 768], P('mp'), may hold values from -0.875 to 0.875
- b_output: bfloat16 [768], replicated, may hold values from -3 to 3
- gain_attn: bfloat16 [768], replicated, may hold values from 0.5 to 1.5
- shift_attn: bfloat16 [768], replicated, may hold values from -2 to 2
- w_expand: bfloat16 [768, 3072], P(None, 'mp'), may hold values from -0.21875 to 0.21875
- b_expand: bfloat16 [3072], P('mp'), may hold values from -3 to 3
- w_reduce: bfloat16 [3072, 768], P('mp'), may hold values from -0.21875 to 0.21875
- b_reduce: bfloat16 [768], replicated, may hold values from -2 to 2
- gain_ffn: bfloat16 [768], replicated, may hold values from 0.5 to 1.5
- shift_ffn: bfloat16 [768], replicated, may hold values from -2 to 2
- cotangent: bfloat16 [32, 512, 768], P('dp'), may hold values from -6 to 6
Outputs:
- output: bfloat16 [32, 512, 768], P('dp')
- grad_tokens: bfloat16 [32, 512, 768], P('dp')
- grad_w_query: float32 [768, 768], P(None, 'mp')
- grad_b_query: float32 [768], P('mp')
- grad_w_key: float32 [768, 768], P(None, 'mp')
- grad_w_value: float32 [768, 768], P(None, 'mp')
- grad_b_value: float32 [768], P('mp')
- grad_w_output: float32 [768, 768], P('mp')
- grad_b_output: float32 [768], replicated
- grad_gain_attn: float32 [768], replicated
- grad_shift_attn: float32 [768], replicated
- grad_w_expand: float32 [768, 3072], P(None, 'mp')
- grad_b_expand: float32 [3072], P('mp')
- grad_w_reduce: float32 [3072, 768], P('mp')
- grad_b_reduce: float32 [768], replicated
- grad_gain_ffn: float32 [768], replicated
- grad_shift_ffn: float32 [768], replicated
Inputs may be any that keep to these rules, and one draw needn't show every extreme that they name: `doc_lengths`: the 4 lengths of a row sum to 512, and the largest of every row is 256.
All inputs are finite; a program needn't handle non-finite values.
Results may differ from a plain program's by a relative error of at most 0.014.
Values sent between devices are 32-bit elements; how exact they have to be, the bound alone decides.
No kernel may reach another device: no remote copies, remote signals or barrier semaphores. Data moves between devices by JAX's collectives and lax.ppermute only.
A program may use at most 128 MiB of HBM per device.

v0:
```python
import jax
import jax.numpy as jnp
from jax import lax
from jax.sharding import PartitionSpec as P

HD = 64


norm_eps = 1e-12
masked_score = -1000000000.0


def layer_norm(hidden, gain_vec, shift_vec):
    center = hidden - jnp.mean(hidden, axis=-1, keepdims=True)
    spread = jnp.mean(center * center, axis=-1, keepdims=True)
    return center * lax.rsqrt(spread + norm_eps) * gain_vec + shift_vec


def gelu_tanh(values):
    return jax.nn.gelu(values, approximate=True)


def segment_ids(doc_lengths, length):
    doc_ends = jnp.cumsum(doc_lengths, axis=-1)
    position = jnp.arange(length, dtype=jnp.int32)
    return jnp.sum((position[None, :, None] >= doc_ends[:, None, :]).astype(jnp.int32), axis=-1)


def masked_scores(queries, keys_row, segment):
    scores = jnp.einsum(
        "qhd,khd->hqk", queries, keys_row, preferred_element_type=jnp.float32
    ) * HD ** (-0.5)
    same_doc = segment[:, None] == segment[None, :]
    return jnp.where(same_doc[None], scores, masked_score)


def attend_forward(packed):
    queries, keys_row, values_row, segment = packed
    scores = masked_scores(queries, keys_row, segment)
    highest = jnp.max(scores, axis=-1, keepdims=True)
    exponent = jnp.exp(scores - highest)
    totals = jnp.sum(exponent, axis=-1, keepdims=True)
    attn_probs = exponent / totals
    log_total = highest[..., 0] + jnp.log(totals[..., 0])
    context = jnp.einsum(
        "hqk,khd->qhd",
        attn_probs.astype(jnp.bfloat16),
        values_row,
        preferred_element_type=jnp.float32,
    )
    return (context.astype(jnp.bfloat16), log_total, attn_probs)


def recomputed_probs(packed):
    queries, keys_row, values_row, segment, log_total, grad_context = packed
    return jnp.exp(masked_scores(queries, keys_row, segment) - log_total[..., None])


def attend_backward(packed, attn_probs):
    queries, keys_row, values_row, segment, log_total, grad_context = packed
    grad_probs = jnp.einsum(
        "qhd,khd->hqk", grad_context, values_row, preferred_element_type=jnp.float32
    )
    inner_sum = jnp.sum(attn_probs * grad_probs, axis=-1, keepdims=True)
    grad_scores = (attn_probs * (grad_probs - inner_sum)).astype(jnp.bfloat16)
    grad_query = jnp.einsum(
        "hqk,khd->qhd", grad_scores, keys_row, preferred_element_type=jnp.float32
    ) * HD ** (-0.5)
    grad_key = jnp.einsum(
        "hqk,qhd->khd", grad_scores, queries, preferred_element_type=jnp.float32
    ) * HD ** (-0.5)
    grad_value = jnp.einsum(
        "hqk,qhd->khd",
        attn_probs.astype(jnp.bfloat16),
        grad_context,
        preferred_element_type=jnp.float32,
    )
    return (
        grad_query.astype(jnp.bfloat16),
        grad_key.astype(jnp.bfloat16),
        grad_value.astype(jnp.bfloat16),
    )


def local(
    tokens,
    doc_lengths,
    w_query,
    b_query,
    w_key,
    w_value,
    b_value,
    w_output,
    b_output,
    gain_attn,
    shift_attn,
    w_expand,
    b_expand,
    w_reduce,
    b_reduce,
    gain_ffn,
    shift_ffn,
    cotangent,
):
    row_count, length, model_width = tokens.shape
    heads_local = w_query.shape[1] // HD
    token_count = row_count * length
    inputs = tokens.reshape(token_count, model_width)
    segment = segment_ids(doc_lengths, length)
    queries = (
        jnp.dot(inputs, w_query, preferred_element_type=jnp.float32) + b_query.astype(jnp.float32)
    ).astype(jnp.bfloat16)
    keys_all = jnp.dot(inputs, w_key, preferred_element_type=jnp.float32).astype(jnp.bfloat16)
    values_all = (
        jnp.dot(inputs, w_value, preferred_element_type=jnp.float32) + b_value.astype(jnp.float32)
    ).astype(jnp.bfloat16)
    head_split = (row_count, length, heads_local, HD)
    packed = (
        queries.reshape(head_split),
        keys_all.reshape(head_split),
        values_all.reshape(head_split),
        segment,
    )
    context, log_total = lax.map(lambda row_item: attend_forward(row_item)[:2], packed)
    context = context.reshape(token_count, heads_local * HD)
    attended = lax.psum(
        jnp.dot(context, w_output, preferred_element_type=jnp.float32), "mp"
    ) + b_output.astype(jnp.float32)
    residual_one = inputs.astype(jnp.float32) + attended
    normed, attn_norm_back = jax.vjp(
        layer_norm, residual_one, gain_attn.astype(jnp.float32), shift_attn.astype(jnp.float32)
    )
    normed_low = normed.astype(jnp.bfloat16)
    hidden = jnp.dot(normed_low, w_expand, preferred_element_type=jnp.float32) + b_expand.astype(
        jnp.float32
    )
    gelu_value, gelu_back = jax.vjp(gelu_tanh, hidden)
    active = gelu_value.astype(jnp.bfloat16)
    mixed_out = lax.psum(
        jnp.dot(active, w_reduce, preferred_element_type=jnp.float32), "mp"
    ) + b_reduce.astype(jnp.float32)
    residual_two = normed + mixed_out
    output, ffn_norm_back = jax.vjp(
        layer_norm, residual_two, gain_ffn.astype(jnp.float32), shift_ffn.astype(jnp.float32)
    )
    grad_output = cotangent.reshape(token_count, model_width).astype(jnp.float32)
    grad_two, grad_gain_ffn, grad_shift_ffn = ffn_norm_back(grad_output)
    grad_two_low = grad_two.astype(jnp.bfloat16)
    grad_b_reduce = jnp.sum(grad_two, axis=0)
    grad_w_reduce = jnp.einsum(
        "tf,td->fd", active, grad_two_low, preferred_element_type=jnp.float32
    )
    grad_active = jnp.einsum(
        "td,fd->tf", grad_two_low, w_reduce, preferred_element_type=jnp.float32
    )
    grad_hidden = gelu_back(grad_active)[0].astype(jnp.bfloat16)
    grad_b_expand = jnp.sum(grad_hidden.astype(jnp.float32), axis=0)
    grad_w_expand = jnp.einsum(
        "td,tf->df", normed_low, grad_hidden, preferred_element_type=jnp.float32
    )
    grad_normed = grad_two + lax.psum(
        jnp.einsum("tf,df->td", grad_hidden, w_expand, preferred_element_type=jnp.float32), "mp"
    )
    grad_one, grad_gain_attn, grad_shift_attn = attn_norm_back(grad_normed)
    grad_b_output = jnp.sum(grad_one, axis=0)
    grad_one_low = grad_one.astype(jnp.bfloat16)
    grad_w_output = jnp.einsum(
        "tc,td->cd", context, grad_one_low, preferred_element_type=jnp.float32
    )
    grad_context = jnp.einsum(
        "td,cd->tc", grad_one_low, w_output, preferred_element_type=jnp.float32
    ).astype(jnp.bfloat16)
    packed_back = packed + (log_total, grad_context.reshape(head_split))
    grad_query, grad_key, grad_value = lax.map(
        lambda row_item: attend_backward(row_item, recomputed_probs(row_item)), packed_back
    )
    grad_query = grad_query.reshape(token_count, heads_local * HD)
    grad_key = grad_key.reshape(token_count, heads_local * HD)
    grad_value = grad_value.reshape(token_count, heads_local * HD)
    grad_b_query = jnp.sum(grad_query.astype(jnp.float32), axis=0)
    grad_b_value = jnp.sum(grad_value.astype(jnp.float32), axis=0)
    grad_w_query = jnp.einsum("td,tc->dc", inputs, grad_query, preferred_element_type=jnp.float32)
    grad_w_key = jnp.einsum("td,tc->dc", inputs, grad_key, preferred_element_type=jnp.float32)
    grad_w_value = jnp.einsum("td,tc->dc", inputs, grad_value, preferred_element_type=jnp.float32)
    back_terms = jnp.einsum("tc,dc->td", grad_query, w_query, preferred_element_type=jnp.float32)
    back_terms = back_terms + jnp.einsum(
        "tc,dc->td", grad_key, w_key, preferred_element_type=jnp.float32
    )
    back_terms = back_terms + jnp.einsum(
        "tc,dc->td", grad_value, w_value, preferred_element_type=jnp.float32
    )
    grad_inputs = grad_one + lax.psum(back_terms, "mp")
    summed = lax.psum(
        (
            grad_w_query,
            grad_b_query,
            grad_w_key,
            grad_w_value,
            grad_b_value,
            grad_w_output,
            grad_b_output,
            grad_gain_attn,
            grad_shift_attn,
            grad_w_expand,
            grad_b_expand,
            grad_w_reduce,
            grad_b_reduce,
            grad_gain_ffn,
            grad_shift_ffn,
        ),
        "dp",
    )
    (
        grad_w_query,
        grad_b_query,
        grad_w_key,
        grad_w_value,
        grad_b_value,
        grad_w_output,
        grad_b_output,
        grad_gain_attn,
        grad_shift_attn,
    ) = summed[:9]
    grad_w_expand, grad_b_expand, grad_w_reduce, grad_b_reduce, grad_gain_ffn, grad_shift_ffn = (
        summed[9:]
    )
    return (
        output.astype(jnp.bfloat16).reshape(row_count, length, model_width),
        grad_inputs.astype(jnp.bfloat16).reshape(row_count, length, model_width),
        grad_w_query,
        grad_b_query,
        grad_w_key,
        grad_w_value,
        grad_b_value,
        grad_w_output,
        grad_b_output,
        grad_gain_attn,
        grad_shift_attn,
        grad_w_expand,
        grad_b_expand,
        grad_w_reduce,
        grad_b_reduce,
        grad_gain_ffn,
        grad_shift_ffn,
    )


def solution(mesh):
    placed = (
        P("dp", None, None),
        P("dp", None),
        P(None, "mp"),
        P("mp"),
        P(None, "mp"),
        P(None, "mp"),
        P("mp"),
        P("mp", None),
        P(),
        P(),
        P(),
        P(None, "mp"),
        P("mp"),
        P("mp", None),
        P(),
        P(),
        P(),
        P("dp", None, None),
    )
    return jax.shard_map(
        local,
        mesh=mesh,
        in_specs=placed,
        out_specs=(
            P("dp", None, None),
            P("dp", None, None),
            P(None, "mp"),
            P("mp"),
            P(None, "mp"),
            P(None, "mp"),
            P("mp"),
            P("mp", None),
            P(),
            P(),
            P(),
            P(None, "mp"),
            P("mp"),
            P("mp", None),
            P(),
            P(),
            P(),
        ),
        check_vma=False,
    )
```

profile of v0, /device:TPU:0, one launch (start us, length us, event | category | flops | bytes accessed | tf_op | source)
XLA Modules:
  0.0 1190.5 jit_solution(14834933972039977539)
XLA Ops:
  13.4 3.1 fusion.67
  17.3 3.1 convolution_convert_fusion.1
  24.0 16.3 %while.26 = (s32[]{:T(128)}, bf16[4,512,3,64]{1,3,2,0:T(8,128)(2,1)}, f32[4,3,512]{2,1,0:T(4,128)}, bf16[4,512,3,64]{1,3,2,0:T(8,128)(2,1)S(1)}, s32[4,512]{1,0:...) while((s32[]{:T(128)}, ...), condition=%wide.region_5.6_spmd, body=%wide.region_2.5_spmd.sunk | while | flops 211122688 | bytes 11335781 | solution.py:124
  42.6 4.7 fusion.77
  50.7 222.3 %all-reduce.8.cloned.1.call-done = f32[2048,768]{1,0:T(8,128)} async-done(((f32[2048,768]{1,0:T(8,128)}), f32[2048,768]{1,0:T(8,128)}) %all-reduce.8.cloned.1.call-update) | async-done | bytes 6291472 | tf_op jit(solution)/shard_map/psum | solution.py:126
  273.0 4.6 fusion.76
  280.3 5.3 multiply_convert_fusion.1
  287.4 4.5 fusion.78
  295.8 218.1 %all-reduce.10.cloned.1.call-done = f32[2048,768]{1,0:T(8,128)} async-done(((f32[2048,768]{1,0:T(8,128)}), f32[2048,768]{1,0:T(8,128)}) %all-reduce.10.cloned.1.call-update) | async-done | bytes 6291472 | tf_op jit(solution)/shard_map/psum | solution.py:139
  513.8 5.7 fusion.75
  524.6 4.3 fusion.74
  528.9 7.5 convert_reduce_fusion.1
  538.1 4.5 fusion.79
  543.0 221.7 %all-reduce.12.cloned.1.call-done = f32[2048,768]{1,0:T(8,128)} async-done(((f32[2048,768]{1,0:T(8,128)}), f32[2048,768]{1,0:T(8,128)}) %all-reduce.12.cloned.1.call-update) | async-done | bytes 6291472 | tf_op jit(solution)/shard_map/psum | solution.py:161
  764.6 8.1 multiply_reduce_fusion.1
  772.8 4.3 fusion.73
  786.7 35.2 %while.27 = (s32[]{:T(128)}, bf16[4,512,3,64]{1,3,2,0:T(8,128)(2,1)}, bf16[4,512,3,64]{1,3,2,0:T(8,128)(2,1)}, bf16[4,512,3,64]{1,3,2,0:T(8,128)(2,1)}, bf16[4,5...) while((s32[]{:T(128)}, ...), condition=%wide.region_19.20_spmd, body=%wide.region_17.19_spmd.sunk | while | flops 511146496 | bytes 26127484 | solution.py:174
  828.8 3.7 add_add_fusion.2
  832.9 7.1 fusion.82
  839.9 7.2 fusion.70
  857.1 197.5 %all-reduce.14.cloned.1.call-done = f32[2048,768]{1,0:T(8,128)} async-done(((f32[2048,768]{1,0:T(8,128)}), f32[2048,768]{1,0:T(8,128)}) %all-reduce.14.cloned.1.call-update) | async-done | bytes 6291472 | tf_op jit(solution)/shard_map/psum | solution.py:192
  1054.5 6.8 add_reduce_fusion
  1061.3 26.0 %all-reduce = (f32[192]{0:T(256)}, f32[192]{0:T(256)}, f32[768]{0:T(1024)}, f32[768]{0:T(1024)}, f32[768]{0:T(1024)}, /*index=5*/f32[768]{0:T(1024)}, f32[768]{0:T(1024)}, f32[768]{0:T(1024)}, f32[768]{0:T(1024)}) all-reduce(f32[192]{0:T(256)S(1)} %reduce_sum.226, f32[192]{0:T(256)S(1)} %reduce_sum.228, ...), channel_id=1, replica_groups=mesh['dp'=8,'mp'=4] {'dp'}, use_global_device_ids=true, to_apply=%region_23.24 | all-reduce | flops 5760 | bytes 46080 | tf_op jit(solution)/shard_map/psum | solution.py:193
  1087.4 85.5 %all-reduce.16.cloned.1.call-done = (f32[768,192]{0,1:T(8,128)}, f32[768,192]{0,1:T(8,128)}, f32[768,192]{0,1:T(8,128)}, f32[192,768]{1,0:T(8,128)}, f32[768,768]{1,0:T(8,128)}, /*index=5*/f32[768,768]{1,0:T(8,128)}) async-done(((f32[768,192]{0,1:T(8,128)}, f32[768,192]{0,1:T(8,128)}, f32[768,192]{0,1:T(8,128)}, f32[192,768]{1,0:T(8,128)}, f32[768,768]{1,0:T(8,128)}, /*index=5*/f32[768,768]{1,0:T(8,128)}), ...) | async-done | bytes 7077904 | tf_op jit(solution)/shard_map/psum | solution.py:193
  (220 shorter events, 120.1 us)
Async XLA Ops:
  7.2 273.1 %copy-start = (bf16[768,768]{1,0:T(8,128)(2,1)S(1)}, bf16[768,768]{1,0:T(8,128)(2,1)}, u32[]{:S(2)}) copy-start(bf16[768,768]{1,0:T(8,128)(2,1)} %param.33) | copy-start | bytes 3538948
  7.2 265.8 %all-reduce.8.cloned.1.call-start = ((), (), s32[]{:S(2)}) async-start(), calls=%async_computation | async-start | bytes 12582912 | tf_op jit(solution)/shard_map/psum | solution.py:126
  40.4 6.9 copy-start.20
  42.6 5.5 copy-start.33
  47.3 466.5 %all-reduce.10.cloned.1.call-start = ((), (), s32[]{:S(2)}) async-start(), calls=%async_computation.1 | async-start | bytes 12582912 | tf_op jit(solution)/shard_map/psum | solution.py:139
  278.5 7.1 copy-start.21
  280.3 7.1 copy-start.34
  291.9 472.7 %all-reduce.12.cloned.1.call-start = ((), (), s32[]{:S(2)}) async-start(), calls=%async_computation.2 | async-start | bytes 12582912 | tf_op jit(solution)/shard_map/psum | solution.py:161
  521.5 7.4 slice-start.2
  528.9 7.5 copy-start.6
  528.9 7.5 copy-start.25
  542.6 222.0 %copy-start.19 = (f32[768]{0:T(1024)S(1)}, f32[768]{0:T(1024)}, u32[]{:S(2)}) copy-start(f32[768]{0:T(1024)} %convert_element_type.127) | copy-start | bytes 9220
  542.7 222.0 %copy-start.26 = (f32[2048]{0:T(1024)S(1)}, f32[2048]{0:T(1024)}, u32[]{:S(2)}) copy-start(f32[2048]{0:T(1024)} %copy-done.25) | copy-start | bytes 24580
  542.7 230.1 %copy-start.22 = (f32[2048]{0:T(1024)S(1)}, f32[2048]{0:T(1024)}, u32[]{:S(2)}) copy-start(f32[2048]{0:T(1024)} %copy-done.21) | copy-start | bytes 24580
  542.7 511.8 %all-reduce.14.cloned.1.call-start = ((), (), s32[]{:S(2)}) async-start(), calls=%async_computation.3 | async-start | bytes 12582912 | tf_op jit(solution)/shard_map/psum | solution.py:192
  772.8 6.9 copy-start.14
  832.6 340.3 %all-reduce.16.cloned.1.call-start = ((), (), s32[]{:S(2)}) async-start(), calls=%async_computation.4 | async-start | bytes 14155776 | tf_op jit(solution)/shard_map/psum | solution.py:193
  832.9 7.1 copy-start.38
  839.9 7.2 copy-start.4
  857.1 204.3 %copy-start.27 = (f32[768]{0:T(1024)S(1)}, f32[768]{0:T(1024)}, u32[]{:S(2)}) copy-start(f32[768]{0:T(1024)} %get-tuple-element.167) | copy-start | bytes 9220
  857.1 204.3 %copy-start.29 = (f32[768]{0:T(1024)S(1)}, f32[768]{0:T(1024)}, u32[]{:S(2)}) copy-start(f32[768]{0:T(1024)} %get-tuple-element.238) | copy-start | bytes 9220
  1172.8 7.9 copy-start.13
  1172.8 9.3 copy-start.12
  1172.8 10.7 copy-start.1
  (24 other events, 70.2 us)
Sparse Core Ops, SparseCore 0:
  47.4 225.5 all-reduce.7
  292.0 221.7 all-reduce.9
  542.8 221.7 all-reduce.11
  832.7 221.7 all-reduce.13
  1059.6 113.1 all-reduce.15
where the time goes:
time: 1200 us; the launch traced here: 1190 us
  waiting for transfers between devices  945 us (79%)
  matrix products  99.4 us (8%)
  other arithmetic  62.1 us (5%)
  local copies, waits for them, and re-layouts  42 us (4%)
  blocking collectives  26 us (2%)
  between operations  14.8 us (1%)
    psum x1, waiting for transfers between devices, local(): lax.psum(jnp.dot(context, w_output, preferred_element_type=jnp.float32),...  222 us
    psum x1, waiting for transfers between devices, local(): lax.psum(jnp.einsum('tf,df->td', grad_hidden, w_expand, preferred_element...  222 us
    psum x1, waiting for transfers between devices, local(): lax.psum(jnp.dot(active, w_reduce, preferred_element_type=jnp.float32), '...  218 us
    psum x1, waiting for transfers between devices, local(): grad_inputs = grad_one + lax.psum(back_terms, 'mp')  197 us
    psum x1, waiting for transfers between devices, local(): lax.psum((grad_w_query, grad_b_query, grad_w_key, grad_w_value, grad_b_va...  85.5 us
    psum x1, blocking collectives, local(): lax.psum((grad_w_query, grad_b_query, grad_w_key, grad_w_value, grad_b_va...  26 us
  transfers between devices with their start and end apart: 5, of which 5 were waited for; matrix products, arithmetic and copies ran while one was open for 3% of the time, Pallas kernels for 0%

commit v1 on v0

v1 whole, which is shorter than its diff:
```python
import jax
import jax.numpy as jnp
from jax import lax
from jax.experimental import pallas as pl
from jax.experimental.pallas import tpu as pltpu
from jax.sharding import PartitionSpec as P

HD = 64
GROUP = 8
EXTRA = 16
MASK = -float(2**30)
EPS = 1e-12
F32 = jnp.float32
BF16 = jnp.bfloat16
LIMIT = 60 << 20


def dot(left, right, left_dim, right_dim):
    return lax.dot_general(
        left, right, (((left_dim,), (right_dim,)), ((), ())), preferred_element_type=F32
    )


def params():
    return pltpu.CompilerParams(vmem_limit_bytes=LIMIT)


def cost(flops, moved):
    return pl.CostEstimate(flops=int(flops), bytes_accessed=int(moved), transcendentals=0)


def whole(shape):
    zeros = (0,) * len(shape)
    return pl.BlockSpec(shape, lambda *_: zeros, pipeline_mode=pl.Buffered(1))


def split3(row):
    high = row.astype(BF16).astype(F32)
    rest = row - high
    mid = rest.astype(BF16).astype(F32)
    return high, mid, rest - mid


def rows_of(height, first, parts, width):
    place = lax.broadcasted_iota(jnp.int32, (height, width), 0)
    out = jnp.zeros((height, width), F32)
    for i, part in enumerate(parts):
        out = jnp.where(place == first + i, part, out)
    return out


def assemble_small_kernel(place_ref, mine_ref, other_ref, out_ref):
    rows = mine_ref.shape[2]
    for rel in range(4):
        for source, ref in enumerate((mine_ref, other_ref)):
            start = pl.multiple_of(place_ref[2 * rel + source] * rows, rows)
            for k in range(mine_ref.shape[1]):
                out_ref[k, pl.ds(start, rows), :] = ref[rel, k].astype(BF16)


def assemble_small(place, mine, other):
    _, peers, rows, width = mine.shape
    return pl.pallas_call(
        assemble_small_kernel,
        grid_spec=pltpu.PrefetchScalarGridSpec(
            num_scalar_prefetch=1,
            grid=(1,),
            in_specs=[whole(mine.shape), whole(other.shape)],
            out_specs=whole((peers, GROUP * rows, width)),
        ),
        out_shape=jax.ShapeDtypeStruct((peers, GROUP * rows, width), BF16),
        compiler_params=params(),
        cost_estimate=cost(0, mine.size * 12),
        name="assemble_heads",
    )(place, mine, other)


def assemble_big_kernel(place_ref, own_ref, mine_ref, other_ref, out_ref):
    rows = mine_ref.shape[2]
    shards = out_ref.shape[0]
    me = place_ref[8]
    out_ref[me] = own_ref[...]
    for k in range(mine_ref.shape[1]):
        shard = lax.rem(me + shards - 1 - k, shards)
        for rel in range(4):
            for source, ref in enumerate((mine_ref, other_ref)):
                start = pl.multiple_of(place_ref[2 * rel + source] * rows, rows)
                out_ref[shard, pl.ds(start, rows), :] = ref[rel, k].astype(BF16)


def assemble_big(place, own, mine, other):
    _, peers, rows, width = mine.shape
    shape = (peers + 1,) + own.shape
    return pl.pallas_call(
        assemble_big_kernel,
        grid_spec=pltpu.PrefetchScalarGridSpec(
            num_scalar_prefetch=1,
            grid=(1,),
            in_specs=[whole(own.shape), whole(mine.shape), whole(other.shape)],
            out_specs=whole(shape),
        ),
        out_shape=jax.ShapeDtypeStruct(shape, BF16),
        compiler_params=params(),
        cost_estimate=cost(0, mine.size * 12),
        name="assemble_ffn",
    )(place, own, mine, other)


def attend_forward_kernel(length, x_ref, w_ref, bias_ref, qf_ref, kf_ref, qkv_ref, ctx_ref, aug_ref):
    tokens = x_ref.shape[0]
    proj = dot(w_ref[0, : 3 * HD, :], x_ref[...], 1, 1) + bias_ref[0]
    scale = HD ** (-0.5)
    qkv_ref[0, :HD, :] = (proj[:HD] * scale).astype(BF16)
    qkv_ref[0, HD:, :] = proj[HD:].astype(BF16)
    ones_rows = rows_of(EXTRA, 0, (jnp.ones((1, length), F32),), length).astype(BF16)

    def row(r, carry):
        at = pl.ds(pl.multiple_of(r * length, length), length)
        queries = jnp.concatenate([qkv_ref[0, :HD, at], qf_ref[:, at]], axis=0)
        keys = jnp.concatenate([qkv_ref[0, HD : 2 * HD, at], kf_ref[:, at]], axis=0)
        values = jnp.concatenate([qkv_ref[0, 2 * HD :, at], ones_rows], axis=0)
        scores = dot(keys, queries, 0, 0)
        highest = jnp.max(scores, axis=0, keepdims=True)
        weight = jnp.exp(scores - highest).astype(BF16)
        context = dot(values, weight, 1, 0)
        total = context[HD : HD + 1]
        ctx_ref[0, :, at] = (context[:HD] * (1.0 / total)).astype(BF16)
        log_total = highest + jnp.log(total)
        extra = rows_of(EXTRA, 4, split3(-log_total), length)
        aug_ref[0, :, at] = (extra + qf_ref[:, at].astype(F32)).astype(BF16)
        return carry

    lax.fori_loop(0, tokens // length, row, 0, unroll=2)


def attend_forward(length, inputs, weights, bias, qf, kf):
    heads, height, width = weights.shape
    tokens = inputs.shape[0]
    by_head = lambda *shape: pl.BlockSpec((1,) + shape, lambda h: (h, 0, 0))
    return pl.pallas_call(
        lambda *refs: attend_forward_kernel(length, *refs),
        grid=(heads,),
        in_specs=[
            whole(inputs.shape),
            by_head(height, width),
            by_head(3 * HD, 1),
            whole(qf.shape),
            whole(kf.shape),
        ],
        out_specs=[by_head(3 * HD, tokens), by_head(HD, tokens), by_head(EXTRA, tokens)],
        out_shape=[
            jax.ShapeDtypeStruct((heads, 3 * HD, tokens), BF16),
            jax.ShapeDtypeStruct((heads, HD, tokens), BF16),
            jax.ShapeDtypeStruct((heads, EXTRA, tokens), BF16),
        ],
        compiler_params=params(),
        cost_estimate=cost(heads * tokens * (6 * HD * width + 16 * 64 * length), 12e6),
        name="attend_forward",
    )(inputs, weights, bias, qf, kf)


def attend_backward_kernel(length, qkv_ref, ctx_ref, aug_ref, grad_ref, kf_ref, out_ref):
    tokens = kf_ref.shape[1]
    scale = HD ** (-0.5)
    one = jnp.ones((1, length), F32)
    ones_rows = rows_of(EXTRA, 0, (one, one, one), length).astype(BF16)

    def row(r, carry):
        at = pl.ds(pl.multiple_of(r * length, length), length)
        queries = qkv_ref[0, :HD, at]
        keys = qkv_ref[0, HD : 2 * HD, at]
        values = qkv_ref[0, 2 * HD :, at]
        grad_context = grad_ref[0, :, at]
        inner = jnp.sum(
            grad_context.astype(F32) * ctx_ref[0, :, at].astype(F32), axis=0, keepdims=True
        )
        grad_extra = rows_of(EXTRA, 0, split3(-inner), length).astype(BF16)
        scores = dot(
            jnp.concatenate([keys, kf_ref[:, at]], axis=0),
            jnp.concatenate([queries, aug_ref[0, :, at]], axis=0),
            0,
            0,
        )
        probs = jnp.exp(scores)
        spread = dot(
            jnp.concatenate([values, ones_rows], axis=0),
            jnp.concatenate([grad_context, grad_extra], axis=0),
            0,
            0,
        )
        grad_scores = (probs * spread).astype(BF16)
        out_ref[0, 2 * HD :, at] = dot(grad_context, probs.astype(BF16), 1, 1).astype(BF16)
        out_ref[0, HD : 2 * HD, at] = dot(queries, grad_scores, 1, 1).astype(BF16)
        out_ref[0, :HD, at] = (dot(keys, grad_scores, 1, 0) * scale).astype(BF16)
        return carry

    lax.fori_loop(0, tokens // length, row, 0, unroll=2)


def attend_backward(length, qkv, ctx, aug, grad, kf):
    heads, _, tokens = qkv.shape
    by_head = lambda *shape: pl.BlockSpec((1,) + shape, lambda h: (h, 0, 0))
    return pl.pallas_call(
        lambda *refs: attend_backward_kernel(length, *refs),
        grid=(heads,),
        in_specs=[
            by_head(3 * HD, tokens),
            by_head(HD, tokens),
            by_head(EXTRA, tokens),
            by_head(HD, tokens),
            whole(kf.shape),
        ],
        out_specs=by_head(3 * HD, tokens),
        out_shape=jax.ShapeDtypeStruct((heads, 3 * HD, tokens), BF16),
        compiler_params=params(),
        cost_estimate=cost(heads * tokens * 40 * 64 * length, 12e6),
        name="attend_backward",
    )(qkv, ctx, aug, grad, kf)


def norm_forward(hidden):
    center = hidden - jnp.mean(hidden, axis=-1, keepdims=True)
    inverse = lax.rsqrt(jnp.mean(center * center, axis=-1, keepdims=True) + EPS)
    return center * inverse, inverse


def norm_backward(grad, gain, norm, inverse):
    scaled = grad * gain
    first = jnp.mean(scaled, axis=-1, keepdims=True)
    second = jnp.mean(scaled * norm, axis=-1, keepdims=True)
    return (scaled - first - norm * second) * inverse


def column_sum(values):
    return jnp.sum(values, axis=0, keepdims=True)


def dense_kernel(
    local_heads,
    place_ref,
    x_ref,
    cot_ref,
    ctx_own_ref,
    ctx_refs,
    wo_own_ref,
    wo_refs,
    we_ref,
    wr_ref,
    bias_ref,
    vec_ref,
    out_ref,
    g1_ref,
    dctx_own_ref,
    dctx_refs,
    dwe_ref,
    dwr_ref,
    dwo_ref,
    small_ref,
    wo_scr,
    ctx_scr,
    act_scr,
    slope_scr,
    gh_scr,
    dctx_scr,
):
    step = pl.program_id(0)
    shards = we_ref.shape[0]
    me = place_ref[8]
    span = local_heads * HD

    def start_of(k, j):
        shard = lax.rem(me + shards - k, shards)
        return pl.multiple_of(shard * span + j * HD, HD)

    @pl.when(step == 0)
    def _():
        for j in range(local_heads):
            wo_scr[pl.ds(start_of(0, j), HD), :] = wo_own_ref[j]
            for k in range(1, shards):
                wo_scr[pl.ds(start_of(k, j), HD), :] = wo_refs[j][k - 1]
        dwe_ref[...] = jnp.zeros_like(dwe_ref)
        dwr_ref[...] = jnp.zeros_like(dwr_ref)
        dwo_ref[...] = jnp.zeros_like(dwo_ref)
        small_ref[...] = jnp.zeros_like(small_ref)

    for j in range(local_heads):
        ctx_scr[pl.ds(start_of(0, j), HD), :] = ctx_own_ref[j]
        for k in range(1, shards):
            ctx_scr[pl.ds(start_of(k, j), HD), :] = ctx_refs[j][k - 1]

    b_output, gain_one, shift_one = vec_ref[0:1], vec_ref[1:2], vec_ref[2:3]
    b_reduce, gain_two, shift_two = vec_ref[3:4], vec_ref[4:5], vec_ref[5:6]

    attended = dot(ctx_scr[...], wo_scr[...], 0, 0) + b_output
    norm_one, inverse_one = norm_forward(x_ref[...].astype(F32) + attended)
    normed = norm_one * gain_one + shift_one
    normed_low = normed.astype(BF16)

    mixed = jnp.zeros_like(normed)
    for s in range(shards):
        b_expand = bias_ref[lax.rem(me + shards - s, shards), 1:2]
        hidden = dot(normed_low, we_ref[s], 1, 0) + b_expand
        square = hidden * hidden
        inner = 0.7978845608028654 * (hidden + 0.044715 * hidden * square)
        bent = jnp.tanh(inner)
        half = 0.5 * (1.0 + bent)
        active = (hidden * half).astype(BF16)
        act_scr[s] = active
        slope_scr[s] = half + 0.5 * hidden * (1.0 - bent * bent) * (
            0.7978845608028654 * (1.0 + 0.134145 * square)
        )
        mixed = mixed + dot(active, wr_ref[s], 1, 0)

    norm_two, inverse_two = norm_forward(normed + (mixed + b_reduce))
    out_ref[...] = (norm_two * gain_two + shift_two).astype(BF16)

    cot = cot_ref[...].astype(F32)
    grad_two = norm_backward(cot, gain_two, norm_two, inverse_two)
    grad_two_low = grad_two.astype(BF16)

    grad_normed = grad_two
    for s in range(shards):
        grad_active = dot(grad_two_low, wr_ref[s], 1, 1)
        grad_hidden = (grad_active * slope_scr[s]).astype(BF16)
        gh_scr[s] = grad_hidden
        grad_normed = grad_normed + dot(grad_hidden, we_ref[s], 1, 1)

    own = gh_scr[me]
    dwr_ref[...] += dot(act_scr[me], grad_two_low, 0, 0)
    dwe_ref[...] += dot(normed_low, own, 0, 0)

    grad_one = norm_backward(grad_normed, gain_one, norm_one, inverse_one)
    grad_one_low = grad_one.astype(BF16)
    g1_ref[...] = grad_one
    for j in range(local_heads):
        dwo_ref[j] += dot(ctx_own_ref[j], grad_one_low, 1, 0)
    dctx_scr[...] = dot(wo_scr[...], grad_one_low, 1, 1).astype(BF16)
    for j in range(local_heads):
        dctx_own_ref[j] = dctx_scr[pl.ds(start_of(0, j), HD), :]
        for k in range(1, shards):
            dctx_refs[j][k - 1] = dctx_scr[pl.ds(start_of(k, j), HD), :]

    small_ref[0:1] += column_sum(grad_one)
    small_ref[1:2] += column_sum(grad_normed * norm_one)
    small_ref[2:3] += column_sum(grad_normed)
    small_ref[3:4] += column_sum(grad_two)
    small_ref[4:5] += column_sum(cot * norm_two)
    small_ref[5:6] += column_sum(cot)
    small_ref[6:7] += column_sum(own.astype(F32))


def dense(place, inputs, cot, ctx_sets, weight_sets, w_expand, w_reduce, biases, vectors):
    tokens, width = inputs.shape
    shards, _, hidden = w_expand.shape
    local_heads = ctx_sets[0].shape[0]
    block = 256
    by_token = lambda: pl.BlockSpec((block, width), lambda i, *_: (i, 0))
    columns = lambda a: pl.BlockSpec((a.shape[0], HD, block), lambda i, *_: (0, 0, i))
    wo_spec = lambda a: pl.BlockSpec(
        (a.shape[0], HD, width), lambda i, *_: (0, 3, 0), pipeline_mode=pl.Buffered(1)
    )
    n = local_heads

    def body(place_ref, *refs):
        refs = list(refs)
        take = lambda count: [refs.pop(0) for _ in range(count)]
        x_ref, cot_ref, ctx_own = take(3)
        ctx_refs = take(n)
        (wo_own,) = take(1)
        wo_refs = take(n)
        we_ref, wr_ref, bias_ref, vec_ref, out_ref, g1_ref, dctx_own = take(7)
        dctx_refs = take(n)
        dense_kernel(
            n,
            place_ref,
            x_ref,
            cot_ref,
            ctx_own,
            ctx_refs,
            wo_own,
            wo_refs,
            we_ref,
            wr_ref,
            bias_ref,
            vec_ref,
            out_ref,
            g1_ref,
            dctx_own,
            dctx_refs,
            *refs,
        )

    shapes = [
        jax.ShapeDtypeStruct((tokens, width), BF16),
        jax.ShapeDtypeStruct((tokens, width), F32),
        *[jax.ShapeDtypeStruct(a.shape, BF16) for a in ctx_sets],
        jax.ShapeDtypeStruct((width, hidden), F32),
        jax.ShapeDtypeStruct((hidden, width), F32),
        jax.ShapeDtypeStruct((n, HD, width), F32),
        jax.ShapeDtypeStruct((8, width), F32),
    ]
    return pl.pallas_call(
        body,
        grid_spec=pltpu.PrefetchScalarGridSpec(
            num_scalar_prefetch=1,
            grid=(tokens // block,),
            in_specs=[
                by_token(),
                by_token(),
                *[columns(a) for a in ctx_sets],
                *[wo_spec(a) for a in weight_sets],
                whole(w_expand.shape),
                whole(w_reduce.shape),
                whole(biases.shape),
                whole(vectors.shape),
            ],
            out_specs=[
                by_token(),
                by_token(),
                *[columns(a) for a in ctx_sets],
                whole((width, hidden)),
                whole((hidden, width)),
                whole((n, HD, width)),
                whole((8, width)),
            ],
            scratch_shapes=[
                pltpu.VMEM((shards * n * HD, width), BF16),
                pltpu.VMEM((shards * n * HD, block), BF16),
                pltpu.VMEM((shards, block, hidden), BF16),
                pltpu.VMEM((shards, block, hidden), F32),
                pltpu.VMEM((shards, block, hidden), BF16),
                pltpu.VMEM((shards * n * HD, block), BF16),
            ],
        ),
        out_shape=shapes,
        compiler_params=params(),
        cost_estimate=cost(tokens * width * (8 * shards + 8) * hidden, 30e6),
        name="dense_middle",
    )(place, inputs, cot, *ctx_sets, *weight_sets, w_expand, w_reduce, biases, vectors)


def own_grads_kernel(dqkv_ref, x_ref, out_ref, sum_ref):
    for j in range(dqkv_ref.shape[0]):
        out_ref[j] = dot(dqkv_ref[j], x_ref[...], 1, 0)
        sums = jnp.sum(dqkv_ref[j].astype(F32), axis=1, keepdims=True)
        sum_ref[j] = jnp.broadcast_to(sums, sum_ref.shape[1:])


def own_grads(dqkv, inputs):
    heads, height, tokens = dqkv.shape
    width = inputs.shape[1]
    return pl.pallas_call(
        own_grads_kernel,
        out_shape=[
            jax.ShapeDtypeStruct((heads, height, width), F32),
            jax.ShapeDtypeStruct((heads, height, 128), F32),
        ],
        compiler_params=params(),
        cost_estimate=cost(2 * heads * height * tokens * width, 8e6),
        name="own_grads",
    )(dqkv, inputs)


def input_grads_kernel(place_ref, g1_ref, *refs):
    step = pl.program_id(0)
    me = place_ref[8]
    sets = (len(refs) - 3) // 2
    grads, weights = refs[:sets], refs[sets : 2 * sets]
    out_ref, grad_scr, w_scr = refs[2 * sets :]
    heads = grads[0].shape[0]
    height = 3 * HD
    shards = grad_scr.shape[0] // (heads * height)

    def start_of(k, j):
        shard = lax.rem(me + shards - k, shards)
        return pl.multiple_of((shard * heads + j) * height, HD)

    @pl.when(step == 0)
    def _():
        for j in range(heads):
            w_scr[pl.ds(start_of(0, j), height), :] = weights[0][j, :height, :]
            for k in range(1, shards):
                w_scr[pl.ds(start_of(k, j), height), :] = weights[j + 1][k - 1, :height, :]

    for j in range(heads):
        grad_scr[pl.ds(start_of(0, j), height), :] = grads[0][j]
        for k in range(1, shards):
            grad_scr[pl.ds(start_of(k, j), height), :] = grads[j + 1][k - 1]
    out_ref[...] = (g1_ref[...] + dot(grad_scr[...], w_scr[...], 0, 0)).astype(BF16)


def input_grads(place, grad_one, grad_sets, weight_sets):
    tokens, width = grad_one.shape
    block = 256
    count = sum(a.shape[0] for a in grad_sets) * 3 * HD
    by_token = lambda: pl.BlockSpec((block, width), lambda i, *_: (i, 0))
    return pl.pallas_call(
        input_grads_kernel,
        grid_spec=pltpu.PrefetchScalarGridSpec(
            num_scalar_prefetch=1,
            grid=(tokens // block,),
            in_specs=[
                by_token(),
                *[
                    pl.BlockSpec((a.shape[0], 3 * HD, block), lambda i, *_: (0, 0, i))
                    for a in grad_sets
                ],
                *[whole(a.shape) for a in weight_sets],
            ],
            out_specs=by_token(),
            scratch_shapes=[pltpu.VMEM((count, block), BF16), pltpu.VMEM((count, width), BF16)],
        ),
        out_shape=jax.ShapeDtypeStruct((tokens, width), BF16),
        compiler_params=params(),
        cost_estimate=cost(2 * tokens * width * count, 20e6),
        name="input_grads",
    )(place, grad_one, *grad_sets, *weight_sets)


def solution(mesh):
    peers = mesh.shape["mp"]
    lanes = mesh.shape["dp"]
    rotations = [[(i, (i + k) % peers) for i in range(peers)] for k in range(1, peers)]
    flips = lambda bit: [(i, i ^ bit) for i in range(lanes)]

    def flip(values, bit):
        return lax.ppermute(values, "dp", flips(bit))

    def gather(piece):
        mine = jnp.stack([lax.ppermute(piece, "mp", perm) for perm in rotations])
        half = piece.shape[0] // 2
        by_x, by_y = flip(mine, 2), flip(mine, 4)
        first, second = flip(by_y[:, :half], 2), flip(by_x[:, half:], 4)
        mine = jnp.stack([mine, by_x, by_y, jnp.concatenate([first, second], axis=1)])
        return mine, flip(mine, 1)

    def sum_over_dp(values, index):
        def part(array, bit_set):
            size = array.shape[0] // 2
            return lax.dynamic_slice_in_dim(array, bit_set * size, size, 0)

        bit = lambda b: jnp.where((index & b) != 0, 1, 0)

        def scatter(array, b):
            return part(array, bit(b)) + flip(part(array, 1 - bit(b)), b)

        def collect(array, b):
            other = flip(array, b)
            low = jnp.where(bit(b) == 0, array, other)
            high = jnp.where(bit(b) == 0, other, array)
            return jnp.concatenate([low, high], axis=0)

        chip = scatter(values, 1)
        half = chip.shape[0] // 2
        first, second = chip[:half], chip[half:]
        first, second = scatter(first, 2), scatter(second, 4)
        first, second = scatter(first, 4), scatter(second, 2)
        step = GROUP
        while step < lanes:
            first = first + flip(first, step)
            second = second + flip(second, step)
            step *= 2
        first, second = collect(first, 4), collect(second, 2)
        first, second = collect(first, 2), collect(second, 4)
        return collect(jnp.concatenate([first, second], axis=0), 1)

    def local(
        tokens,
        doc_lengths,
        w_query,
        b_query,
        w_key,
        w_value,
        b_value,
        w_output,
        b_output,
        gain_attn,
        shift_attn,
        w_expand,
        b_expand,
        w_reduce,
        b_reduce,
        gain_ffn,
        shift_ffn,
        cotangent,
    ):
        row_count, length, width = tokens.shape
        heads = w_query.shape[1] // HD
        count = row_count * length
        inputs = tokens.reshape(count, width)
        cot = cotangent.reshape(count, width)
        index = lax.axis_index("dp")
        me = lax.axis_index("mp")
        inside = index % GROUP
        place = jnp.stack(
            [inside ^ flipped for rel in (0, 2, 4, 6) for flipped in (rel, rel ^ 1)] + [me]
        ).astype(jnp.int32)

        by_head = lambda w: w.T.reshape(heads, HD, width)
        own_heads = jnp.concatenate(
            [by_head(w_query), by_head(w_key), by_head(w_value), w_output.reshape(heads, HD, width)],
            axis=1,
        )
        blank = jnp.zeros((width - 2 * heads * HD,), BF16)
        own_bias = jnp.stack(
            [jnp.concatenate([b_query, b_value, blank]), b_expand]
            + [jnp.zeros((width,), BF16)] * 6
        ).astype(F32)

        def piece_of(array):
            size = array.shape[0] // GROUP
            return lax.dynamic_slice_in_dim(array, inside * size, size, 0).astype(F32)

        peer_bias = [lax.ppermute(own_bias, "mp", perm) for perm in rotations]
        gathered = [gather(piece_of(own_heads[j])) for j in range(heads)]
        gathered_expand = gather(piece_of(w_expand))
        gathered_reduce = gather(piece_of(w_reduce))

        biases = jnp.stack([own_bias] + peer_bias)
        parts = biases[:, 0, : 2 * heads * HD].reshape(peers, 2, heads, HD)
        columns = jnp.concatenate(
            [parts[:, 0], jnp.zeros((peers, heads, HD), F32), parts[:, 1]], axis=-1
        )[..., None]

        ends = jnp.cumsum(doc_lengths, axis=-1)
        position = jnp.arange(length, dtype=jnp.int32)
        segment = jnp.sum((position[None, :, None] >= ends[:, None, :]).astype(jnp.int32), axis=-1)
        segment = segment.reshape(1, count)
        docs = doc_lengths.shape[1]
        label = jnp.arange(EXTRA, dtype=jnp.int32)[:, None]
        is_doc = label < docs
        qf = jnp.where(is_doc & (segment == label), 1.0, 0.0).astype(BF16)
        kf = jnp.where(
            is_doc,
            jnp.where(segment == label, 0.0, MASK),
            jnp.where(label < docs + 3, 1.0, 0.0),
        ).astype(BF16)

        forward = [attend_forward(length, inputs, own_heads, columns[0], qf, kf)]
        weight_sets = [own_heads]
        for j in range(heads):
            weights = assemble_small(place, *gathered[j])
            weight_sets.append(weights)
            forward.append(attend_forward(length, inputs, weights, columns[1:, j], qf, kf))
        all_expand = assemble_big(place, w_expand, *gathered_expand)
        all_reduce = assemble_big(place, w_reduce, *gathered_reduce)

        vectors = jnp.stack(
            [b_output, gain_attn, shift_attn, b_reduce, gain_ffn, shift_ffn]
            + [jnp.zeros((width,), BF16)] * 2
        ).astype(F32)
        results = dense(
            place,
            inputs,
            cot,
            [f[1] for f in forward],
            weight_sets,
            all_expand,
            all_reduce,
            biases,
            vectors,
        )
        output, grad_one = results[0], results[1]
        dctx = results[2 : 3 + heads]
        dwe, dwr, dwo, small = results[3 + heads :]

        first = jnp.concatenate([dwe, dwr, dwo.reshape(heads * HD, width), small], axis=0)
        first = jnp.pad(first, ((0, -first.shape[0] % 128), (0, 0)))
        first = sum_over_dp(first, inside)

        backward = [attend_backward(length, *forward[0], dctx[0], kf)]
        own_dw, own_sum = own_grads(backward[0], inputs)
        second = own_dw.reshape(heads * 3 * HD, width)
        bias_row = own_sum[:, :, 0].reshape(1, heads * 3 * HD)
        bias_row = jnp.pad(bias_row, ((0, 7), (0, width - heads * 3 * HD)))
        second = jnp.concatenate([second, bias_row], axis=0)
        second = jnp.pad(second, ((0, -second.shape[0] % 128), (0, 0)))
        second = sum_over_dp(second, inside)

        for j in range(heads):
            backward.append(attend_backward(length, *forward[j + 1], dctx[j + 1], kf))
        grad_tokens = input_grads(place, grad_one, backward, weight_sets)

        hidden = w_expand.shape[1]
        edge = width + hidden
        dwe, dwr = first[:width], first[width:edge]
        dwo, small = first[edge : edge + heads * HD], first[edge + heads * HD :]
        dqkv = second[: heads * 3 * HD].reshape(heads, 3, HD, width)
        dbias = second[heads * 3 * HD, : heads * 3 * HD].reshape(heads, 3, HD)
        turned = lambda i: dqkv[:, i].reshape(heads * HD, width).T
        flat = lambda i: dbias[:, i].reshape(heads * HD)
        shape = (row_count, length, width)
        return (
            output.reshape(shape),
            grad_tokens.reshape(shape),
            turned(0),
            flat(0),
            turned(1),
            turned(2),
            flat(2),
            dwo,
            small[0],
            small[1],
            small[2],
            dwe,
            small[6],
            dwr,
            small[3],
            small[4],
            small[5],
        )

    rows, split = P("dp", None, None), P(None, "mp")
    return jax.shard_map(
        local,
        mesh=mesh,
        in_specs=(
            rows,
            P("dp", None),
            split,
            P("mp"),
            split,
            split,
            P("mp"),
            P("mp", None),
            P(),
            P(),
            P(),
            split,
            P("mp"),
            P("mp", None),
            P(),
            P(),
            P(),
            rows,
        ),
        out_specs=(
            rows,
            rows,
            split,
            P("mp"),
            split,
            split,
            P("mp"),
            P("mp", None),
            P(),
            P(),
            P(),
            split,
            P("mp"),
            P("mp", None),
            P(),
            P(),
            P(),
        ),
        check_vma=False,
    )
```

time: 1200 us -> 503 us (0.42)
  waiting for transfers between devices: 945 us -> 131 us
  Pallas kernels: 0 us -> 221 us
  matrix products: 99.4 us -> 0 us
  starting transfers between devices: 0.84 us -> 63.3 us
  blocking collectives: 26 us -> 0 us
  other arithmetic: 62.1 us -> 43.5 us
  between operations: 14.8 us -> 1.8 us
    psum x5 -> x0, waiting for transfers between devices: 945 us -> none  [the longest x1 222 us: local(): lax.psum(jnp.dot(context, w_output, preferred_element_type=jnp.float32),...]
    pallas_call x0 -> x16, Pallas kernels: none -> 221 us  [the longest x1 78 us: dense(): pl.pallas_call(body, grid_spec=pltpu.PrefetchScalarGridSpec(num_scalar_pr...]
    ppermute x0 -> x63, waiting for transfers between devices: none -> 131 us  [the longest x45 67.3 us: flip(): return lax.ppermute(values, 'dp', flips(bit))]
    dot_general x46 -> x0, matrix products: 99.4 us -> none  [the longest x8 7.74 us: masked_scores(): jnp.einsum('qhd,khd->hqk', queries, keys_row, preferred_element_type=jnp....]
    ppermute x0 -> x63, starting transfers between devices: none -> 63.3 us  [the longest x45 42.9 us: flip(): return lax.ppermute(values, 'dp', flips(bit))]
    reduce_sum x16 -> x1, other arithmetic: 44.3 us -> 0.1 us  [local(): jnp.sum((position[None, :, None] >= ends[:, None, :]).astype(jnp.int32),...]
    psum x1 -> x0, blocking collectives: 26 us -> none  [local(): lax.psum((grad_w_query, grad_b_query, grad_w_key, grad_w_value, grad_b_va...]
    another operation x1 -> x17, other arithmetic: 0.85 us -> 17.6 us  [the longest x15 16.6 us: gather(): jnp.stack([mine, by_x, by_y, jnp.concatenate([first, second], axis=1)])]
  transfers between devices with their start and end apart: 5 -> 63, of which waited for: 5 -> 24; matrix products, arithmetic and copies ran while one was open for 3% -> 14% of each run, Pallas kernels for 0% -> 24%
where the time goes in v1:
time: 503 us; the launch traced here: 499 us
  Pallas kernels  221 us (44%)
  waiting for transfers between devices  131 us (26%)
  starting transfers between devices  63.3 us (13%)
  other arithmetic  43.5 us (9%)
  local copies, waits for them, and re-layouts  38.2 us (8%)
    pallas_call x1, Pallas kernels, dense(): pl.pallas_call(body, grid_spec=pltpu.PrefetchScalarGridSpec(num_scalar_pr...  78 us
    ppermute x45, waiting for transfers between devices, flip(): return lax.ppermute(values, 'dp', flips(bit))  67.3 us
    pallas_call x4, Pallas kernels, attend_forward(): pl.pallas_call(lambda *refs: attend_forward_kernel(length, *refs), grid=(...  53.7 us
    ppermute x15, waiting for transfers between devices, gather(): mine = jnp.stack([lax.ppermute(piece, 'mp', perm) for perm in rotations])  44.1 us
    pallas_call x4, Pallas kernels, attend_backward(): pl.pallas_call(lambda *refs: attend_backward_kernel(length, *refs), grid=...  43.6 us
    ppermute x45, starting transfers between devices, flip(): return lax.ppermute(values, 'dp', flips(bit))  42.9 us
    ppermute x3, waiting for transfers between devices, local(): peer_bias = [lax.ppermute(own_bias, 'mp', perm) for perm in rotations]  19.5 us
    ppermute x15, starting transfers between devices, gather(): mine = jnp.stack([lax.ppermute(piece, 'mp', perm) for perm in rotations])  19.3 us
  transfers between devices with their start and end apart: 63, of which 24 were waited for; matrix products, arithmetic and copies ran while one was open for 14% of the time, Pallas kernels for 24%

profile of v1, /device:TPU:0, one launch (start us, length us, event | category | flops | bytes accessed | tf_op | source)
XLA Modules:
  0.0 498.8 jit_solution(2349913387311663767)
XLA Ops:
  15.6 11.8 %collective-permute-done = f32[8,768]{1,0:T(8,128)S(1)} collective-permute-done((f32[8,768]{1,0:T(8,128)S(1)}, f32[8,768]{1,0:T(8,128)S(1)}, u32[]{:S(2)}, u32[]{:S(2)}) %collective-permute-start) | collective-permute-done | bytes 24608 | tf_op jit(solution)/shard_map/ppermute | solution.py:614
  27.3 7.0 %collective-permute-done.1 = f32[8,768]{1,0:T(8,128)S(1)} collective-permute-done((f32[8,768]{1,0:T(8,128)S(1)}, f32[8,768]{1,0:T(8,128)S(1)}, u32[]{:S(2)}, u32[]{:S(2)}) %collective-permute-start.1) | collective-permute-done | bytes 24608 | tf_op jit(solution)/shard_map/ppermute | solution.py:614
  37.6 4.1 collective-permute-done.19
  47.4 23.1 %collective-permute-done.20 = f32[32,768]{1,0:T(8,128)S(1)} collective-permute-done((f32[32,768]{1,0:T(8,128)S(1)}, f32[32,768]{1,0:T(8,128)S(1)}, u32[]{:S(2)}, u32[]{:S(2)}) %collective-permute-start.20) | collective-permute-done | bytes 98336 | tf_op jit(solution)/shard_map/ppermute | solution.py:530
  81.1 3.6 collective-permute-done.12
  88.6 6.1 %collective-permute-done.4 = f32[32,768]{1,0:T(8,128)S(1)} collective-permute-done((f32[32,768]{1,0:T(8,128)}, f32[32,768]{1,0:T(8,128)S(1)}, u32[]{:S(2)}, u32[]{:S(2)}) %collective-permute-start.4) | collective-permute-done | bytes 98336 | tf_op jit(solution)/shard_map/ppermute | solution.py:530
  106.5 11.8 %collective-permute-done.23 = f32[3,32,768]{2,1,0:T(8,128)S(1)} collective-permute-done((f32[3,32,768]{2,1,0:T(8,128)S(1)}, f32[3,32,768]{2,1,0:T(8,128)S(1)}, u32[]{:S(2)}, u32[]{:S(2)}) %collective-permute-start.23) | collective-permute-done | bytes 294944 | tf_op jit(solution)/shard_map/ppermute | solution.py:527
  178.3 13.4 %attend_forward.4 = (bf16[3,192,2048]{2,1,0:T(8,128)(2,1)}, bf16[3,64,2048]{2,1,0:T(8,128)(2,1)}, bf16[3,16,2048]{2,1,0:T(8,128)(2,1)}) custom-call(bf16[2048,768]{1,0:T(8,128)(2,1)} %bitcast.153, bf16[3,256,768]{2,1,0:T(8,128)(2,1)} %copy-done.2, f32[3,192,1]{2,1,0:T(8,128)} %squeeze.55.refs_2_, bf16[16,2048]{1,0:T(8,128)(2,1)} %select_convert_fusion.1.refs_3_, ...), custom_call_target="tpu_custom_call" | custom-call | flops 5033164800 | bytes 12000000 | tf_op jit(solution)/shard_map/attend_forward/pallas_call | solution.py:140
  201.9 13.4 %attend_forward.7 = (bf16[3,192,2048]{2,1,0:T(8,128)(2,1)}, bf16[3,64,2048]{2,1,0:T(8,128)(2,1)}, bf16[3,16,2048]{2,1,0:T(8,128)(2,1)}) custom-call(bf16[2048,768]{1,0:T(8,128)(2,1)} %bitcast.154, bf16[3,256,768]{2,1,0:T(8,128)(2,1)} %assemble_heads.5.refs_1_.refs_9_.refs_7_, f32[3,192,1]{2,1,0:T(8,128)} %copy.79.refs_2_, ...), custom_call_target="tpu_custom_call" | custom-call | flops 5033164800 | bytes 12000000 | tf_op jit(solution)/shard_map/attend_forward/pallas_call | solution.py:140
  215.3 13.5 %attend_forward.6 = (bf16[3,192,2048]{2,1,0:T(8,128)(2,1)}, bf16[3,64,2048]{2,1,0:T(8,128)(2,1)}, bf16[3,16,2048]{2,1,0:T(8,128)(2,1)}) custom-call(bf16[2048,768]{1,0:T(8,128)(2,1)} %bitcast.155, bf16[3,256,768]{2,1,0:T(8,128)(2,1)} %assemble_heads.4.refs_1_.refs_8_.refs_6_, f32[3,192,1]{2,1,0:T(8,128)} %copy.78.refs_2_, ...), custom_call_target="tpu_custom_call" | custom-call | flops 5033164800 | bytes 12000000 | tf_op jit(solution)/shard_map/attend_forward/pallas_call | solution.py:140
  228.8 13.4 %attend_forward.5 = (bf16[3,192,2048]{2,1,0:T(8,128)(2,1)}, bf16[3,64,2048]{2,1,0:T(8,128)(2,1)}, bf16[3,16,2048]{2,1,0:T(8,128)(2,1)}) custom-call(bf16[2048,768]{1,0:T(8,128)(2,1)} %bitcast.156, bf16[3,256,768]{2,1,0:T(8,128)(2,1)} %assemble_heads.3.refs_1_.refs_7_.refs_5_, f32[3,192,1]{2,1,0:T(8,128)} %copy.77.refs_2_, ...), custom_call_target="tpu_custom_call" | custom-call | flops 5033164800 | bytes 12000000 | tf_op jit(solution)/shard_map/attend_forward/pallas_call | solution.py:140
  242.2 6.7 %assemble_ffn.3.refs_11_ = bf16[4,768,768]{2,1,0:T(8,128)(2,1)} custom-call(s32[9]{0:T(128)} %stack.230.place_ref, bf16[768,768]{1,0:T(8,128)(2,1)} %own_ref.3, f32[4,3,96,768]{3,2,1,0:T(8,128)} %copy-done.1, f32[4,3,96,768]{3,2,1,0:T(8,128)} %collective-permute-done.42.other_ref), custom_call_target="tpu_custom_call" | custom-call | bytes 10616832 | tf_op jit(solution)/shard_map/assemble_ffn/pallas_call | solution.py:94
  248.9 6.6 %assemble_ffn.2.refs_10_ = bf16[4,768,768]{2,1,0:T(8,128)(2,1)} custom-call(s32[9]{0:T(128)} %stack.230.place_ref, bf16[768,768]{1,0:T(8,128)(2,1)} %own_ref.2, f32[4,3,96,768]{3,2,1,0:T(8,128)} %pad_maximum_fusion.mine_ref, f32[4,3,96,768]{3,2,1,0:T(8,128)} %collective-permute-done.34.other_ref), custom_call_target="tpu_custom_call" | custom-call | bytes 10616832 | tf_op jit(solution)/shard_map/assemble_ffn/pallas_call | solution.py:94
  255.5 78.0 %dense_middle.1 = (bf16[2048,768]{1,0:T(8,128)(2,1)}, f32[2048,768]{1,0:T(8,128)}, bf16[3,64,2048]{2,1,0:T(8,128)(2,1)}, bf16[3,64,2048]{2,1,0:T(8,128)(2,1)}, b...) custom-call(s32[9]{0:T(128)} %stack.230.place_ref, ...), custom_call_target="tpu_custom_call" | custom-call | flops 48318382080 | bytes 30000000 | tf_op jit(solution)/shard_map/dense_middle/pallas_call | solution.py:402
  333.5 10.9 %attend_backward.4.refs_0_.dqkv_ref = bf16[3,192,2048]{2,1,0:T(8,128)(2,1)} custom-call(bf16[3,192,2048]{2,1,0:T(8,128)(2,1)} %get-tuple-element.47.refs_0_, bf16[3,64,2048]{2,1,0:T(8,128)(2,1)} %get-tuple-element.41.refs_2_.refs_1_, bf16[3,16,2048]{2,1,0:T(8,128)(2,1)} %get-tuple-element.48.refs_2_, bf16[3,64,2048]{2,1,0:T(8,128)(2,1)} %get-tuple-element.49.refs_3_, ...), custom_call_target="tpu_custom_call" | custom-call | flops 8053063680 | bytes 12000000 | tf_op jit(solution)/shard_map/attend_backward/pallas_call | solution.py:203
  344.5 6.0 %own_grads.1 = (f32[3,192,768]{2,1,0:T(8,128)}, f32[3,192,128]{2,1,0:T(8,128)}) custom-call(bf16[3,192,2048]{2,1,0:T(8,128)(2,1)} %attend_backward.4.refs_0_.dqkv_ref, bf16[2048,768]{1,0:T(8,128)(2,1)} %bitcast.158), custom_call_target="tpu_custom_call" | custom-call | flops 1811939328 | bytes 8000000 | tf_op jit(solution)/shard_map/own_grads/pallas_call | solution.py:452
  359.0 10.9 %attend_backward.7.refs_3_ = bf16[3,192,2048]{2,1,0:T(8,128)(2,1)} custom-call(bf16[3,192,2048]{2,1,0:T(8,128)(2,1)} %get-tuple-element.56.refs_0_, bf16[3,64,2048]{2,1,0:T(8,128)(2,1)} %get-tuple-element.44.refs_5_.refs_1_, bf16[3,16,2048]{2,1,0:T(8,128)(2,1)} %get-tuple-element.57.refs_2_, bf16[3,64,2048]{2,1,0:T(8,128)(2,1)} %get-tuple-element.58.refs_3_, ...), custom_call_target="tpu_custom_call" | custom-call | flops 8053063680 | bytes 12000000 | tf_op jit(solution)/shard_map/attend_backward/pallas_call | solution.py:203
  371.1 10.9 %attend_backward.6.refs_2_ = bf16[3,192,2048]{2,1,0:T(8,128)(2,1)} custom-call(bf16[3,192,2048]{2,1,0:T(8,128)(2,1)} %get-tuple-element.53.refs_0_, bf16[3,64,2048]{2,1,0:T(8,128)(2,1)} %get-tuple-element.43.refs_4_.refs_1_, bf16[3,16,2048]{2,1,0:T(8,128)(2,1)} %get-tuple-element.54.refs_2_, bf16[3,64,2048]{2,1,0:T(8,128)(2,1)} %get-tuple-element.55.refs_3_, ...), custom_call_target="tpu_custom_call" | custom-call | flops 8053063680 | bytes 12000000 | tf_op jit(solution)/shard_map/attend_backward/pallas_call | solution.py:203
  384.3 6.7 %collective-permute-done.48 = f32[80,768]{1,0:T(8,128)S(1)} collective-permute-done((f32[80,768]{1,0:T(8,128)S(1)}, f32[80,768]{1,0:T(8,128)S(1)}, u32[]{:S(2)}, u32[]{:S(2)}) %collective-permute-start.48) | collective-permute-done | bytes 245792 | tf_op jit(solution)/shard_map/ppermute | solution.py:527
  402.8 9.3 %collective-permute-done.54 = f32[224,768]{1,0:T(8,128)S(1)} collective-permute-done((f32[224,768]{1,0:T(8,128)S(1)}, f32[224,768]{1,0:T(8,128)S(1)}, u32[]{:S(2)}, u32[]{:S(2)}) %collective-permute-start.54) | collective-permute-done | bytes 688160 | tf_op jit(solution)/shard_map/ppermute | solution.py:527
  429.8 9.0 %collective-permute-done.60 = f32[112,768]{1,0:T(8,128)S(1)} collective-permute-done((f32[112,768]{1,0:T(8,128)S(1)}, f32[112,768]{1,0:T(8,128)S(1)}, u32[]{:S(2)}, u32[]{:S(2)}) %collective-permute-start.60) | collective-permute-done | bytes 344096 | tf_op jit(solution)/shard_map/ppermute | solution.py:527
  441.2 9.7 %collective-permute-done.57 = f32[224,768]{1,0:T(8,128)S(1)} collective-permute-done((f32[224,768]{1,0:T(8,128)S(1)}, f32[224,768]{1,0:T(8,128)S(1)}, u32[]{:S(2)}, u32[]{:S(2)}) %collective-permute-start.57) | collective-permute-done | bytes 688160 | tf_op jit(solution)/shard_map/ppermute | solution.py:527
  457.6 10.9 %attend_backward.5.refs_1_ = bf16[3,192,2048]{2,1,0:T(8,128)(2,1)} custom-call(bf16[3,192,2048]{2,1,0:T(8,128)(2,1)} %get-tuple-element.50.refs_0_, bf16[3,64,2048]{2,1,0:T(8,128)(2,1)} %get-tuple-element.42.refs_3_.refs_1_, bf16[3,16,2048]{2,1,0:T(8,128)(2,1)} %get-tuple-element.51.refs_2_, bf16[3,64,2048]{2,1,0:T(8,128)(2,1)} %get-tuple-element.52.refs_3_, ...), custom_call_target="tpu_custom_call" | custom-call | flops 8053063680 | bytes 12000000 | tf_op jit(solution)/shard_map/attend_backward/pallas_call | solution.py:203
  468.5 16.3 %input_grads.1 = bf16[2048,768]{1,0:T(8,128)(2,1)} custom-call(s32[9]{0:T(128)} %stack.230.place_ref, f32[2048,768]{1,0:T(8,128)} %get-tuple-element.46.g1_ref, bf16[3,192,2048]{2,1,0:T(8,128)(2,1)} %attend_backward.4.refs_0_.dqkv_ref, bf16[3,192,2048]{2,1,0:T(8,128)(2,1)} %attend_backward.5.refs_1_, bf16[3,192,2048]{2,1,0:T(8,128)(2,1)} %attend_backward.6.refs_2_, ...), custom_call_target="tpu_custom_call" | custom-call | flops 7247757312 | bytes 20000000 | tf_op jit(solution)/shard_map/input_grads/pallas_call | solution.py:497
  (317 shorter events, 184.0 us)
Async XLA Ops:
  1.6 40.2 %collective-permute-start.35 = (f32[96,768]{1,0:T(8,128)S(1)}, f32[96,768]{1,0:T(8,128)S(1)}, u32[]{:S(2)}, u32[]{:S(2)}) collective-permute-start(f32[96,768]{1,0:T(8,128)S(1)} %dynamic-slice_convert_fusion), channel_id=1, source_target_pairs={{0,1},{1,2},{2,3},{3,0},{4,5},{5,6},{6,7},{7,4},{8,9},{9,10},{10,1... | collective-permute-start | bytes 884744 | tf_op jit(solution)/shard_map/ppermute | solution.py:530
  4.7 37.6 %collective-permute-start.36 = (f32[96,768]{1,0:T(8,128)S(1)}, f32[96,768]{1,0:T(8,128)S(1)}, u32[]{:S(2)}, u32[]{:S(2)}) collective-permute-start(f32[96,768]{1,0:T(8,128)S(1)} %dynamic-slice_convert_fusion), channel_id=1, source_target_pairs={{0,2},{1,3},{2,0},{3,1},{4,6},{5,7},{6,4},{7,5},{8,10},{9,11},{10,... | collective-permute-start | bytes 884744 | tf_op jit(solution)/shard_map/ppermute | solution.py:530
  7.3 37.5 %collective-permute-start.37 = (f32[96,768]{1,0:T(8,128)S(1)}, f32[96,768]{1,0:T(8,128)S(1)}, u32[]{:S(2)}, u32[]{:S(2)}) collective-permute-start(f32[96,768]{1,0:T(8,128)S(1)} %dynamic-slice_convert_fusion), channel_id=1, source_target_pairs={{0,3},{1,0},{2,1},{3,2},{4,7},{5,4},{6,5},{7,6},{8,11},{9,8},{10,9... | collective-permute-start | bytes 884744 | tf_op jit(solution)/shard_map/ppermute | solution.py:530
  35.1 38.4 %collective-permute-start.27 = (f32[96,768]{1,0:T(8,128)S(1)}, f32[96,768]{1,0:T(8,128)S(1)}, u32[]{:S(2)}, u32[]{:S(2)}) collective-permute-start(f32[96,768]{1,0:T(8,128)S(1)} %dynamic-slice_convert_fusion.1), channel_id=1, source_target_pairs={{0,1},{1,2},{2,3},{3,0},{4,5},{5,6},{6,7},{7,4},{8,9},{9,10},{10,1... | collective-permute-start | bytes 884744 | tf_op jit(solution)/shard_map/ppermute | solution.py:530
  41.8 32.8 %collective-permute-start.28 = (f32[96,768]{1,0:T(8,128)S(1)}, f32[96,768]{1,0:T(8,128)S(1)}, u32[]{:S(2)}, u32[]{:S(2)}) collective-permute-start(f32[96,768]{1,0:T(8,128)S(1)} %dynamic-slice_convert_fusion.1), channel_id=1, source_target_pairs={{0,2},{1,3},{2,0},{3,1},{4,6},{5,7},{6,4},{7,5},{8,10},{9,11},{10,... | collective-permute-start | bytes 884744 | tf_op jit(solution)/shard_map/ppermute | solution.py:530
  41.8 34.3 %collective-permute-start.29 = (f32[96,768]{1,0:T(8,128)S(1)}, f32[96,768]{1,0:T(8,128)S(1)}, u32[]{:S(2)}, u32[]{:S(2)}) collective-permute-start(f32[96,768]{1,0:T(8,128)S(1)} %dynamic-slice_convert_fusion.1), channel_id=1, source_target_pairs={{0,3},{1,0},{2,1},{3,2},{4,7},{5,4},{6,5},{7,6},{8,11},{9,8},{10,9... | collective-permute-start | bytes 884744 | tf_op jit(solution)/shard_map/ppermute | solution.py:530
  42.3 28.2 %collective-permute-start.20 = (f32[32,768]{1,0:T(8,128)S(1)}, f32[32,768]{1,0:T(8,128)S(1)}, u32[]{:S(2)}, u32[]{:S(2)}) collective-permute-start(f32[32,768]{1,0:T(8,128)S(1)} %bitcast_convert_fusion), channel_id=1, source_target_pairs={{0,2},{1,3},{2,0},{3,1},{4,6},{5,7},{6,4},{7,5},{8,10},{9,11},{10,... | collective-permute-start | bytes 294920 | tf_op jit(solution)/shard_map/ppermute | solution.py:530
  44.8 27.2 %collective-permute-start.21 = (f32[32,768]{1,0:T(8,128)S(1)}, f32[32,768]{1,0:T(8,128)S(1)}, u32[]{:S(2)}, u32[]{:S(2)}) collective-permute-start(f32[32,768]{1,0:T(8,128)S(1)} %bitcast_convert_fusion), channel_id=1, source_target_pairs={{0,3},{1,0},{2,1},{3,2},{4,7},{5,4},{6,5},{7,6},{8,11},{9,8},{10,9... | collective-permute-start | bytes 294920 | tf_op jit(solution)/shard_map/ppermute | solution.py:530
  70.5 30.6 %collective-permute-start.39 = (f32[3,96,768]{2,1,0:T(8,128)S(1)}, f32[3,96,768]{2,1,0:T(8,128)S(1)}, u32[]{:S(2)}, u32[]{:S(2)}) collective-permute-start(f32[3,96,768]{2,1,0:T(8,128)S(1)} %get-tuple-element.95), channel_id=1, source_target_pairs={{0,16},{4,20},{8,24},{12,28},{16,0},{20,4},{24,8},{28,12},{1,17},{... | collective-permute-start | bytes 2654216 | tf_op jit(solution)/shard_map/ppermute | solution.py:527
  72.0 30.4 %collective-permute-start.38 = (f32[3,96,768]{2,1,0:T(8,128)S(1)}, f32[3,96,768]{2,1,0:T(8,128)S(1)}, u32[]{:S(2)}, u32[]{:S(2)}) collective-permute-start(f32[3,96,768]{2,1,0:T(8,128)S(1)} %get-tuple-element.95), channel_id=1, source_target_pairs={{0,8},{4,12},{8,0},{12,4},{16,24},{20,28},{24,16},{28,20},{1,9},{5... | collective-permute-start | bytes 2654216 | tf_op jit(solution)/shard_map/ppermute | solution.py:527
  84.8 41.3 %collective-permute-start.31 = (f32[3,96,768]{2,1,0:T(8,128)S(1)}, f32[3,96,768]{2,1,0:T(8,128)S(1)}, u32[]{:S(2)}, u32[]{:S(2)}) collective-permute-start(f32[3,96,768]{2,1,0:T(8,128)S(1)} %get-tuple-element.97), channel_id=1, source_target_pairs={{0,16},{4,20},{8,24},{12,28},{16,0},{20,4},{24,8},{28,12},{1,17},{... | collective-permute-start | bytes 2654216 | tf_op jit(solution)/shard_map/ppermute | solution.py:527
  84.8 41.9 %collective-permute-start.30 = (f32[3,96,768]{2,1,0:T(8,128)S(1)}, f32[3,96,768]{2,1,0:T(8,128)S(1)}, u32[]{:S(2)}, u32[]{:S(2)}) collective-permute-start(f32[3,96,768]{2,1,0:T(8,128)S(1)} %get-tuple-element.97), channel_id=1, source_target_pairs={{0,8},{4,12},{8,0},{12,4},{16,24},{20,28},{24,16},{28,20},{1,9},{5... | collective-permute-start | bytes 2654216 | tf_op jit(solution)/shard_map/ppermute | solution.py:527
  124.6 24.5 %collective-permute-start.6 = (f32[3,32,768]{2,1,0:T(8,128)}, f32[3,32,768]{2,1,0:T(8,128)}, u32[]{:S(2)}, u32[]{:S(2)}) collective-permute-start(f32[3,32,768]{2,1,0:T(8,128)} %get-tuple-element.111), channel_id=1, source_target_pairs={{0,8},{4,12},{8,0},{12,4},{16,24},{20,28},{24,16},{28,20},{1,9},{5... | collective-permute-start | bytes 884744 | tf_op jit(solution)/shard_map/ppermute | solution.py:527
  126.1 24.5 %collective-permute-start.40 = (f32[3,48,768]{2,1,0:T(8,128)}, f32[3,48,768]{2,1,0:T(8,128)}, u32[]{:S(2)}, u32[]{:S(2)}) collective-permute-start(f32[3,48,768]{2,1,0:T(8,128)} %slice.195), channel_id=1, source_target_pairs={{0,8},{4,12},{8,0},{12,4},{16,24},{20,28},{24,16},{28,20},{1,9},{5... | collective-permute-start | bytes 1327112 | tf_op jit(solution)/shard_map/ppermute | solution.py:527
  126.7 25.6 %collective-permute-start.41 = (f32[3,48,768]{2,1,0:T(8,128)}, f32[3,48,768]{2,1,0:T(8,128)}, u32[]{:S(2)}, u32[]{:S(2)}) collective-permute-start(f32[3,48,768]{2,1,0:T(8,128)} %slice.196), channel_id=1, source_target_pairs={{0,16},{4,20},{8,24},{12,28},{16,0},{20,4},{24,8},{28,12},{1,17},{... | collective-permute-start | bytes 1327112 | tf_op jit(solution)/shard_map/ppermute | solution.py:527
  161.6 80.6 %collective-permute-start.42 = (f32[4,3,96,768]{3,2,1,0:T(8,128)S(1)}, f32[4,3,96,768]{3,2,1,0:T(8,128)}, u32[]{:S(2)}, u32[]{:S(2)}) collective-permute-start(f32[4,3,96,768]{3,2,1,0:T(8,128)S(1)} %pad_maximum_fusion.1.mine_ref), channel_id=1, source_target_pairs={{0,4},{4,0},{8,12},{12,8},{16,20},{20,16},{24,28},{28,24},{1,5},{5... | collective-permute-start | bytes 10616840 | tf_op jit(solution)/shard_map/ppermute | solution.py:527
  161.7 87.2 %collective-permute-start.34 = (f32[4,3,96,768]{3,2,1,0:T(8,128)}, f32[4,3,96,768]{3,2,1,0:T(8,128)}, u32[]{:S(2)}, u32[]{:S(2)}) collective-permute-start(f32[4,3,96,768]{3,2,1,0:T(8,128)} %pad_maximum_fusion.mine_ref), channel_id=1, source_target_pairs={{0,4},{4,0},{8,12},{12,8},{16,20},{20,16},{24,28},{28,24},{1,5},{5... | collective-permute-start | bytes 10616840 | tf_op jit(solution)/shard_map/ppermute | solution.py:527
  164.2 27.4 %collective-permute-start.26 = (f32[4,3,32,768]{3,2,1,0:T(8,128)}, f32[4,3,32,768]{3,2,1,0:T(8,128)}, u32[]{:S(2)}, u32[]{:S(2)}) collective-permute-start(f32[4,3,32,768]{3,2,1,0:T(8,128)} %pad_maximum_fusion.8.mine_ref), channel_id=1, source_target_pairs={{0,4},{4,0},{8,12},{12,8},{16,20},{20,16},{24,28},{28,24},{1,5},{5... | collective-permute-start | bytes 3538952 | tf_op jit(solution)/shard_map/ppermute | solution.py:527
  166.4 28.7 %collective-permute-start.18 = (f32[4,3,32,768]{3,2,1,0:T(8,128)}, f32[4,3,32,768]{3,2,1,0:T(8,128)}, u32[]{:S(2)}, u32[]{:S(2)}) collective-permute-start(f32[4,3,32,768]{3,2,1,0:T(8,128)} %pad_maximum_fusion.7.mine_ref), channel_id=1, source_target_pairs={{0,4},{4,0},{8,12},{12,8},{16,20},{20,16},{24,28},{28,24},{1,5},{5... | collective-permute-start | bytes 3538952 | tf_op jit(solution)/shard_map/ppermute | solution.py:527
  171.4 27.1 %collective-permute-start.10 = (f32[4,3,32,768]{3,2,1,0:T(8,128)}, f32[4,3,32,768]{3,2,1,0:T(8,128)}, u32[]{:S(2)}, u32[]{:S(2)}) collective-permute-start(f32[4,3,32,768]{3,2,1,0:T(8,128)} %pad_maximum_fusion.6.mine_ref), channel_id=1, source_target_pairs={{0,4},{4,0},{8,12},{12,8},{16,20},{20,16},{24,28},{28,24},{1,5},{5... | collective-permute-start | bytes 3538952 | tf_op jit(solution)/shard_map/ppermute | solution.py:527
  358.5 33.8 %collective-permute-start.53 = (f32[896,768]{1,0:T(8,128)}, f32[896,768]{1,0:T(8,128)}, u32[]{:S(2)}, u32[]{:S(2)}) collective-permute-start(f32[896,768]{1,0:T(8,128)} %constant_dynamic-slice_fusion.4), channel_id=1, source_target_pairs={{0,4},{4,0},{8,12},{12,8},{16,20},{20,16},{24,28},{28,24},{1,5},{5... | collective-permute-start | bytes 8257544 | tf_op jit(solution)/shard_map/ppermute | solution.py:527
  398.6 40.9 %collective-permute-start.50 = (f32[40,768]{1,0:T(8,128)S(1)}, f32[40,768]{1,0:T(8,128)S(1)}, u32[]{:S(2)}, u32[]{:S(2)}) collective-permute-start(f32[40,768]{1,0:T(8,128)S(1)} %dynamic-slice_add_fusion.7), channel_id=1, source_target_pairs={{0,8},{4,12},{8,0},{12,4},{16,24},{20,28},{24,16},{28,20},{1,9},{5... | collective-permute-start | bytes 368648 | tf_op jit(solution)/shard_map/ppermute | solution.py:527
  455.8 36.5 %collective-permute-start.62 = (f32[896,768]{1,0:T(8,128)}, f32[896,768]{1,0:T(8,128)}, u32[]{:S(2)}, u32[]{:S(2)}) collective-permute-start(f32[896,768]{1,0:T(8,128)} %pad_maximum_fusion.2), channel_id=1, source_target_pairs={{0,4},{4,0},{8,12},{12,8},{16,20},{20,16},{24,28},{28,24},{1,5},{5... | collective-permute-start | bytes 8257544 | tf_op jit(solution)/shard_map/ppermute | solution.py:527
  457.6 27.2 %collective-permute-start.52 = (f32[320,768]{1,0:T(8,128)}, f32[320,768]{1,0:T(8,128)}, u32[]{:S(2)}, u32[]{:S(2)}) collective-permute-start(f32[320,768]{1,0:T(8,128)} %pad_maximum_fusion.9), channel_id=1, source_target_pairs={{0,4},{4,0},{8,12},{12,8},{16,20},{20,16},{24,28},{28,24},{1,5},{5... | collective-permute-start | bytes 2949128 | tf_op jit(solution)/shard_map/ppermute | solution.py:527
  (75 other events, 1005.6 us)

commit v2 on v1

v2 whole, which is shorter than its diff:
```python
import jax
import jax.numpy as jnp
from jax import lax
from jax.experimental import pallas as pl
from jax.experimental.pallas import tpu as pltpu
from jax.sharding import PartitionSpec as P

HD = 64
GROUP = 8
EXTRA = 16
MASK = -float(2**30)
EPS = 1e-12
F32 = jnp.float32
BF16 = jnp.bfloat16
LIMIT = 60 << 20


def dot(left, right, left_dim, right_dim):
    return lax.dot_general(
        left, right, (((left_dim,), (right_dim,)), ((), ())), preferred_element_type=F32
    )


def params():
    return pltpu.CompilerParams(vmem_limit_bytes=LIMIT)


def cost(flops, moved):
    return pl.CostEstimate(flops=int(flops), bytes_accessed=int(moved), transcendentals=0)


def whole(shape):
    zeros = (0,) * len(shape)
    return pl.BlockSpec(shape, lambda *_: zeros, pipeline_mode=pl.Buffered(1))


def split3(row):
    high = row.astype(BF16).astype(F32)
    rest = row - high
    mid = rest.astype(BF16).astype(F32)
    return high, mid, rest - mid


def rows_of(height, first, parts, width):
    place = lax.broadcasted_iota(jnp.int32, (height, width), 0)
    out = jnp.zeros((height, width), F32)
    for i, part in enumerate(parts):
        out = jnp.where(place == first + i, part, out)
    return out


def put_pieces(place_ref, pieces, out_ref, lead, width, take):
    for ref, index, offset in pieces:
        values = take(ref)
        start = pl.multiple_of(place_ref[index] * width + offset, 16)
        out_ref[lead, pl.ds(start, values.shape[0]), :] = values.astype(BF16)


def attend_forward_kernel(length, spots, place_ref, x_ref, bias_ref, qf_ref, kf_ref, *refs):
    weights, outs = refs[:-3], refs[-3:]
    tokens = x_ref.shape[0]
    if spots is None:
        w_ref = weights[0]
    else:
        w_ref, weights = weights[-1], weights[:-1]
        pieces = [(ref, index, offset) for ref, (index, offset) in zip(weights, spots)]
        put_pieces(place_ref, pieces, w_ref, 0, w_ref.shape[1] // GROUP, lambda ref: ref[0, 0])
    qkv_ref, ctx_ref, aug_ref = outs
    proj = dot(w_ref[0, : 3 * HD, :], x_ref[...], 1, 1) + bias_ref[0]
    scale = HD ** (-0.5)
    qkv_ref[0, :HD, :] = (proj[:HD] * scale).astype(BF16)
    qkv_ref[0, HD:, :] = proj[HD:].astype(BF16)
    ones_rows = rows_of(EXTRA, 0, (jnp.ones((1, length), F32),), length).astype(BF16)

    def row(r, carry):
        at = pl.ds(pl.multiple_of(r * length, length), length)
        queries = jnp.concatenate([qkv_ref[0, :HD, at], qf_ref[:, at]], axis=0)
        keys = jnp.concatenate([qkv_ref[0, HD : 2 * HD, at], kf_ref[:, at]], axis=0)
        values = jnp.concatenate([qkv_ref[0, 2 * HD :, at], ones_rows], axis=0)
        scores = dot(keys, queries, 0, 0)
        highest = jnp.max(scores, axis=0, keepdims=True)
        weight = jnp.exp(scores - highest).astype(BF16)
        context = dot(values, weight, 1, 0)
        total = context[HD : HD + 1]
        ctx_ref[0, :, at] = (context[:HD] * (1.0 / total)).astype(BF16)
        log_total = highest + jnp.log(total)
        extra = rows_of(EXTRA, 4, split3(-log_total), length)
        aug_ref[0, :, at] = (extra + qf_ref[:, at].astype(F32)).astype(BF16)
        return carry

    lax.fori_loop(0, tokens // length, row, 0, unroll=2)


def attend_forward(length, place, inputs, bias, qf, kf, own=None, pieces=None, slot=0):
    heads = bias.shape[0]
    tokens, width = inputs.shape
    height = 4 * HD
    by_head = lambda *shape: pl.BlockSpec((1,) + shape, lambda h, *_: (h, 0, 0))
    out_specs = [by_head(3 * HD, tokens), by_head(HD, tokens), by_head(EXTRA, tokens)]
    out_shape = [
        jax.ShapeDtypeStruct((heads, rows, tokens), BF16) for rows in (3 * HD, HD, EXTRA)
    ]
    if pieces is None:
        spots, arrays, specs = None, [own], [by_head(height, width)]
    else:
        spots = [(index, offset) for _, index, offset in pieces]
        arrays = [array for array, _, _ in pieces]
        specs = [
            pl.BlockSpec((1, 1) + a.shape[2:], lambda h, *_: (h, slot, 0, 0)) for a in arrays
        ]
        out_specs = [by_head(height, width)] + out_specs
        out_shape = [jax.ShapeDtypeStruct((heads, height, width), BF16)] + out_shape
    return pl.pallas_call(
        lambda *refs: attend_forward_kernel(length, spots, *refs),
        grid_spec=pltpu.PrefetchScalarGridSpec(
            num_scalar_prefetch=1,
            grid=(heads,),
            in_specs=[
                whole(inputs.shape),
                by_head(3 * HD, 1),
                whole(qf.shape),
                whole(kf.shape),
                *specs,
            ],
            out_specs=out_specs,
        ),
        out_shape=out_shape,
        compiler_params=params(),
        cost_estimate=cost(heads * tokens * (6 * HD * width + 16 * 64 * length), 12e6),
        name="attend_forward",
    )(place, inputs, bias, qf, kf, *arrays)


def attend_backward_kernel(length, qkv_ref, ctx_ref, aug_ref, grad_ref, kf_ref, out_ref):
    tokens = kf_ref.shape[1]
    scale = HD ** (-0.5)
    one = jnp.ones((1, length), F32)
    ones_rows = rows_of(EXTRA, 0, (one, one, one), length).astype(BF16)

    def row(r, carry):
        at = pl.ds(pl.multiple_of(r * length, length), length)
        queries = qkv_ref[0, :HD, at]
        keys = qkv_ref[0, HD : 2 * HD, at]
        values = qkv_ref[0, 2 * HD :, at]
        grad_context = grad_ref[0, :, at]
        inner = jnp.sum(
            grad_context.astype(F32) * ctx_ref[0, :, at].astype(F32), axis=0, keepdims=True
        )
        grad_extra = rows_of(EXTRA, 0, split3(-inner), length).astype(BF16)
        scores = dot(
            jnp.concatenate([keys, kf_ref[:, at]], axis=0),
            jnp.concatenate([queries, aug_ref[0, :, at]], axis=0),
            0,
            0,
        )
        probs = jnp.exp(scores)
        spread = dot(
            jnp.concatenate([values, ones_rows], axis=0),
            jnp.concatenate([grad_context, grad_extra], axis=0),
            0,
            0,
        )
        grad_scores = (probs * spread).astype(BF16)
        out_ref[0, 2 * HD :, at] = dot(grad_context, probs.astype(BF16), 1, 1).astype(BF16)
        out_ref[0, HD : 2 * HD, at] = dot(queries, grad_scores, 1, 1).astype(BF16)
        out_ref[0, :HD, at] = (dot(keys, grad_scores, 1, 0) * scale).astype(BF16)
        return carry

    lax.fori_loop(0, tokens // length, row, 0, unroll=2)


def attend_backward(length, qkv, ctx, aug, grad, kf):
    heads, _, tokens = qkv.shape
    by_head = lambda *shape: pl.BlockSpec((1,) + shape, lambda h: (h, 0, 0))
    return pl.pallas_call(
        lambda *refs: attend_backward_kernel(length, *refs),
        grid=(heads,),
        in_specs=[
            by_head(3 * HD, tokens),
            by_head(HD, tokens),
            by_head(EXTRA, tokens),
            by_head(HD, tokens),
            whole(kf.shape),
        ],
        out_specs=by_head(3 * HD, tokens),
        out_shape=jax.ShapeDtypeStruct((heads, 3 * HD, tokens), BF16),
        compiler_params=params(),
        cost_estimate=cost(heads * tokens * 40 * 64 * length, 12e6),
        name="attend_backward",
    )(qkv, ctx, aug, grad, kf)


def norm_forward(hidden):
    center = hidden - jnp.mean(hidden, axis=-1, keepdims=True)
    inverse = lax.rsqrt(jnp.mean(center * center, axis=-1, keepdims=True) + EPS)
    return center * inverse, inverse


def norm_backward(grad, gain, norm, inverse):
    scaled = grad * gain
    first = jnp.mean(scaled, axis=-1, keepdims=True)
    second = jnp.mean(scaled * norm, axis=-1, keepdims=True)
    return (scaled - first - norm * second) * inverse


def column_sum(values):
    return jnp.sum(values, axis=0, keepdims=True)


def head_start(place_ref, shards, k, j, heads, height):
    shard = lax.rem(place_ref[GROUP] + shards - k, shards)
    return pl.multiple_of((shard * heads + j) * height, HD)


def gather_heads(place_ref, shards, heads, sets, refs, out_ref, height):
    for members, ref in zip(sets, refs):
        for i, (k, j) in enumerate(members):
            start = head_start(place_ref, shards, k, j, heads, height)
            out_ref[pl.ds(start, height), :] = ref[i, :height, :]


def fill_shards(place_ref, own_ref, refs, spots, out_ref):
    shards, height, _ = out_ref.shape
    out_ref[place_ref[GROUP]] = own_ref[...]
    for k in range(1, shards):
        shard = lax.rem(place_ref[GROUP] + shards - k, shards)
        pieces = [(ref, index, offset) for ref, (index, offset) in zip(refs, spots)]
        put_pieces(place_ref, pieces, out_ref, shard, height // GROUP, lambda ref: ref[k - 1])


def expand_kernel(sets, heads, shards, place_ref, x_ref, *refs):
    refs = list(refs)
    take = lambda count: [refs.pop(0) for _ in range(count)]
    ctx_refs, wo_refs = take(len(sets)), take(len(sets))
    bias_ref, vec_ref, full_ref = take(3)
    sum_ref, act_ref, slope_ref, we_ref, wo_ref, ctx_scr = refs

    @pl.when(pl.program_id(0) == 0)
    def _():
        gather_heads(place_ref, shards, heads, sets, wo_refs, wo_ref, HD)
        for s in range(shards):
            we_ref[s] = full_ref[s].astype(BF16)

    gather_heads(place_ref, shards, heads, sets, ctx_refs, ctx_scr, HD)
    b_output, gain_one, shift_one = vec_ref[0:1], vec_ref[1:2], vec_ref[2:3]
    attended = dot(ctx_scr[...], wo_ref[...], 0, 0) + b_output
    residual = x_ref[...].astype(F32) + attended
    sum_ref[...] = residual
    norm_one, _ = norm_forward(residual)
    normed_low = (norm_one * gain_one + shift_one).astype(BF16)
    for s in range(shards):
        b_expand = bias_ref[lax.rem(place_ref[GROUP] + shards - s, shards), 1:2]
        hidden = dot(normed_low, we_ref[s], 1, 0) + b_expand
        square = hidden * hidden
        bent = jnp.tanh(hidden * (0.7978845608028654 + 0.035677408136300125 * square))
        gate = 0.5 + 0.5 * bent
        active = hidden * gate
        act_ref[s] = active.astype(BF16)
        slope = gate + (active * (1.0 - gate)) * (1.5957691216057308 + 0.21406444881780075 * square)
        slope_ref[s] = slope.astype(BF16)


def expand(place, inputs, sets, ctx_sets, weight_sets, biases, vectors, full):
    tokens, width = inputs.shape
    shards, _, hidden = full.shape
    heads = sum(len(s) for s in sets) // shards
    block = 256
    by_token = lambda: pl.BlockSpec((block, width), lambda i, *_: (i, 0))
    by_shard = lambda: pl.BlockSpec((shards, block, hidden), lambda i, *_: (0, i, 0))
    features = shards * heads * HD
    return pl.pallas_call(
        lambda *refs: expand_kernel(sets, heads, shards, *refs),
        grid_spec=pltpu.PrefetchScalarGridSpec(
            num_scalar_prefetch=1,
            grid=(tokens // block,),
            in_specs=[
                by_token(),
                *[
                    pl.BlockSpec((a.shape[0], HD, block), lambda i, *_: (0, 0, i))
                    for a in ctx_sets
                ],
                *[
                    pl.BlockSpec(
                        (a.shape[0], HD, width),
                        lambda i, *_: (0, 3, 0),
                        pipeline_mode=pl.Buffered(1),
                    )
                    for a in weight_sets
                ],
                whole(biases.shape),
                whole(vectors.shape),
                whole(full.shape),
            ],
            out_specs=[
                by_token(),
                by_shard(),
                by_shard(),
                whole((shards, width, hidden)),
                whole((features, width)),
            ],
            scratch_shapes=[pltpu.VMEM((features, block), BF16)],
        ),
        out_shape=[
            jax.ShapeDtypeStruct((tokens, width), F32),
            jax.ShapeDtypeStruct((shards, tokens, hidden), BF16),
            jax.ShapeDtypeStruct((shards, tokens, hidden), BF16),
            jax.ShapeDtypeStruct((shards, width, hidden), BF16),
            jax.ShapeDtypeStruct((features, width), BF16),
        ],
        compiler_params=params(),
        cost_estimate=cost(2 * tokens * width * (shards * hidden + features), 40e6),
        name="expand",
    )(place, inputs, *ctx_sets, *weight_sets, biases, vectors, full)


def reduce_kernel(sets, spots, heads, place_ref, sum_ref, cot_ref, act_ref, slope_ref, *refs):
    refs = list(refs)
    take = lambda count: [refs.pop(0) for _ in range(count)]
    ctx_ref, we_ref, wo_ref, vec_ref, own_ref = take(5)
    piece_refs = take(len(spots))
    out_ref, g1_ref = take(2)
    dctx_refs = take(len(sets))
    mine_ref, send_ref = take(2)
    wr_scr, dwe_scr, dwr_scr, dwo_scr, small_scr, gh_scr, dctx_scr = refs
    step = pl.program_id(0)
    shards = we_ref.shape[0]
    me = place_ref[GROUP]

    @pl.when(step == 0)
    def _():
        fill_shards(place_ref, own_ref, piece_refs, spots, wr_scr)
        for scr in (dwe_scr, dwr_scr, dwo_scr, small_scr):
            scr[...] = jnp.zeros_like(scr)

    gain_one, shift_one = vec_ref[1:2], vec_ref[2:3]
    b_reduce, gain_two, shift_two = vec_ref[3:4], vec_ref[4:5], vec_ref[5:6]
    norm_one, inverse_one = norm_forward(sum_ref[...])
    normed = norm_one * gain_one + shift_one
    normed_low = normed.astype(BF16)
    mixed = dot(act_ref[0], wr_scr[0], 1, 0)
    for s in range(1, shards):
        mixed = mixed + dot(act_ref[s], wr_scr[s], 1, 0)
    norm_two, inverse_two = norm_forward(normed + (mixed + b_reduce))
    out_ref[...] = (norm_two * gain_two + shift_two).astype(BF16)

    cot = cot_ref[...].astype(F32)
    grad_two = norm_backward(cot, gain_two, norm_two, inverse_two)
    grad_two_low = grad_two.astype(BF16)
    grad_normed = grad_two
    for s in range(shards):
        grad_active = dot(grad_two_low, wr_scr[s], 1, 1)
        grad_hidden = (grad_active * slope_ref[s].astype(F32)).astype(BF16)
        gh_scr[s] = grad_hidden
        grad_normed = grad_normed + dot(grad_hidden, we_ref[s], 1, 1)

    own = gh_scr[me]
    dwr_scr[...] += dot(act_ref[me], grad_two_low, 0, 0)
    dwe_scr[...] += dot(normed_low, own, 0, 0)

    grad_one = norm_backward(grad_normed, gain_one, norm_one, inverse_one)
    grad_one_low = grad_one.astype(BF16)
    g1_ref[...] = grad_one
    for j in range(heads):
        dwo_scr[j * HD : (j + 1) * HD] += dot(ctx_ref[j], grad_one_low, 1, 0)
    dctx_scr[...] = dot(wo_ref[...], grad_one_low, 1, 1).astype(BF16)
    for members, ref in zip(sets, dctx_refs):
        for i, (k, j) in enumerate(members):
            ref[i] = dctx_scr[pl.ds(head_start(place_ref, shards, k, j, heads, HD), HD), :]

    small_scr[0:1] += column_sum(grad_one)
    small_scr[1:2] += column_sum(grad_normed * norm_one)
    small_scr[2:3] += column_sum(grad_normed)
    small_scr[3:4] += column_sum(grad_two)
    small_scr[4:5] += column_sum(cot * norm_two)
    small_scr[5:6] += column_sum(cot)
    small_scr[6:7] += column_sum(own.astype(F32))

    @pl.when(step == pl.num_programs(0) - 1)
    def _():
        for rel in range(4):
            for source, ref in enumerate((mine_ref, send_ref)):
                owner = place_ref[2 * rel + source]
                top = 0
                for scr in (dwe_scr, dwr_scr, dwo_scr):
                    size = scr.shape[0] // GROUP
                    start = pl.multiple_of(owner * size, 8)
                    ref[rel, top : top + size, :] = scr[pl.ds(start, size), :]
                    top += size
                ref[rel, top:, :] = jnp.where(owner == 0, small_scr[...], 0.0)


def reduce(place, residual, cot, act, slope, sets, ctx, w_expand, w_output, vectors, own, pieces):
    tokens, width = residual.shape
    shards, _, hidden = act.shape
    heads = sum(len(s) for s in sets) // shards
    block = 256
    spots = [(index, offset) for _, index, offset in pieces]
    arrays = [array for array, _, _ in pieces]
    by_token = lambda: pl.BlockSpec((block, width), lambda i, *_: (i, 0))
    by_shard = lambda: pl.BlockSpec((shards, block, hidden), lambda i, *_: (0, i, 0))
    columns = lambda count: pl.BlockSpec((count, HD, block), lambda i, *_: (0, 0, i))
    share = (width + hidden + heads * HD) // GROUP + 8
    flops = tokens * width * (6 * shards * hidden + 4 * hidden + 2 * width + 2 * heads * HD)
    return pl.pallas_call(
        lambda *refs: reduce_kernel(sets, spots, heads, *refs),
        grid_spec=pltpu.PrefetchScalarGridSpec(
            num_scalar_prefetch=1,
            grid=(tokens // block,),
            in_specs=[
                by_token(),
                by_token(),
                by_shard(),
                by_shard(),
                columns(heads),
                whole(w_expand.shape),
                whole(w_output.shape),
                whole(vectors.shape),
                whole(own.shape),
                *[whole(a.shape) for a in arrays],
            ],
            out_specs=[
                by_token(),
                by_token(),
                *[columns(len(s)) for s in sets],
                whole((4, share, width)),
                whole((4, share, width)),
            ],
            scratch_shapes=[
                pltpu.VMEM((shards, hidden, width), BF16),
                pltpu.VMEM((width, hidden), F32),
                pltpu.VMEM((hidden, width), F32),
                pltpu.VMEM((heads * HD, width), F32),
                pltpu.VMEM((8, width), F32),
                pltpu.VMEM((shards, block, hidden), BF16),
                pltpu.VMEM((shards * heads * HD, block), BF16),
            ],
        ),
        out_shape=[
            jax.ShapeDtypeStruct((tokens, width), BF16),
            jax.ShapeDtypeStruct((tokens, width), F32),
            *[jax.ShapeDtypeStruct((len(s), HD, tokens), BF16) for s in sets],
            jax.ShapeDtypeStruct((4, share, width), F32),
            jax.ShapeDtypeStruct((4, share, width), F32),
        ],
        compiler_params=params(),
        cost_estimate=cost(flops, 60e6),
        name="reduce",
    )(place, residual, cot, act, slope, ctx, w_expand, w_output, vectors, own, *arrays)


def own_grads_kernel(place_ref, dqkv_ref, x_ref, mine_ref, send_ref, grad_scr):
    heads = dqkv_ref.shape[0]
    height = heads * HD
    ones = jnp.ones((8, x_ref.shape[0]), BF16)
    row = lax.broadcasted_iota(jnp.int32, (8, 3 * HD), 0)
    sums = jnp.zeros((8, 3 * HD), F32)
    for j in range(heads):
        grad = dot(dqkv_ref[j], x_ref[...], 1, 0)
        for i in range(3):
            grad_scr[i * height + j * HD : i * height + (j + 1) * HD, :] = grad[i * HD : (i + 1) * HD]
        sums = jnp.where(row == j, dot(ones, dqkv_ref[j], 1, 1), sums)
    size = 3 * height // GROUP
    for rel in range(4):
        for source, ref in enumerate((mine_ref, send_ref)):
            owner = place_ref[2 * rel + source]
            ref[rel, :size, :] = grad_scr[pl.ds(pl.multiple_of(owner * size, 8), size), :]
            ref[rel, size:, :] = jnp.zeros((8, x_ref.shape[1]), F32)
            ref[rel, size:, : 3 * HD] = jnp.where(owner == 0, sums, 0.0)


def own_grads(place, dqkv, inputs):
    heads, height, tokens = dqkv.shape
    width = inputs.shape[1]
    share = heads * height // GROUP + 8
    return pl.pallas_call(
        own_grads_kernel,
        grid_spec=pltpu.PrefetchScalarGridSpec(
            num_scalar_prefetch=1,
            grid=(1,),
            in_specs=[whole(dqkv.shape), whole(inputs.shape)],
            out_specs=[whole((4, share, width)), whole((4, share, width))],
            scratch_shapes=[pltpu.VMEM((heads * height, width), F32)],
        ),
        out_shape=[jax.ShapeDtypeStruct((4, share, width), F32)] * 2,
        compiler_params=params(),
        cost_estimate=cost(2 * heads * height * tokens * width, 8e6),
        name="own_grads",
    )(place, dqkv, inputs)


def spread_kernel(sizes, place_ref, *refs):
    parts, outs = refs[:GROUP], refs[GROUP:]
    for i, ref in enumerate(parts):
        owner = place_ref[i]
        top = 0
        for size, out_ref in zip(sizes, outs):
            out_ref[pl.ds(pl.multiple_of(owner * size, 8), size), :] = ref[top : top + size, :]
            top += size

        @pl.when(owner == 0)
        def _():
            outs[-1][...] = ref[top:, :]


def spread(place, parts, sizes):
    width = parts[0].shape[1]
    shapes = [(GROUP * size, width) for size in sizes] + [(8, width)]
    return pl.pallas_call(
        lambda *refs: spread_kernel(sizes, *refs),
        grid_spec=pltpu.PrefetchScalarGridSpec(
            num_scalar_prefetch=1,
            grid=(1,),
            in_specs=[whole(a.shape) for a in parts],
            out_specs=[whole(s) for s in shapes],
        ),
        out_shape=[jax.ShapeDtypeStruct(s, F32) for s in shapes],
        compiler_params=params(),
        cost_estimate=cost(0, 8 * parts[0].size * 8),
        name="spread",
    )(place, *parts)


def input_grads_kernel(sets, heads, shards, place_ref, g1_ref, *refs):
    count = len(sets)
    grads, weights = refs[:count], refs[count : 2 * count]
    out_ref, grad_scr, w_scr = refs[2 * count :]
    height = 3 * HD

    @pl.when(pl.program_id(0) == 0)
    def _():
        gather_heads(place_ref, shards, heads, sets, weights, w_scr, height)

    gather_heads(place_ref, shards, heads, sets, grads, grad_scr, height)
    out_ref[...] = (g1_ref[...] + dot(grad_scr[...], w_scr[...], 0, 0)).astype(BF16)


def input_grads(place, grad_one, sets, grad_sets, weight_sets, shards):
    tokens, width = grad_one.shape
    block = 256
    heads = sum(len(s) for s in sets) // shards
    count = shards * heads * 3 * HD
    by_token = lambda: pl.BlockSpec((block, width), lambda i, *_: (i, 0))
    return pl.pallas_call(
        lambda *refs: input_grads_kernel(sets, heads, shards, *refs),
        grid_spec=pltpu.PrefetchScalarGridSpec(
            num_scalar_prefetch=1,
            grid=(tokens // block,),
            in_specs=[
                by_token(),
                *[
                    pl.BlockSpec((a.shape[0], 3 * HD, block), lambda i, *_: (0, 0, i))
                    for a in grad_sets
                ],
                *[whole(a.shape) for a in weight_sets],
            ],
            out_specs=by_token(),
            scratch_shapes=[pltpu.VMEM((count, block), BF16), pltpu.VMEM((count, width), BF16)],
        ),
        out_shape=jax.ShapeDtypeStruct((tokens, width), BF16),
        compiler_params=params(),
        cost_estimate=cost(2 * tokens * width * count, 20e6),
        name="input_grads",
    )(place, grad_one, *grad_sets, *weight_sets)


def after(values, *others):
    return lax.optimization_barrier((values, others))[0]


def solution(mesh):
    peers = mesh.shape["mp"]
    lanes = mesh.shape["dp"]
    rotations = [[(i, (i + k) % peers) for i in range(peers)] for k in range(1, peers)]

    def flip(values, bits):
        return lax.ppermute(values, "dp", [(i, i ^ bits) for i in range(lanes)])

    def from_peers(piece):
        return jnp.stack([lax.ppermute(piece, "mp", perm) for perm in rotations])

    def swapped(piece):
        copies = jnp.broadcast_to(piece[None], (peers,) + piece.shape)
        got = lax.all_to_all(copies, "mp", 0, 0, tiled=True)
        me = lax.axis_index("mp")
        return jnp.concatenate(
            [
                lax.dynamic_slice_in_dim(got, lax.rem(me + peers - k, peers), 1, 0)
                for k in range(1, peers)
            ]
        )

    def with_core(pieces):
        out = []
        for array, rel, offset in pieces:
            out.append((array, 2 * rel, offset))
            out.append((flip(array, 1), 2 * rel + 1, offset))
        return out

    def scatter(mine, got, *ready):
        got = after(got, *ready)
        parts = [mine[rel] + got[rel] for rel in range(4)]
        return parts[0], [flip(parts[rel], 2 * rel) for rel in (1, 2, 3)]

    def collect(first, rest, *ready):
        rest = after(rest, *ready)
        total = first + rest[0] + rest[1] + rest[2]
        step = GROUP
        while step < lanes:
            total = total + flip(total, step)
            step *= 2
        return [total] + [flip(total, bits) for bits in (2, 4, 6)]

    def finish(arrays, *ready):
        out = []
        for array in after(arrays, *ready):
            out += [array, flip(array, 1)]
        return out

    def local(
        tokens,
        doc_lengths,
        w_query,
        b_query,
        w_key,
        w_value,
        b_value,
        w_output,
        b_output,
        gain_attn,
        shift_attn,
        w_expand,
        b_expand,
        w_reduce,
        b_reduce,
        gain_ffn,
        shift_ffn,
        cotangent,
    ):
        row_count, length, width = tokens.shape
        heads = w_query.shape[1] // HD
        hidden = w_expand.shape[1]
        count = row_count * length
        inputs = tokens.reshape(count, width)
        cot = cotangent.reshape(count, width)
        inside = lax.axis_index("dp") % GROUP
        me = lax.axis_index("mp")
        place = jnp.stack([inside ^ i for i in range(GROUP)] + [me]).astype(jnp.int32)
        sets = [[(0, j) for j in range(heads)]]
        sets += [[(k, j) for k in range(1, peers)] for j in range(heads)]

        by_head = lambda w: w.T.reshape(heads, HD, width)
        own_heads = jnp.concatenate(
            [by_head(w_query), by_head(w_key), by_head(w_value), w_output.reshape(heads, HD, width)],
            axis=1,
        )
        blank = jnp.zeros((width - 2 * heads * HD,), BF16)
        own_bias = jnp.stack(
            [jnp.concatenate([b_query, b_value, blank]), b_expand]
            + [jnp.zeros((width,), BF16)] * 6
        ).astype(F32)

        def piece_of(array, which=0, axis=0):
            size = array.shape[axis] // GROUP
            start = (inside ^ which) * size
            return lax.dynamic_slice_in_dim(array, start, size, axis).astype(F32)

        def both(near):
            return flip(near, 2), flip(near, 4)

        def corner(by_x, by_y, axis):
            half = by_x.shape[axis] // 2
            first = flip(lax.slice_in_dim(by_y, 0, half, axis=axis), 2)
            second = flip(lax.slice_in_dim(by_x, half, 2 * half, axis=axis), 4)
            return first, second

        def listed(near, by_x, by_y, first, second, axis):
            half = first.shape[axis]
            return with_core(
                [(near, 0, 0), (by_x, 1, 0), (by_y, 2, 0), (first, 3, 0), (second, 3, half)]
            )

        early = piece_of(own_heads[:1], axis=1)
        near = from_peers(jnp.concatenate([early[0], own_bias]))
        near_early, biases = near[:, None, : early.shape[1]], near[:, early.shape[1] :]
        near_late = swapped(after(piece_of(own_heads[1:], axis=1), near))
        start = lax.axis_index("dp") * (width // lanes)
        share = lax.dynamic_slice_in_dim(w_expand, start, width // lanes, 0).astype(F32)
        all_expand = lax.all_gather(after(share, near), ("mp", "dp")).reshape(peers, width, hidden)

        def columns(rows):
            parts = rows[:, 0, : 2 * heads * HD].reshape(-1, 2, heads, HD)
            blank = jnp.zeros((rows.shape[0], heads, HD), F32)
            return jnp.concatenate([parts[:, 0], blank, parts[:, 1]], axis=-1)[..., None]

        own_columns, peer_columns = columns(own_bias[None]), columns(biases)
        biases = jnp.concatenate([own_bias[None], biases])

        ends = jnp.cumsum(doc_lengths, axis=-1)
        position = jnp.arange(length, dtype=jnp.int32)
        segment = jnp.sum((position[None, :, None] >= ends[:, None, :]).astype(jnp.int32), axis=-1)
        segment = segment.reshape(1, count)
        docs = doc_lengths.shape[1]
        label = jnp.arange(EXTRA, dtype=jnp.int32)[:, None]
        is_doc = label < docs
        qf = jnp.where(is_doc & (segment == label), 1.0, 0.0).astype(BF16)
        kf = jnp.where(
            is_doc,
            jnp.where(segment == label, 0.0, MASK),
            jnp.where(label < docs + 3, 1.0, 0.0),
        ).astype(BF16)

        attend = lambda bias, **w: attend_forward(length, place, inputs, bias, qf, kf, **w)
        ready = [(near_early, 0, 0)]
        ready += [(flip(near_early, 2 * rel), rel, 0) for rel in (1, 2, 3)]
        saved = [None]
        weight_sets = [own_heads]
        weights, *kept = attend(peer_columns[:, 0], pieces=with_core(ready))
        saved.append(kept)
        weight_sets.append(weights)
        sides_late = both(after(near_late, kept))
        near_reduce = swapped(after(piece_of(w_reduce), kept, near_late))
        saved[0] = own = attend(after(own_columns[0], kept, near_late), own=own_heads)
        sides_late = after(sides_late, own)
        corner_late = corner(*sides_late, 2)
        pieces_late = listed(near_late, *sides_late, *corner_late, 2)

        weights, *kept = attend(peer_columns[:, 1], pieces=pieces_late, slot=0)
        saved.append(kept)
        weight_sets.append(weights)
        near_reduce = after(near_reduce, kept)
        sides_reduce = both(near_reduce)
        weights, *kept = attend(
            after(peer_columns[:, 2], near_reduce), pieces=pieces_late, slot=1
        )
        saved.append(kept)
        weight_sets.append(weights)
        sides_reduce = after(sides_reduce, kept)
        corner_reduce = corner(*sides_reduce, 1)
        pieces_reduce = listed(near_reduce, *sides_reduce, *corner_reduce, 1)
        biases = after(biases, sides_reduce)

        vectors = jnp.stack(
            [b_output, gain_attn, shift_attn, b_reduce, gain_ffn, shift_ffn]
            + [jnp.zeros((width,), BF16)] * 2
        ).astype(F32)
        residual, act, slope, all_expand, all_output = expand(
            place,
            inputs,
            sets,
            [s[1] for s in saved],
            weight_sets,
            biases,
            vectors,
            all_expand,
        )
        output, grad_one, *dctx, mine, send = reduce(
            place,
            residual,
            cot,
            act,
            slope,
            sets,
            saved[0][1],
            all_expand,
            all_output,
            vectors,
            w_reduce,
            pieces_reduce,
        )
        got = flip(send, 1)
        step = lambda i: attend_backward(length, *saved[i], dctx[i], kf)
        backward = [step(0)]
        first, rest = scatter(mine, got, backward[0])
        mine, send = own_grads(place, backward[0], inputs)
        got = flip(send, 1)
        backward.append(step(1))
        second, rest_two = scatter(mine, got, backward[1])
        backward += [step(i) for i in range(2, heads + 1)]
        first = collect(first, rest, backward[-1])
        second = collect(second, rest_two, backward[-1])
        grad_tokens = input_grads(place, grad_one, sets, backward, weight_sets, peers)
        first = finish(first, grad_tokens)
        other = finish(second, grad_tokens)

        dwe, dwr, dwo, small = spread(
            place, first, [width // GROUP, hidden // GROUP, heads * HD // GROUP]
        )
        dqkv, dbias = spread(place, other, [3 * heads * HD // GROUP])
        turned = lambda i: dqkv[i * heads * HD : (i + 1) * heads * HD].T
        flat = lambda i: dbias[:heads, i * HD : (i + 1) * HD].reshape(heads * HD)
        shape = (row_count, length, width)
        return (
            output.reshape(shape),
            grad_tokens.reshape(shape),
            turned(0),
            flat(0),
            turned(1),
            turned(2),
            flat(2),
            dwo,
            small[0],
            small[1],
            small[2],
            dwe,
            small[6],
            dwr,
            small[3],
            small[4],
            small[5],
        )

    rows, split = P("dp", None, None), P(None, "mp")
    return jax.shard_map(
        local,
        mesh=mesh,
        in_specs=(
            rows,
            P("dp", None),
            split,
            P("mp"),
            split,
            split,
            P("mp"),
            P("mp", None),
            P(),
            P(),
            P(),
            split,
            P("mp"),
            P("mp", None),
            P(),
            P(),
            P(),
            rows,
        ),
        out_specs=(
            rows,
            rows,
            split,
            P("mp"),
            split,
            split,
            P("mp"),
            P("mp", None),
            P(),
            P(),
            P(),
            split,
            P("mp"),
            P("mp", None),
            P(),
            P(),
            P(),
        ),
        check_vma=False,
    )
```

time: 503 us -> 401 us (0.80)
  waiting for transfers between devices: 131 us -> 70.9 us
  other arithmetic: 43.5 us -> 16 us
  starting transfers between devices: 63.3 us -> 43.1 us
  local copies, waits for them, and re-layouts: 38.2 us -> 20.1 us
  Pallas kernels: 221 us -> 235 us
  between operations: 1.8 us -> 14.8 us
    ppermute x63 -> x50, waiting for transfers between devices: 131 us -> 70.9 us  [the longest x47 62.9 us: flip(): return lax.ppermute(values, 'dp', [(i, i ^ bits) for i in range(lanes)])]
    ppermute x63 -> x50, starting transfers between devices: 63.3 us -> 35.5 us  [the longest x47 29.4 us: flip(): return lax.ppermute(values, 'dp', [(i, i ^ bits) for i in range(lanes)])]
    another operation x16 -> x1, other arithmetic: 17.4 us -> 0.04 us  [from_peers(): return jnp.stack([lax.ppermute(piece, 'mp', perm) for perm in rotations])]
    pallas_call x12 -> x10, Pallas kernels: 178 us -> 192 us  [the longest x1 66 us: reduce(): pl.pallas_call(lambda *refs: reduce_kernel(sets, spots, heads, *refs), gr...]
    slice x20 -> x10, local copies, waits for them, and re-layouts: 12.5 us -> 2.89 us  [the longest x2 2.02 us: corner(): second = flip(lax.slice_in_dim(by_x, half, 2 * half, axis=axis), 4)]
    concatenate x11 -> x5, other arithmetic: 10.1 us -> 0.78 us  [the longest x1 0.65 us: local(): biases = jnp.concatenate([own_bias[None], biases])]
    another operation x7, local copies, waits for them, and re-layouts: 8.37 us -> 0.08 us  [local(): jnp.stack([b_output, gain_attn, shift_attn, b_reduce, gain_ffn, shift_ffn...]
    all_to_all x0 -> x2, starting transfers between devices: none -> 7.52 us  [swapped(): got = lax.all_to_all(copies, 'mp', 0, 0, tiled=True)]
  transfers between devices with their start and end apart: 63 -> 53, of which waited for: 24 -> 17; matrix products, arithmetic and copies ran while one was open for 14% -> 7% of each run, Pallas kernels for 24% -> 41%
where the time goes in v2:
time: 401 us; the launch traced here: 400 us
  Pallas kernels  235 us (59%)
  waiting for transfers between devices  70.9 us (18%)
  starting transfers between devices  43.1 us (11%)
  local copies, waits for them, and re-layouts  20.1 us (5%)
  other arithmetic  16 us (4%)
  between operations  14.8 us (4%)
    pallas_call x1, Pallas kernels, reduce(): pl.pallas_call(lambda *refs: reduce_kernel(sets, spots, heads, *refs), gr...  66 us
    ppermute x47, waiting for transfers between devices, flip(): return lax.ppermute(values, 'dp', [(i, i ^ bits) for i in range(lanes)])  62.9 us
    pallas_call x4, Pallas kernels, attend_forward(): pl.pallas_call(lambda *refs: attend_forward_kernel(length, spots, *refs),...  58.4 us
    pallas_call x4, Pallas kernels, attend_backward(): pl.pallas_call(lambda *refs: attend_backward_kernel(length, *refs), grid=...  43.7 us
    pallas_call x1, Pallas kernels, expand(): pl.pallas_call(lambda *refs: expand_kernel(sets, heads, shards, *refs), g...  34.2 us
    ppermute x47, starting transfers between devices, flip(): return lax.ppermute(values, 'dp', [(i, i ^ bits) for i in range(lanes)])  29.4 us
    pallas_call x1, Pallas kernels, input_grads(): pl.pallas_call(lambda *refs: input_grads_kernel(sets, heads, shards, *ref...  16.2 us
    pallas_call x2, Pallas kernels, spread(): pl.pallas_call(lambda *refs: spread_kernel(sizes, *refs), grid_spec=pltpu...  9.62 us
  transfers between devices with their start and end apart: 53, of which 17 were waited for; matrix products, arithmetic and copies ran while one was open for 7% of the time, Pallas kernels for 41%

profile of v2, /device:TPU:0, one launch (start us, length us, event | category | flops | bytes accessed | tf_op | source)
XLA Modules:
  0.0 400.2 jit_solution(4198707450602304788)
XLA Ops:
  10.2 5.1 %collective-permute-start.2 = (f32[40,768]{1,0:T(8,128)S(1)}, f32[40,768]{1,0:T(8,128)S(1)}, u32[]{:S(2)}, u32[]{:S(2)}) collective-permute-start(f32[40,768]{1,0:T(8,128)S(1)} %concatenate.39), channel_id=1, source_target_pairs={{0,3},{1,0},{2,1},{3,2},{4,7},{5,4},{6,5},{7,6},{8,11},{9,8},{10,9... | collective-permute-start | bytes 368648 | tf_op jit(solution)/shard_map/ppermute | solution.py:579
  19.0 6.9 %collective-permute-done.1 = f32[40,768]{1,0:T(8,128)S(1)} collective-permute-done((f32[40,768]{1,0:T(8,128)S(1)}, f32[40,768]{1,0:T(8,128)S(1)}, u32[]{:S(2)}, u32[]{:S(2)}) %collective-permute-start.1) | collective-permute-done | bytes 122912 | tf_op jit(solution)/shard_map/ppermute | solution.py:579
  35.0 3.8 all-to-all-start
  39.0 4.6 %collective-permute-done.8 = f32[3,1,32,768]{3,2,0,1:T(8,128)S(1)} collective-permute-done((f32[3,1,32,768]{3,2,0,1:T(8,128)S(1)}, f32[3,1,32,768]{3,2,0,1:T(8,128)S(1)}, u32[]{:S(2)}, u32[]{:S(2)}) %collective-permute-start.8) | collective-permute-done | bytes 294944 | tf_op jit(solution)/shard_map/ppermute | solution.py:576
  43.5 4.6 %collective-permute-done.6 = f32[3,1,32,768]{3,2,0,1:T(8,128)S(1)} collective-permute-done((f32[3,1,32,768]{3,2,0,1:T(8,128)S(1)}, f32[3,1,32,768]{3,2,0,1:T(8,128)S(1)}, u32[]{:S(2)}, u32[]{:S(2)}) %collective-permute-start.6) | collective-permute-done | bytes 294944 | tf_op jit(solution)/shard_map/ppermute | solution.py:576
  50.3 14.6 %attend_forward.4 = (bf16[3,256,768]{2,1,0:T(8,128)(2,1)}, bf16[3,192,2048]{2,1,0:T(8,128)(2,1)}, bf16[3,64,2048]{2,1,0:T(8,128)(2,1)}, bf16[3,16,2048]{2,1,0:T(8,128)(2,1)}) custom-call(s32[9]{0:T(128)} %stack.92.refs_0_.place_ref, bf16[2048,768]{1,0:T(8,128)(2,1)} %bitcast.103, f32[3,192,1]{2,1,0:T(8,128)} %copy.87.refs_2_, ...), custom_call_target="tpu_custom_call" | custom-call | flops 5033164800 | bytes 12000000 | tf_op jit(solution)/shard_map/attend_forward/pallas_call | solution.py:113
  73.3 14.1 %attend_forward.5 = (bf16[3,192,2048]{2,1,0:T(8,128)(2,1)}, bf16[3,64,2048]{2,1,0:T(8,128)(2,1)}, bf16[3,16,2048]{2,1,0:T(8,128)(2,1)}) custom-call(s32[9]{0:T(128)} %stack.92.refs_0_.place_ref, bf16[2048,768]{1,0:T(8,128)(2,1)} %bitcast.104, f32[3,192,1]{2,1,0:T(8,128)} %copy.96.refs_2_, bf16[16,2048]{1,0:T(8,128)(2,1)} %select_convert_fusion.1.refs_3_, ...), custom_call_target="tpu_custom_call" | custom-call | flops 5033164800 | bytes 12000000 | tf_op jit(solution)/shard_map/attend_forward/pallas_call | solution.py:113
  90.9 8.7 %collective-permute-done.15.refs_11_ = f32[3,2,16,768]{3,2,1,0:T(8,128)} collective-permute-done((f32[3,2,16,768]{3,2,1,0:T(8,128)S(1)}, f32[3,2,16,768]{3,2,1,0:T(8,128)}, u32[]{:S(2)}, u32[]{:S(2)}) %collective-permute-start.15) | collective-permute-done | bytes 294944 | tf_op jit(solution)/shard_map/ppermute | solution.py:576
  99.6 4.3 %collective-permute-done.17.refs_13_ = f32[3,2,16,768]{3,2,1,0:T(8,128)} collective-permute-done((f32[3,2,16,768]{3,2,1,0:T(8,128)S(1)}, f32[3,2,16,768]{3,2,1,0:T(8,128)}, u32[]{:S(2)}, u32[]{:S(2)}) %collective-permute-start.17) | collective-permute-done | bytes 294944 | tf_op jit(solution)/shard_map/ppermute | solution.py:576
  106.4 14.6 %attend_forward.6 = (bf16[3,256,768]{2,1,0:T(8,128)(2,1)}, bf16[3,192,2048]{2,1,0:T(8,128)(2,1)}, bf16[3,64,2048]{2,1,0:T(8,128)(2,1)}, bf16[3,16,2048]{2,1,0:T(8,128)(2,1)}) custom-call(s32[9]{0:T(128)} %stack.92.refs_0_.place_ref, bf16[2048,768]{1,0:T(8,128)(2,1)} %bitcast.105, f32[3,192,1]{2,1,0:T(8,128)} %copy.97.refs_2_, ...), custom_call_target="tpu_custom_call" | custom-call | flops 5033164800 | bytes 12000000 | tf_op jit(solution)/shard_map/attend_forward/pallas_call | solution.py:113
  124.2 15.0 %attend_forward.7 = (bf16[3,256,768]{2,1,0:T(8,128)(2,1)}, bf16[3,192,2048]{2,1,0:T(8,128)(2,1)}, bf16[3,64,2048]{2,1,0:T(8,128)(2,1)}, bf16[3,16,2048]{2,1,0:T(8,128)(2,1)}) custom-call(s32[9]{0:T(128)} %stack.92.refs_0_.place_ref, bf16[2048,768]{1,0:T(8,128)(2,1)} %bitcast.106, f32[3,192,1]{2,1,0:T(8,128)} %copy.98.refs_2_, ...), custom_call_target="tpu_custom_call" | custom-call | flops 5033164800 | bytes 12000000 | tf_op jit(solution)/shard_map/attend_forward/pallas_call | solution.py:113
  148.4 6.5 %collective-permute-done.24.refs_16_ = f32[3,48,768]{2,1,0:T(8,128)} collective-permute-done((f32[3,48,768]{2,1,0:T(8,128)S(1)}, f32[3,48,768]{2,1,0:T(8,128)}, u32[]{:S(2)}, u32[]{:S(2)}) %collective-permute-start.24) | collective-permute-done | bytes 442400 | tf_op jit(solution)/shard_map/ppermute | solution.py:576
  157.0 34.2 %expand.1 = (f32[2048,768]{1,0:T(8,128)}, bf16[4,2048,768]{2,1,0:T(8,128)(2,1)}, bf16[4,2048,768]{2,1,0:T(8,128)(2,1)}, bf16[4,768,768]{2,1,0:T(8,128)(2,1)}, bf16[768,768]{1,0:T(8,128)(2,1)}) custom-call(s32[9]{0:T(128)} %stack.92.refs_0_.place_ref, bf16[2048,768]{1,0:T(8,128)(2,1)} %bitcast.107, ...), custom_call_target="tpu_custom_call" | custom-call | flops 12079595520 | bytes 40000000 | tf_op jit(solution)/shard_map/expand/pallas_call | solution.py:271
  192.1 66.0 %reduce.19 = (bf16[2048,768]{1,0:T(8,128)(2,1)}, f32[2048,768]{1,0:T(8,128)}, bf16[3,64,2048]{2,1,0:T(8,128)(2,1)}, bf16[3,64,2048]{2,1,0:T(8,128)(2,1)}, bf16[3...) custom-call(s32[9]{0:T(128)} %stack.92.refs_0_.place_ref, ...), custom_call_target="tpu_custom_call" | custom-call | flops 36842766336 | bytes 60000000 | tf_op jit(solution)/shard_map/reduce/pallas_call | solution.py:404
  258.6 10.9 %attend_backward.4.refs_2_.dqkv_ref = bf16[3,192,2048]{2,1,0:T(8,128)(2,1)} custom-call(bf16[3,192,2048]{2,1,0:T(8,128)(2,1)} %get-tuple-element.88.refs_0_, bf16[3,64,2048]{2,1,0:T(8,128)(2,1)} %get-tuple-element.86.refs_2_.refs_5_.refs_1_, bf16[3,16,2048]{2,1,0:T(8,128)(2,1)} %get-tuple-element.89.refs_2_, ...), custom_call_target="tpu_custom_call" | custom-call | flops 8053063680 | bytes 12000000 | tf_op jit(solution)/shard_map/attend_backward/pallas_call | solution.py:175
  269.5 7.2 %own_grads.1 = (f32[4,80,768]{2,1,0:T(8,128)}, f32[4,80,768]{2,1,0:T(8,128)}) custom-call(s32[9]{0:T(128)} %stack.92.refs_0_.place_ref, bf16[3,192,2048]{2,1,0:T(8,128)(2,1)} %attend_backward.4.refs_2_.dqkv_ref, bf16[2048,768]{1,0:T(8,128)(2,1)} %bitcast.108), custom_call_target="tpu_custom_call" | custom-call | flops 1811939328 | bytes 8000000 | tf_op jit(solution)/shard_map/own_grads/pallas_call | solution.py:475
  276.8 11.0 %attend_backward.5.refs_3_ = bf16[3,192,2048]{2,1,0:T(8,128)(2,1)} custom-call(bf16[3,192,2048]{2,1,0:T(8,128)(2,1)} %get-tuple-element.81.refs_0_, bf16[3,64,2048]{2,1,0:T(8,128)(2,1)} %get-tuple-element.82.refs_3_.refs_1_, bf16[3,16,2048]{2,1,0:T(8,128)(2,1)} %get-tuple-element.83.refs_2_, bf16[3,64,2048]{2,1,0:T(8,128)(2,1)} %get-tuple-element.116.refs_3_, ...), custom_call_target="tpu_custom_call" | custom-call | flops 8053063680 | bytes 12000000 | tf_op jit(solution)/shard_map/attend_backward/pallas_call | solution.py:175
  300.4 10.9 %attend_backward.7.refs_5_ = bf16[3,192,2048]{2,1,0:T(8,128)(2,1)} custom-call(bf16[3,192,2048]{2,1,0:T(8,128)(2,1)} %get-tuple-element.102.refs_0_, bf16[3,64,2048]{2,1,0:T(8,128)(2,1)} %get-tuple-element.98.refs_5_.refs_1_, bf16[3,16,2048]{2,1,0:T(8,128)(2,1)} %get-tuple-element.103.refs_2_, bf16[3,64,2048]{2,1,0:T(8,128)(2,1)} %get-tuple-element.118.refs_3_, ...), custom_call_target="tpu_custom_call" | custom-call | flops 8053063680 | bytes 12000000 | tf_op jit(solution)/shard_map/attend_backward/pallas_call | solution.py:175
  314.0 5.6 %collective-permute-done.42 = f32[224,768]{1,0:T(8,128)} collective-permute-done((f32[224,768]{1,0:T(8,128)}, f32[224,768]{1,0:T(8,128)}, u32[]{:S(2)}, u32[]{:S(2)}) %collective-permute-start.42) | collective-permute-done | bytes 688160 | tf_op jit(solution)/shard_map/ppermute | solution.py:576
  319.6 14.6 %collective-permute-done.41 = f32[224,768]{1,0:T(8,128)} collective-permute-done((f32[224,768]{1,0:T(8,128)}, f32[224,768]{1,0:T(8,128)}, u32[]{:S(2)}, u32[]{:S(2)}) %collective-permute-start.41) | collective-permute-done | bytes 688160 | tf_op jit(solution)/shard_map/ppermute | solution.py:576
  337.6 10.9 %attend_backward.6.refs_4_ = bf16[3,192,2048]{2,1,0:T(8,128)(2,1)} custom-call(bf16[3,192,2048]{2,1,0:T(8,128)(2,1)} %get-tuple-element.94.refs_0_, bf16[3,64,2048]{2,1,0:T(8,128)(2,1)} %get-tuple-element.92.refs_4_.refs_1_, bf16[3,16,2048]{2,1,0:T(8,128)(2,1)} %get-tuple-element.95.refs_2_, bf16[3,64,2048]{2,1,0:T(8,128)(2,1)} %get-tuple-element.117.refs_3_, ...), custom_call_target="tpu_custom_call" | custom-call | flops 8053063680 | bytes 12000000 | tf_op jit(solution)/shard_map/attend_backward/pallas_call | solution.py:175
  352.6 16.2 %input_grads.1 = bf16[2048,768]{1,0:T(8,128)(2,1)} custom-call(s32[9]{0:T(128)} %stack.92.refs_0_.place_ref, f32[2048,768]{1,0:T(8,128)} %get-tuple-element.114.refs_1_, bf16[3,192,2048]{2,1,0:T(8,128)(2,1)} %attend_backward.4.refs_2_.dqkv_ref, bf16[3,192,2048]{2,1,0:T(8,128)(2,1)} %attend_backward.5.refs_3_, bf16[3,192,2048]{2,1,0:T(8,128)(2,1)} %attend_backward.6.refs_4_, ...), custom_call_target="tpu_custom_call" | custom-call | flops 7247757312 | bytes 20000000 | tf_op jit(solution)/shard_map/input_grads/pallas_call | solution.py:543
  369.5 4.9 %collective-permute-done.44.refs_5_ = f32[224,768]{1,0:T(8,128)S(1)} collective-permute-done((f32[224,768]{1,0:T(8,128)S(1)}, f32[224,768]{1,0:T(8,128)S(1)}, u32[]{:S(2)}, u32[]{:S(2)}) %collective-permute-start.44) | collective-permute-done | bytes 688160 | tf_op jit(solution)/shard_map/ppermute | solution.py:576
  385.7 6.0 %spread.3 = (f32[768,768]{1,0:T(8,128)}, f32[768,768]{1,0:T(8,128)}, f32[192,768]{1,0:T(8,128)}, f32[8,768]{1,0:T(8,128)}) custom-call(s32[9]{0:T(128)} %stack.92.refs_0_.place_ref, f32[224,768]{1,0:T(8,128)} %copy-done.2, f32[224,768]{1,0:T(8,128)} %collective-permute-done.46.refs_2_, f32[224,768]{1,0:T(8,128)} %copy-done.8, f32[224,768]{1,0:T(8,128)} %copy-done.9, ...), custom_call_target="tpu_custom_call" | custom-call | bytes 11010048 | tf_op jit(solution)/shard_map/spread/pallas_call | solution.py:508
  (236 shorter events, 84.2 us)
Async XLA Ops:
  7.2 149.8 %all-gather.3.cloned.1.call-start = ((), (), s32[]{:S(2)}) async-start(), calls=%async_computation.2 | async-start | bytes 9732096 | tf_op jit(solution)/shard_map/all_gather | solution.py:688
  35.0 29.9 %all-to-all-start = ((f32[4,2,32,768]{3,2,1,0:T(8,128)}), f32[4,2,32,768]{3,2,1,0:T(8,128)S(1)}, u32[]{:S(2)}, u32[]{:S(2)}) async-start(f32[4,2,32,768]{3,2,1,0:T(8,128)} %broadcast_in_dim.77), calls=%async_computation | async-start | bytes 1572864 | tf_op jit(solution)/shard_map/all_to_all | solution.py:583
  66.2 54.8 %all-to-all-start.1 = ((f32[4,96,768]{2,1,0:T(8,128)}), f32[4,96,768]{2,1,0:T(8,128)S(1)}, u32[]{:S(2)}, u32[]{:S(2)}) async-start(f32[4,96,768]{2,1,0:T(8,128)} %broadcast_in_dim.78), calls=%async_computation.1 | async-start | bytes 2359296 | tf_op jit(solution)/shard_map/all_to_all | solution.py:583
  70.0 17.5 %collective-permute-start.12 = (f32[3,2,32,768]{3,2,1,0:T(8,128)S(1)}, f32[3,2,32,768]{3,2,1,0:T(8,128)S(1)}, u32[]{:S(2)}, u32[]{:S(2)}) collective-permute-start(f32[3,2,32,768]{3,2,1,0:T(8,128)S(1)} %pad_maximum_fusion.2.refs_5_), channel_id=1, source_target_pairs={{0,16},{4,20},{8,24},{12,28},{16,0},{20,4},{24,8},{28,12},{1,17},{... | collective-permute-start | bytes 1769480 | tf_op jit(solution)/shard_map/ppermute | solution.py:576
  72.4 32.4 %collective-permute-start.10 = (f32[3,2,32,768]{3,2,1,0:T(8,128)S(1)}, f32[3,2,32,768]{3,2,1,0:T(8,128)}, u32[]{:S(2)}, u32[]{:S(2)}) collective-permute-start(f32[3,2,32,768]{3,2,1,0:T(8,128)S(1)} %pad_maximum_fusion.2.refs_5_), channel_id=1, source_target_pairs={{0,4},{4,0},{8,12},{12,8},{16,20},{20,16},{24,28},{28,24},{1,5},{5... | collective-permute-start | bytes 1769480 | tf_op jit(solution)/shard_map/ppermute | solution.py:576
  121.2 21.8 %collective-permute-start.20 = (f32[3,96,768]{2,1,0:T(8,128)S(1)}, f32[3,96,768]{2,1,0:T(8,128)S(1)}, u32[]{:S(2)}, u32[]{:S(2)}) collective-permute-start(f32[3,96,768]{2,1,0:T(8,128)S(1)} %pad_maximum_fusion.1.refs_10_), channel_id=1, source_target_pairs={{0,16},{4,20},{8,24},{12,28},{16,0},{20,4},{24,8},{28,12},{1,17},{... | collective-permute-start | bytes 2654216 | tf_op jit(solution)/shard_map/ppermute | solution.py:576
  122.1 21.5 %collective-permute-start.19 = (f32[3,96,768]{2,1,0:T(8,128)S(1)}, f32[3,96,768]{2,1,0:T(8,128)}, u32[]{:S(2)}, u32[]{:S(2)}) collective-permute-start(f32[3,96,768]{2,1,0:T(8,128)S(1)} %pad_maximum_fusion.1.refs_10_), channel_id=1, source_target_pairs={{0,8},{4,12},{8,0},{12,4},{16,24},{20,28},{24,16},{28,20},{1,9},{5... | collective-permute-start | bytes 2654216 | tf_op jit(solution)/shard_map/ppermute | solution.py:576
  147.8 43.3 %collective-permute-start.21 = (f32[3,96,768]{2,1,0:T(8,128)S(1)}, f32[3,96,768]{2,1,0:T(8,128)}, u32[]{:S(2)}, u32[]{:S(2)}) collective-permute-start(f32[3,96,768]{2,1,0:T(8,128)S(1)} %pad_maximum_fusion.1.refs_10_), channel_id=1, source_target_pairs={{0,4},{4,0},{8,12},{12,8},{16,20},{20,16},{24,28},{28,24},{1,5},{5... | collective-permute-start | bytes 2654216 | tf_op jit(solution)/shard_map/ppermute | solution.py:576
  147.8 43.4 %collective-permute-start.22 = (f32[3,96,768]{2,1,0:T(8,128)}, f32[3,96,768]{2,1,0:T(8,128)}, u32[]{:S(2)}, u32[]{:S(2)}) collective-permute-start(f32[3,96,768]{2,1,0:T(8,128)} %collective-permute-done.19.refs_12_), channel_id=1, source_target_pairs={{0,4},{4,0},{8,12},{12,8},{16,20},{20,16},{24,28},{28,24},{1,5},{5... | collective-permute-start | bytes 2654216 | tf_op jit(solution)/shard_map/ppermute | solution.py:576
  148.4 42.9 %collective-permute-start.23 = (f32[3,96,768]{2,1,0:T(8,128)S(1)}, f32[3,96,768]{2,1,0:T(8,128)}, u32[]{:S(2)}, u32[]{:S(2)}) collective-permute-start(f32[3,96,768]{2,1,0:T(8,128)S(1)} %collective-permute-done.20.refs_14_), channel_id=1, source_target_pairs={{0,4},{4,0},{8,12},{12,8},{16,20},{20,16},{24,28},{28,24},{1,5},{5... | collective-permute-start | bytes 2654216 | tf_op jit(solution)/shard_map/ppermute | solution.py:576
  154.9 36.3 %collective-permute-start.25 = (f32[3,48,768]{2,1,0:T(8,128)}, f32[3,48,768]{2,1,0:T(8,128)S(1)}, u32[]{:S(2)}, u32[]{:S(2)}) collective-permute-start(f32[3,48,768]{2,1,0:T(8,128)} %collective-permute-done.24.refs_16_), channel_id=1, source_target_pairs={{0,4},{4,0},{8,12},{12,8},{16,20},{20,16},{24,28},{28,24},{1,5},{5... | collective-permute-start | bytes 1327112 | tf_op jit(solution)/shard_map/ppermute | solution.py:576
  156.9 34.2 %collective-permute-start.27 = (f32[3,48,768]{2,1,0:T(8,128)}, f32[3,48,768]{2,1,0:T(8,128)S(1)}, u32[]{:S(2)}, u32[]{:S(2)}) collective-permute-start(f32[3,48,768]{2,1,0:T(8,128)} %collective-permute-done.26.refs_18_), channel_id=1, source_target_pairs={{0,4},{4,0},{8,12},{12,8},{16,20},{20,16},{24,28},{28,24},{1,5},{5... | collective-permute-start | bytes 1327112 | tf_op jit(solution)/shard_map/ppermute | solution.py:576
  258.1 35.2 %collective-permute-start.39 = (f32[4,224,768]{2,1,0:T(8,128)}, f32[4,224,768]{2,1,0:T(8,128)}, u32[]{:S(2)}, u32[]{:S(2)}) collective-permute-start(f32[4,224,768]{2,1,0:T(8,128)} %get-tuple-element.132), channel_id=1, source_target_pairs={{0,4},{4,0},{8,12},{12,8},{16,20},{20,16},{24,28},{28,24},{1,5},{5... | collective-permute-start | bytes 8257544 | tf_op jit(solution)/shard_map/ppermute | solution.py:576
  291.2 20.1 %collective-permute-start.30 = (f32[80,768]{1,0:T(8,128)}, f32[80,768]{1,0:T(8,128)}, u32[]{:S(2)}, u32[]{:S(2)}) collective-permute-start(f32[80,768]{1,0:T(8,128)} %get-tuple-element.156), channel_id=1, source_target_pairs={{0,16},{4,20},{8,24},{12,28},{16,0},{20,4},{24,8},{28,12},{1,17},{... | collective-permute-start | bytes 737288 | tf_op jit(solution)/shard_map/ppermute | solution.py:576
  292.0 19.3 %collective-permute-start.29 = (f32[80,768]{1,0:T(8,128)S(1)}, f32[80,768]{1,0:T(8,128)}, u32[]{:S(2)}, u32[]{:S(2)}) collective-permute-start(f32[80,768]{1,0:T(8,128)S(1)} %get-tuple-element.157), channel_id=1, source_target_pairs={{0,8},{4,12},{8,0},{12,4},{16,24},{20,28},{24,16},{28,20},{1,9},{5... | collective-permute-start | bytes 737288 | tf_op jit(solution)/shard_map/ppermute | solution.py:576
  296.2 23.5 %collective-permute-start.42 = (f32[224,768]{1,0:T(8,128)}, f32[224,768]{1,0:T(8,128)}, u32[]{:S(2)}, u32[]{:S(2)}) collective-permute-start(f32[224,768]{1,0:T(8,128)} %get-tuple-element.152), channel_id=1, source_target_pairs={{0,24},{4,28},{8,16},{12,20},{16,8},{20,12},{24,0},{28,4},{1,25},{... | collective-permute-start | bytes 2064392 | tf_op jit(solution)/shard_map/ppermute | solution.py:576
  297.6 36.6 %collective-permute-start.41 = (f32[224,768]{1,0:T(8,128)}, f32[224,768]{1,0:T(8,128)}, u32[]{:S(2)}, u32[]{:S(2)}) collective-permute-start(f32[224,768]{1,0:T(8,128)} %get-tuple-element.153), channel_id=1, source_target_pairs={{0,16},{4,20},{8,24},{12,28},{16,0},{20,4},{24,8},{28,12},{1,17},{... | collective-permute-start | bytes 2064392 | tf_op jit(solution)/shard_map/ppermute | solution.py:576
  299.6 34.6 %collective-permute-start.40 = (f32[224,768]{1,0:T(8,128)}, f32[224,768]{1,0:T(8,128)}, u32[]{:S(2)}, u32[]{:S(2)}) collective-permute-start(f32[224,768]{1,0:T(8,128)} %get-tuple-element.154), channel_id=1, source_target_pairs={{0,8},{4,12},{8,0},{12,4},{16,24},{20,28},{24,16},{28,20},{1,9},{5... | collective-permute-start | bytes 2064392 | tf_op jit(solution)/shard_map/ppermute | solution.py:576
  312.7 38.6 %collective-permute-start.34 = (f32[80,768]{1,0:T(8,128)S(1)}, f32[80,768]{1,0:T(8,128)}, u32[]{:S(2)}, u32[]{:S(2)}) collective-permute-start(f32[80,768]{1,0:T(8,128)S(1)} %fusion.3.refs_1_), channel_id=1, source_target_pairs={{0,24},{4,28},{8,16},{12,20},{16,8},{20,12},{24,0},{28,4},{1,25},{... | collective-permute-start | bytes 737288 | tf_op jit(solution)/shard_map/ppermute | solution.py:576
  336.1 33.3 %collective-permute-start.45 = (f32[224,768]{1,0:T(8,128)S(1)}, f32[224,768]{1,0:T(8,128)S(1)}, u32[]{:S(2)}, u32[]{:S(2)}) collective-permute-start(f32[224,768]{1,0:T(8,128)S(1)} %fusion.1.refs_1_), channel_id=1, source_target_pairs={{0,24},{4,28},{8,16},{12,20},{16,8},{20,12},{24,0},{28,4},{1,25},{... | collective-permute-start | bytes 2064392 | tf_op jit(solution)/shard_map/ppermute | solution.py:576
  348.5 20.3 %collective-permute-start.33 = (f32[80,768]{1,0:T(8,128)S(1)}, f32[80,768]{1,0:T(8,128)S(1)}, u32[]{:S(2)}, u32[]{:S(2)}) collective-permute-start(f32[80,768]{1,0:T(8,128)S(1)} %fusion.3.refs_1_), channel_id=1, source_target_pairs={{0,16},{4,20},{8,24},{12,28},{16,0},{20,4},{24,8},{28,12},{1,17},{... | collective-permute-start | bytes 737288 | tf_op jit(solution)/shard_map/ppermute | solution.py:576
  349.3 19.5 %collective-permute-start.32 = (f32[80,768]{1,0:T(8,128)S(1)}, f32[80,768]{1,0:T(8,128)S(1)}, u32[]{:S(2)}, u32[]{:S(2)}) collective-permute-start(f32[80,768]{1,0:T(8,128)S(1)} %fusion.3.refs_1_), channel_id=1, source_target_pairs={{0,8},{4,12},{8,0},{12,4},{16,24},{20,28},{24,16},{28,20},{1,9},{5... | collective-permute-start | bytes 737288 | tf_op jit(solution)/shard_map/ppermute | solution.py:576
  350.6 23.8 %collective-permute-start.44 = (f32[224,768]{1,0:T(8,128)S(1)}, f32[224,768]{1,0:T(8,128)S(1)}, u32[]{:S(2)}, u32[]{:S(2)}) collective-permute-start(f32[224,768]{1,0:T(8,128)S(1)} %fusion.1.refs_1_), channel_id=1, source_target_pairs={{0,16},{4,20},{8,24},{12,28},{16,0},{20,4},{24,8},{28,12},{1,17},{... | collective-permute-start | bytes 2064392 | tf_op jit(solution)/shard_map/ppermute | solution.py:576
  351.3 23.1 %collective-permute-start.43 = (f32[224,768]{1,0:T(8,128)S(1)}, f32[224,768]{1,0:T(8,128)S(1)}, u32[]{:S(2)}, u32[]{:S(2)}) collective-permute-start(f32[224,768]{1,0:T(8,128)S(1)} %fusion.1.refs_1_), channel_id=1, source_target_pairs={{0,8},{4,12},{8,0},{12,4},{16,24},{20,28},{24,16},{28,20},{1,9},{5... | collective-permute-start | bytes 2064392 | tf_op jit(solution)/shard_map/ppermute | solution.py:576
  (60 other events, 764.3 us)
Sparse Core Ops, SparseCore 0:
  26.1 106.3 all-gather.2

commit v3 on v2

v3 whole, which is shorter than its diff:
```python
import jax
import jax.numpy as jnp
from jax import lax
from jax.experimental import pallas as pl
from jax.experimental.pallas import tpu as pltpu
from jax.sharding import PartitionSpec as P

HD = 64
GROUP = 8
EXTRA = 16
MASK = -float(2**30)
EPS = 1e-12
F32 = jnp.float32
BF16 = jnp.bfloat16
LIMIT = 60 << 20


def dot(left, right, left_dim, right_dim):
    return lax.dot_general(
        left, right, (((left_dim,), (right_dim,)), ((), ())), preferred_element_type=F32
    )


def params():
    return pltpu.CompilerParams(vmem_limit_bytes=LIMIT)


def cost(flops, moved):
    return pl.CostEstimate(flops=int(flops), bytes_accessed=int(moved), transcendentals=0)


def whole(shape):
    zeros = (0,) * len(shape)
    return pl.BlockSpec(shape, lambda *_: zeros, pipeline_mode=pl.Buffered(1))


def split3(row):
    high = row.astype(BF16).astype(F32)
    rest = row - high
    mid = rest.astype(BF16).astype(F32)
    return high, mid, rest - mid


def rows_of(height, first, parts, width):
    place = lax.broadcasted_iota(jnp.int32, (height, width), 0)
    out = jnp.zeros((height, width), F32)
    for i, part in enumerate(parts):
        out = jnp.where(place == first + i, part, out)
    return out


def put(out_ref, start, values, step):
    rows = pl.ds(pl.multiple_of(start, step), values.shape[0])
    out_ref[rows, :] = values.astype(out_ref.dtype)


def peer_shard(place_ref, shards, k):
    return lax.rem(place_ref[GROUP] + shards - k, shards)


def own_block(*shape):
    return pl.BlockSpec(shape, lambda i, p: (p[GROUP],) + (0,) * (len(shape) - 2) + (i,))


def peer_block(peers, first, *shape):
    middle = (0,) * (len(shape) - 2)
    return pl.BlockSpec(
        shape, lambda k, i, p: (lax.rem(p[GROUP] + peers - first - k, peers),) + middle + (i,)
    )


ANY = pl.BlockSpec(memory_space=pl.ANY)


def shift_matrix(amount, length, forward):
    row = lax.broadcasted_iota(jnp.int32, (length, length), 0)
    column = lax.broadcasted_iota(jnp.int32, (length, length), 1)
    apart = column - row if forward else row - column
    return jnp.where((apart == amount) | (apart == amount - length), 1.0, 0.0).astype(BF16)


def shift_kernel(place_ref, first_ref, second_ref, first_out, second_out):
    length = first_ref.shape[0]
    amount = place_ref[GROUP + 1 + pl.program_id(0)]
    matrix = shift_matrix(amount, length, True)
    first_out[...] = dot(matrix, first_ref[...], 1, 0).astype(BF16)
    second_out[...] = dot(matrix, second_ref[...], 1, 0).astype(BF16)


def shift(place, length, first, second):
    tokens, width = first.shape
    by_row = lambda: pl.BlockSpec((length, width), lambda i, *_: (i, 0))
    return pl.pallas_call(
        shift_kernel,
        grid_spec=pltpu.PrefetchScalarGridSpec(
            num_scalar_prefetch=1,
            grid=(tokens // length,),
            in_specs=[by_row(), by_row()],
            out_specs=[by_row(), by_row()],
        ),
        out_shape=[jax.ShapeDtypeStruct((tokens, width), BF16)] * 2,
        compiler_params=params(),
        cost_estimate=cost(4 * tokens * length * width, 12e6),
        name="shift",
    )(place, first, second)


def unshift_kernel(place_ref, in_ref, out_ref):
    length = in_ref.shape[0]
    matrix = shift_matrix(place_ref[GROUP + 1 + pl.program_id(0)], length, False)
    out_ref[...] = dot(matrix, in_ref[...], 1, 0).astype(BF16)


def unshift(place, length, shifted):
    tokens, width = shifted.shape
    by_row = lambda: pl.BlockSpec((length, width), lambda i, *_: (i, 0))
    return pl.pallas_call(
        unshift_kernel,
        grid_spec=pltpu.PrefetchScalarGridSpec(
            num_scalar_prefetch=1,
            grid=(tokens // length,),
            in_specs=[by_row()],
            out_specs=by_row(),
        ),
        out_shape=jax.ShapeDtypeStruct((tokens, width), BF16),
        compiler_params=params(),
        cost_estimate=cost(2 * tokens * length * width, 6e6),
        name="unshift",
    )(place, shifted)


def tiles(heads, block):
    return [(h, slice(i * block, (i + 1) * block)) for h in range(heads) for i in range(2)]


def attend_rows(x_ref, bias_ref, qf_ref, kf_ref, w_scr, qkv_ref, ctx_ref, aug_ref):
    heads = ctx_ref.shape[0]
    length = x_ref.shape[0]
    block = length // 2
    span = 3 * HD
    proj = dot(w_scr[...], x_ref[...], 1, 1)
    scale = HD ** (-0.5)
    for h in range(heads):
        part = proj[h * span : (h + 1) * span] + bias_ref[h]
        qkv_ref[h, :HD, :] = (part[:HD] * scale).astype(BF16)
        qkv_ref[h, HD:, :] = part[HD:].astype(BF16)
    ones_rows = rows_of(EXTRA, 0, (jnp.ones((1, block), F32),), block).astype(BF16)
    items = tiles(heads, block)
    scores = []
    for h, at in items:
        queries = jnp.concatenate([qkv_ref[h, :HD, at], qf_ref[:, at]], axis=0)
        keys = jnp.concatenate([qkv_ref[h, HD : 2 * HD, at], kf_ref[:, at]], axis=0)
        scores.append(dot(keys, queries, 0, 0))
    highest = [jnp.max(part, axis=0, keepdims=True) for part in scores]
    weight = [jnp.exp(part - top).astype(BF16) for part, top in zip(scores, highest)]
    context = []
    for (h, at), part in zip(items, weight):
        values = jnp.concatenate([qkv_ref[h, 2 * HD :, at], ones_rows], axis=0)
        context.append(dot(values, part, 1, 0))
    for (h, at), part, top in zip(items, context, highest):
        total = part[HD : HD + 1]
        ctx_ref[h, :, at] = (part[:HD] * (1.0 / total)).astype(BF16)
        log_total = top + jnp.log(total)
        extra = rows_of(EXTRA, 4, split3(-log_total), block)
        aug_ref[h, :, at] = (extra + qf_ref[:, at].astype(F32)).astype(BF16)


def attend_own_kernel(place_ref, x_ref, bias_ref, qf_ref, kf_ref, own_ref, *refs):
    w_ref, qkv_ref, ctx_ref, aug_ref = refs

    @pl.when(pl.program_id(0) == 0)
    def _():
        w_ref[...] = own_ref[...]

    attend_rows(x_ref, bias_ref, qf_ref, kf_ref, own_ref, qkv_ref, ctx_ref, aug_ref)


def attend_own(length, peers, place, inputs, bias, qf, kf, own):
    height = own.shape[0]
    heads = height // (3 * HD)
    tokens, width = inputs.shape
    every = peers * heads
    shapes = [(peers * height, width)] + [(every, n, tokens) for n in (3 * HD, HD, EXTRA)]
    by_row = pl.BlockSpec((EXTRA, length), lambda i, *_: (0, i))
    return pl.pallas_call(
        attend_own_kernel,
        grid_spec=pltpu.PrefetchScalarGridSpec(
            num_scalar_prefetch=1,
            grid=(tokens // length,),
            in_specs=[
                pl.BlockSpec((length, width), lambda i, *_: (i, 0)),
                whole(bias.shape),
                by_row,
                by_row,
                whole(own.shape),
            ],
            out_specs=[
                pl.BlockSpec((height, width), lambda i, p: (p[GROUP], 0)),
                *[own_block(heads, n, length) for n in (3 * HD, HD, EXTRA)],
            ],
        ),
        out_shape=[jax.ShapeDtypeStruct(shape, BF16) for shape in shapes],
        compiler_params=params(),
        cost_estimate=cost(heads * tokens * (6 * HD * width + 16 * 64 * length), 12e6),
        name="attend_own",
    )(place, inputs, bias, qf, kf, own)


def attend_peers_kernel(spots, place_ref, x_ref, bias_ref, qf_ref, kf_ref, *refs):
    count = len(spots)
    parts = refs[:count]
    w_ref, qkv_ref, ctx_ref, aug_ref, wide_scr = refs[count + 4 :]

    @pl.when(pl.program_id(1) == 0)
    def _():
        size = w_ref.shape[0] // GROUP
        for ref, (index, offset) in zip(parts, spots):
            put(wide_scr, place_ref[index] * size + offset, ref[0], 8)
        w_ref[...] = wide_scr[...].astype(BF16)

    attend_rows(x_ref, bias_ref.at[0], qf_ref, kf_ref, w_ref, qkv_ref, ctx_ref, aug_ref)


def attend_peers(length, peers, place, inputs, bias, qf, kf, pieces, arrays):
    heads = arrays[1].shape[0] // peers
    height = arrays[0].shape[0] // peers
    tokens, width = inputs.shape
    spots = [(index, offset) for _, index, offset in pieces]
    parts = [array for array, _, _ in pieces]
    by_row = pl.BlockSpec((EXTRA, length), lambda k, i, *_: (0, i))
    return pl.pallas_call(
        lambda *refs: attend_peers_kernel(spots, *refs),
        grid_spec=pltpu.PrefetchScalarGridSpec(
            num_scalar_prefetch=1,
            grid=(peers - 1, tokens // length),
            in_specs=[
                pl.BlockSpec((length, width), lambda k, i, *_: (i, 0)),
                pl.BlockSpec((1,) + bias.shape[1:], lambda k, i, *_: (k, 0, 0, 0)),
                by_row,
                by_row,
                *[
                    pl.BlockSpec((1,) + a.shape[1:], lambda k, i, *_: (k, 0, 0)) for a in parts
                ],
                *[ANY] * 4,
            ],
            out_specs=[
                pl.BlockSpec(
                    (height, width), lambda k, i, p: (lax.rem(p[GROUP] + peers - 1 - k, peers), 0)
                ),
                *[peer_block(peers, 1, heads, n, length) for n in (3 * HD, HD, EXTRA)],
            ],
            scratch_shapes=[pltpu.VMEM((height, width), F32)],
        ),
        out_shape=[jax.ShapeDtypeStruct(a.shape, a.dtype) for a in arrays],
        input_output_aliases={5 + len(parts) + i: i for i in range(4)},
        compiler_params=params(),
        cost_estimate=cost(
            (peers - 1) * heads * tokens * (6 * HD * width + 16 * 64 * length), 30e6
        ),
        name="attend_peers",
    )(place, inputs, bias, qf, kf, *parts, *arrays)


def attend_back_rows(qkv_ref, ctx_ref, aug_ref, grad_ref, kf_ref, out_ref):
    heads, _, length = ctx_ref.shape
    block = length // 2
    scale = HD ** (-0.5)
    one = jnp.ones((1, block), F32)
    ones_rows = rows_of(EXTRA, 0, (one, one, one), block).astype(BF16)
    items = tiles(heads, block)
    scores, spreads = [], []
    for h, at in items:
        scores.append(
            dot(
                jnp.concatenate([qkv_ref[h, HD : 2 * HD, at], kf_ref[:, at]], axis=0),
                jnp.concatenate([qkv_ref[h, :HD, at], aug_ref[h, :, at]], axis=0),
                0,
                0,
            )
        )
    for h, at in items:
        grad = grad_ref[h, :, at]
        inner = jnp.sum(grad.astype(F32) * ctx_ref[h, :, at].astype(F32), axis=0, keepdims=True)
        grad_extra = rows_of(EXTRA, 0, split3(-inner), block).astype(BF16)
        spreads.append(
            dot(
                jnp.concatenate([qkv_ref[h, 2 * HD :, at], ones_rows], axis=0),
                jnp.concatenate([grad, grad_extra], axis=0),
                0,
                0,
            )
        )
    probs = [jnp.exp(part) for part in scores]
    slopes = [(part * spread).astype(BF16) for part, spread in zip(probs, spreads)]
    probs = [part.astype(BF16) for part in probs]
    for (h, at), part in zip(items, probs):
        out_ref[h, 2 * HD :, at] = dot(grad_ref[h, :, at], part, 1, 1).astype(BF16)
    for (h, at), part in zip(items, slopes):
        out_ref[h, HD : 2 * HD, at] = dot(qkv_ref[h, :HD, at], part, 1, 1).astype(BF16)
    for (h, at), part in zip(items, slopes):
        grad = dot(qkv_ref[h, HD : 2 * HD, at], part, 1, 0)
        out_ref[h, :HD, at] = (grad * scale).astype(BF16)


def attend_back_own_kernel(place_ref, qkv_ref, ctx_ref, aug_ref, grad_ref, kf_ref, *refs):
    x_ref, dwo_ref, small_ref, early_ref, out_ref, mine_ref, send_ref, grad_scr, sum_scr = refs
    heads = ctx_ref.shape[0]
    height = heads * HD
    step = pl.program_id(0)

    @pl.when(step == 0)
    def _():
        grad_scr[...] = jnp.zeros_like(grad_scr)
        sum_scr[...] = jnp.zeros_like(sum_scr)

    attend_back_rows(qkv_ref, ctx_ref, aug_ref, grad_ref, kf_ref, out_ref)
    ones = jnp.ones((8, x_ref.shape[0]), BF16)
    row = lax.broadcasted_iota(jnp.int32, (8, 3 * HD), 0)
    sums = jnp.zeros((8, 3 * HD), F32)
    for h in range(heads):
        grad = dot(out_ref[h], x_ref[...], 1, 0)
        for i in range(3):
            grad_scr[i * height + h * HD : i * height + (h + 1) * HD, :] += grad[
                i * HD : (i + 1) * HD
            ]
        sums = jnp.where(row == 3 + h, dot(ones, out_ref[h], 1, 1), sums)
    sum_scr[:, : 3 * HD] += sums

    @pl.when(step == pl.num_programs(0) - 1)
    def _():
        size, size_two = 3 * height // GROUP, height // GROUP
        top = size + size_two
        for rel in range(4):
            for source, ref in enumerate((mine_ref, send_ref)):
                owner = place_ref[2 * rel + source]
                ref[rel, :size, :] = grad_scr[pl.ds(pl.multiple_of(owner * size, 8), size), :]
                start = pl.multiple_of(owner * size_two, 8)
                ref[rel, size:top, :] = dwo_ref[pl.ds(start, size_two), :]
                ref[rel, top : top + 8, :] = jnp.where(
                    owner == 0, small_ref[...] + sum_scr[...], 0.0
                )
                ref[rel, top + 8 :, :] = jnp.where(owner == 0, early_ref[...], 0.0)


def attend_back_own(length, place, qkv, ctx, aug, grad, kf, inputs, dwo, small, early):
    height, width = dwo.shape
    heads = height // HD
    tokens = inputs.shape[0]
    share = 4 * height // GROUP + 16
    return pl.pallas_call(
        attend_back_own_kernel,
        grid_spec=pltpu.PrefetchScalarGridSpec(
            num_scalar_prefetch=1,
            grid=(tokens // length,),
            in_specs=[
                own_block(heads, 3 * HD, length),
                own_block(heads, HD, length),
                own_block(heads, EXTRA, length),
                own_block(heads, HD, length),
                pl.BlockSpec((EXTRA, length), lambda i, *_: (0, i)),
                pl.BlockSpec((length, width), lambda i, *_: (i, 0)),
                whole(dwo.shape),
                whole(small.shape),
                whole(early.shape),
            ],
            out_specs=[
                own_block(heads, 3 * HD, length),
                whole((4, share, width)),
                whole((4, share, width)),
            ],
            scratch_shapes=[pltpu.VMEM((3 * height, width), F32), pltpu.VMEM((8, width), F32)],
        ),
        out_shape=[jax.ShapeDtypeStruct(qkv.shape, BF16)]
        + [jax.ShapeDtypeStruct((4, share, width), F32)] * 2,
        compiler_params=params(),
        cost_estimate=cost(heads * tokens * (20 * 64 * length + 6 * HD * width), 12e6),
        name="attend_back_own",
    )(place, qkv, ctx, aug, grad, kf, inputs, dwo, small, early)


def attend_back_kernel(place_ref, qkv_ref, ctx_ref, aug_ref, grad_ref, kf_ref, old_ref, out_ref):
    attend_back_rows(qkv_ref, ctx_ref, aug_ref, grad_ref, kf_ref, out_ref)


def attend_back(length, peers, first, count, place, qkv, ctx, aug, grad, kf, out):
    every, _, tokens = qkv.shape
    heads = every // peers
    by_peer = lambda n: peer_block(peers, first, heads, n, length)
    return pl.pallas_call(
        attend_back_kernel,
        grid_spec=pltpu.PrefetchScalarGridSpec(
            num_scalar_prefetch=1,
            grid=(count, tokens // length),
            in_specs=[
                by_peer(3 * HD),
                by_peer(HD),
                by_peer(EXTRA),
                by_peer(HD),
                pl.BlockSpec((EXTRA, length), lambda k, i, *_: (0, i)),
                ANY,
            ],
            out_specs=by_peer(3 * HD),
        ),
        out_shape=jax.ShapeDtypeStruct(out.shape, BF16),
        input_output_aliases={6: 0},
        compiler_params=params(),
        cost_estimate=cost(count * heads * tokens * 20 * 64 * length, 12e6),
        name="attend_back",
    )(place, qkv, ctx, aug, grad, kf, out)


def norm_forward(hidden):
    center = hidden - jnp.mean(hidden, axis=-1, keepdims=True)
    inverse = lax.rsqrt(jnp.mean(center * center, axis=-1, keepdims=True) + EPS)
    return center * inverse, inverse


def norm_backward(grad, gain, norm, inverse):
    scaled = grad * gain
    first = jnp.mean(scaled, axis=-1, keepdims=True)
    second = jnp.mean(scaled * norm, axis=-1, keepdims=True)
    return (scaled - first - norm * second) * inverse


def column_sum(values):
    return jnp.sum(values, axis=0, keepdims=True)


def flat(values):
    return values.reshape(-1, values.shape[-1])


def expand_kernel(spots, place_ref, x_ref, ctx_ref, bias_ref, vec_ref, own_ref, own_wo_ref, *refs):
    parts, refs = refs[: len(spots)], refs[len(spots) :]
    sum_ref, act_ref, slope_ref, we_ref, wo_ref, wide_scr = refs
    shards, width, _ = we_ref.shape
    size, size_two = width // GROUP, wo_ref.shape[0] // (shards * GROUP)

    @pl.when(pl.program_id(0) == 0)
    def _():
        me = place_ref[GROUP]
        we_ref[me] = own_ref[...]
        put(wide_scr, me * size_two * GROUP, own_wo_ref[...], 8)
        for k in range(1, shards):
            shard = peer_shard(place_ref, shards, k)
            for ref, (index, offset) in zip(parts, spots):
                part = ref[k - 1]
                count = min(part.shape[0], size - offset)
                put(we_ref.at[shard], place_ref[index] * size + offset, part[:count], 16)
                if count < part.shape[0]:
                    start = (shard * GROUP + place_ref[index]) * size_two
                    put(wide_scr, start, part[count:], 8)
        wo_ref[...] = wide_scr[...].astype(BF16)

    b_output, gain_one, shift_one = vec_ref[0:1], vec_ref[1:2], vec_ref[2:3]
    half = x_ref.shape[0] // 2
    halves = [slice(0, half), slice(half, 2 * half)]
    attended = [dot(flat(ctx_ref[:, :, at]), wo_ref[...], 0, 0) for at in halves]
    low = []
    for at, part in zip(halves, attended):
        residual = x_ref[at, :].astype(F32) + (part + b_output)
        sum_ref[at, :] = residual
        norm_one, _ = norm_forward(residual)
        low.append((norm_one * gain_one + shift_one).astype(BF16))
    items = [(s, i) for s in range(shards) for i in range(2)]
    ahead = dot(low[0], we_ref[0], 1, 0)
    for n, (s, i) in enumerate(items):
        hidden = ahead + bias_ref[peer_shard(place_ref, shards, s), 1:2]
        if n + 1 < len(items):
            s_next, i_next = items[n + 1]
            ahead = dot(low[i_next], we_ref[s_next], 1, 0)
        square = hidden * hidden
        bent = jnp.tanh(hidden * (0.7978845608028654 + 0.035677408136300125 * square))
        gate = 0.5 + 0.5 * bent
        active = hidden * gate
        act_ref[s, halves[i], :] = active.astype(BF16)
        slope = gate + (active * (1.0 - gate)) * (1.5957691216057308 + 0.21406444881780075 * square)
        slope_ref[s, halves[i], :] = slope.astype(BF16)


def expand(place, inputs, ctx, biases, vectors, own, own_wo, pieces, shards):
    tokens, width = inputs.shape
    hidden = own.shape[1]
    every = ctx.shape[0]
    block = 512
    spots = [(index, offset) for _, index, offset in pieces]
    parts = [array for array, _, _ in pieces]
    full = (shards, width, hidden)
    by_token = lambda: pl.BlockSpec((block, width), lambda i, *_: (i, 0))
    by_shard = lambda: pl.BlockSpec((shards, block, hidden), lambda i, *_: (0, i, 0))
    return pl.pallas_call(
        lambda *refs: expand_kernel(spots, *refs),
        grid_spec=pltpu.PrefetchScalarGridSpec(
            num_scalar_prefetch=1,
            grid=(tokens // block,),
            in_specs=[
                by_token(),
                pl.BlockSpec((every, HD, block), lambda i, *_: (0, 0, i)),
                whole(biases.shape),
                whole(vectors.shape),
                whole(own.shape),
                whole(own_wo.shape),
                *[whole(a.shape) for a in parts],
            ],
            out_specs=[
                by_token(),
                by_shard(),
                by_shard(),
                whole(full),
                whole((every * HD, width)),
            ],
            scratch_shapes=[pltpu.VMEM((every * HD, width), F32)],
        ),
        out_shape=[
            jax.ShapeDtypeStruct((tokens, width), F32),
            jax.ShapeDtypeStruct((shards, tokens, hidden), BF16),
            jax.ShapeDtypeStruct((shards, tokens, hidden), BF16),
            jax.ShapeDtypeStruct(full, BF16),
            jax.ShapeDtypeStruct((every * HD, width), BF16),
        ],
        compiler_params=params(),
        cost_estimate=cost(2 * tokens * width * (shards * hidden + every * HD), 40e6),
        name="expand",
    )(place, inputs, ctx, biases, vectors, own, own_wo, *parts)


def reduce_kernel(spots, place_ref, sum_ref, cot_ref, act_ref, slope_ref, vec_ref, *refs):
    own_ref, refs = refs[0], refs[1:]
    piece_refs, refs = refs[: len(spots)], refs[len(spots) :]
    out_ref, g2_ref, wr_ref, mine_ref, send_ref, small_scr, dwe_scr, dwr_scr = refs
    step = pl.program_id(0)
    shards = act_ref.shape[0]
    me = place_ref[GROUP]

    @pl.when(step == 0)
    def _():
        wr_ref[me] = own_ref[...]
        for k in range(1, shards):
            shard = peer_shard(place_ref, shards, k)
            for ref, (index, offset) in zip(piece_refs, spots):
                start = place_ref[index] * (wr_ref.shape[1] // GROUP) + offset
                put(wr_ref.at[shard], start, ref[k - 1], 16)
        for scr in (dwe_scr, dwr_scr, small_scr):
            scr[...] = jnp.zeros_like(scr)

    gain_one, shift_one = vec_ref[1:2], vec_ref[2:3]
    b_reduce, gain_two, shift_two = vec_ref[3:4], vec_ref[4:5], vec_ref[5:6]
    half = sum_ref.shape[0] // 2
    halves = [slice(0, half), slice(half, 2 * half)]
    mixed = []
    for at in halves:
        part = dot(act_ref[0, at, :], wr_ref[0], 1, 0)
        for s in range(1, shards):
            part = part + dot(act_ref[s, at, :], wr_ref[s], 1, 0)
        mixed.append(part)
    small = [jnp.zeros((1, sum_ref.shape[1]), F32)] * 4
    low, normed_low, active = [], [], []
    for at, part in zip(halves, mixed):
        norm_one, _ = norm_forward(sum_ref[at, :])
        normed = norm_one * gain_one + shift_one
        normed_low.append(normed.astype(BF16))
        norm_two, inverse_two = norm_forward(normed + (part + b_reduce))
        out_ref[at, :] = (norm_two * gain_two + shift_two).astype(BF16)
        cot = cot_ref[at, :].astype(F32)
        grad_two = norm_backward(cot, gain_two, norm_two, inverse_two)
        g2_ref[at, :] = grad_two
        low.append(grad_two.astype(BF16))
        active.append(dot(low[-1], own_ref[...], 1, 1))
        small[0] = small[0] + column_sum(grad_two)
        small[1] = small[1] + column_sum(cot * norm_two)
        small[2] = small[2] + column_sum(cot)
    dwr_scr[...] += dot(act_ref[me], jnp.concatenate(low, axis=0), 0, 0)
    own = []
    for at, part in zip(halves, active):
        own.append((part * slope_ref[0, at, :].astype(F32)).astype(BF16))
        small[3] = small[3] + column_sum(own[-1].astype(F32))
    dwe_scr[...] += dot(
        jnp.concatenate(normed_low, axis=0), jnp.concatenate(own, axis=0), 0, 0
    )
    for n, part in enumerate(small):
        small_scr[n : n + 1] += part

    @pl.when(step == pl.num_programs(0) - 1)
    def _():
        for plane in range(4):
            for ref, core in ((mine_ref, place_ref[0]), (send_ref, place_ref[1])):
                owner = 2 * plane + lax.rem(core, 2)
                top = 0
                for scr in (dwe_scr, dwr_scr):
                    size = scr.shape[0] // GROUP
                    start = pl.multiple_of(owner * size, 8)
                    ref[plane, top : top + size, :] = scr[pl.ds(start, size), :]
                    top += size


def reduce(place, residual, cot, act, slope, vectors, own, pieces):
    tokens, width = residual.shape
    shards, _, hidden = act.shape
    block = 512
    share = (width + hidden) // GROUP
    spots = [(index, offset) for _, index, offset in pieces]
    arrays = [array for array, _, _ in pieces]
    by_token = lambda: pl.BlockSpec((block, width), lambda i, *_: (i, 0))
    return pl.pallas_call(
        lambda *refs: reduce_kernel(spots, *refs),
        grid_spec=pltpu.PrefetchScalarGridSpec(
            num_scalar_prefetch=1,
            grid=(tokens // block,),
            in_specs=[
                by_token(),
                by_token(),
                pl.BlockSpec((shards, block, hidden), lambda i, *_: (0, i, 0)),
                pl.BlockSpec((1, block, hidden), lambda i, p: (p[GROUP], i, 0)),
                whole(vectors.shape),
                whole(own.shape),
                *[whole(a.shape) for a in arrays],
            ],
            out_specs=[
                by_token(),
                by_token(),
                whole((shards, hidden, width)),
                whole((4, share, width)),
                whole((4, share, width)),
                whole((8, width)),
            ],
            scratch_shapes=[pltpu.VMEM((width, hidden), F32), pltpu.VMEM((hidden, width), F32)],
        ),
        out_shape=[
            jax.ShapeDtypeStruct((tokens, width), BF16),
            jax.ShapeDtypeStruct((tokens, width), F32),
            jax.ShapeDtypeStruct((shards, hidden, width), BF16),
            jax.ShapeDtypeStruct((4, share, width), F32),
            jax.ShapeDtypeStruct((4, share, width), F32),
            jax.ShapeDtypeStruct((8, width), F32),
        ],
        compiler_params=params(),
        cost_estimate=cost(tokens * width * hidden * (2 * shards + 6), 40e6),
        name="reduce",
    )(place, residual, cot, act, slope, vectors, own, *arrays)


def return_kernel(place_ref, sum_ref, g2_ref, slope_ref, ctx_ref, we_ref, wr_ref, w_ref, *refs):
    vec_ref, g1_ref, dctx_ref, dwo_ref, small_ref = refs
    shards = we_ref.shape[0]

    @pl.when(pl.program_id(0) == 0)
    def _():
        dwo_ref[...] = jnp.zeros_like(dwo_ref)
        small_ref[...] = jnp.zeros_like(small_ref)

    half = sum_ref.shape[0] // 2
    halves = [slice(0, half), slice(half, 2 * half)]
    gain_one = vec_ref[1:2]
    low = [g2_ref[at, :].astype(BF16) for at in halves]
    items = [(s, i) for s in range(shards) for i in range(2)]
    total = [g2_ref[at, :] for at in halves]
    ahead = dot(low[0], wr_ref[0], 1, 1)
    for n, (s, i) in enumerate(items):
        grad_active = ahead
        if n + 1 < len(items):
            s_next, i_next = items[n + 1]
            ahead = dot(low[i_next], wr_ref[s_next], 1, 1)
        grad_hidden = (grad_active * slope_ref[s, halves[i], :].astype(F32)).astype(BF16)
        total[i] = total[i] + dot(grad_hidden, we_ref[s], 1, 1)
    small = [jnp.zeros((1, sum_ref.shape[1]), F32)] * 3
    one = []
    for at, grad_normed in zip(halves, total):
        norm_one, inverse_one = norm_forward(sum_ref[at, :])
        grad_one = norm_backward(grad_normed, gain_one, norm_one, inverse_one)
        g1_ref[at, :] = grad_one
        one.append(grad_one.astype(BF16))
        small[0] = small[0] + column_sum(grad_one)
        small[1] = small[1] + column_sum(grad_normed * norm_one)
        small[2] = small[2] + column_sum(grad_normed)
    one = jnp.concatenate(one, axis=0)
    dctx = dot(w_ref[...], one, 1, 1)
    dwo_ref[...] += dot(flat(ctx_ref[...]), one, 1, 0)
    dctx_ref[...] = dctx.astype(BF16).reshape(dctx_ref.shape)
    for n, part in enumerate(small):
        small_ref[n : n + 1] += part


def back_to_context(place, residual, grad_two, slope, ctx, w_expand, w_reduce, weights, vectors):
    tokens, width = residual.shape
    shards, _, hidden = w_expand.shape
    every = ctx.shape[0]
    heads = every // shards
    block = 512
    by_token = lambda: pl.BlockSpec((block, width), lambda i, *_: (i, 0))
    return pl.pallas_call(
        return_kernel,
        grid_spec=pltpu.PrefetchScalarGridSpec(
            num_scalar_prefetch=1,
            grid=(tokens // block,),
            in_specs=[
                by_token(),
                by_token(),
                pl.BlockSpec((shards, block, hidden), lambda i, *_: (0, i, 0)),
                own_block(heads, HD, block),
                whole(w_expand.shape),
                whole(w_reduce.shape),
                whole(weights.shape),
                whole(vectors.shape),
            ],
            out_specs=[
                by_token(),
                pl.BlockSpec((every, HD, block), lambda i, *_: (0, 0, i)),
                whole((heads * HD, width)),
                whole((8, width)),
            ],
        ),
        out_shape=[
            jax.ShapeDtypeStruct((tokens, width), F32),
            jax.ShapeDtypeStruct(ctx.shape, BF16),
            jax.ShapeDtypeStruct((heads * HD, width), F32),
            jax.ShapeDtypeStruct((8, width), F32),
        ],
        compiler_params=params(),
        cost_estimate=cost(tokens * width * (4 * shards * hidden + 2 * every * HD), 40e6),
        name="back_to_context",
    )(place, residual, grad_two, slope, ctx, w_expand, w_reduce, weights, vectors)


def spread_kernel(sizes, place_ref, mine_ref, other_ref, *outs):
    for plane in range(4):
        for ref, core in ((mine_ref, place_ref[0]), (other_ref, place_ref[1])):
            owner = 2 * plane + lax.rem(core, 2)
            top = 0
            for size, out_ref in zip(sizes, outs):
                put(out_ref, owner * size, ref[plane, top : top + size, :], 8)
                top += size


def spread(place, mine, other, sizes):
    width = mine.shape[2]
    shapes = [(GROUP * size, width) for size in sizes]
    return pl.pallas_call(
        lambda *refs: spread_kernel(sizes, *refs),
        grid_spec=pltpu.PrefetchScalarGridSpec(
            num_scalar_prefetch=1,
            grid=(1,),
            in_specs=[whole(mine.shape), whole(other.shape)],
            out_specs=[whole(s) for s in shapes],
        ),
        out_shape=[jax.ShapeDtypeStruct(s, F32) for s in shapes],
        compiler_params=params(),
        cost_estimate=cost(0, 16 * mine.size),
        name="spread",
    )(place, mine, other)


def spread_late_kernel(heads, place_ref, *refs):
    parts = refs[:GROUP]
    dq_ref, dk_ref, dv_ref, dwo_ref, small_ref, grad_scr = refs[GROUP:]
    height = heads * HD
    size, size_two = 3 * height // GROUP, height // GROUP
    top = size + size_two
    for i, ref in enumerate(parts):
        owner = place_ref[i]
        put(grad_scr, owner * size, ref[:size, :], 8)
        put(dwo_ref, owner * size_two, ref[size:top, :], 8)

        @pl.when(owner == 0)
        def _():
            small_ref[...] = ref[top:, :]

    for i, out_ref in enumerate((dq_ref, dk_ref, dv_ref)):
        out_ref[...] = grad_scr[i * height : (i + 1) * height, :]


def spread_late(place, parts, heads):
    share, width = parts[0].shape
    height = heads * HD
    shapes = [(height, width)] * 4 + [(16, width)]
    return pl.pallas_call(
        lambda *refs: spread_late_kernel(heads, *refs),
        grid_spec=pltpu.PrefetchScalarGridSpec(
            num_scalar_prefetch=1,
            grid=(1,),
            in_specs=[whole(a.shape) for a in parts],
            out_specs=[whole(s) for s in shapes],
            scratch_shapes=[pltpu.VMEM((3 * height, width), F32)],
        ),
        out_shape=[jax.ShapeDtypeStruct(s, F32) for s in shapes],
        compiler_params=params(),
        cost_estimate=cost(0, 8 * parts[0].size * 8),
        name="spread_late",
    )(place, *parts)


def input_grads_kernel(place_ref, g1_ref, grad_ref, w_ref, out_ref):
    amount = place_ref[GROUP + 1 + pl.program_id(0)]
    matrix = shift_matrix(amount, g1_ref.shape[0], False)
    total = g1_ref[...] + dot(flat(grad_ref[...]), w_ref[...], 0, 0)
    out_ref[...] = dot(matrix, total.astype(BF16), 1, 0).astype(BF16)


def input_grads(place, length, grad_one, grads, weights):
    tokens, width = grad_one.shape
    every = grads.shape[0]
    by_row = lambda: pl.BlockSpec((length, width), lambda i, *_: (i, 0))
    return pl.pallas_call(
        input_grads_kernel,
        grid_spec=pltpu.PrefetchScalarGridSpec(
            num_scalar_prefetch=1,
            grid=(tokens // length,),
            in_specs=[
                by_row(),
                pl.BlockSpec((every, 3 * HD, length), lambda i, *_: (0, 0, i)),
                whole(weights.shape),
            ],
            out_specs=by_row(),
        ),
        out_shape=jax.ShapeDtypeStruct((tokens, width), BF16),
        compiler_params=params(),
        cost_estimate=cost(2 * tokens * width * (every * 3 * HD + length), 20e6),
        name="input_grads",
    )(place, grad_one, grads, weights)


def after(values, *others):
    return lax.optimization_barrier((values, others))[0]


def solution(mesh):
    peers = mesh.shape["mp"]
    lanes = mesh.shape["dp"]
    rotations = [[(i, (i + k) % peers) for i in range(peers)] for k in range(1, peers)]

    def flip(values, bits):
        return lax.ppermute(values, "dp", [(i, i ^ bits) for i in range(lanes)])

    def from_peers(piece):
        return jnp.stack([lax.ppermute(piece, "mp", perm) for perm in rotations])

    def swapped(piece, *ready):
        copies = jnp.broadcast_to(piece[None], (peers,) + piece.shape)
        got = lax.all_to_all(after(copies, *ready), "mp", 0, 0, tiled=True)
        me = lax.axis_index("mp")
        return jnp.concatenate(
            [
                lax.dynamic_slice_in_dim(got, lax.rem(me + peers - k, peers), 1, 0)
                for k in range(1, peers)
            ]
        )

    def both(near):
        return flip(near, 2), flip(near, 4)

    def corner(by_x, by_y, cut):
        return flip(by_y[:, :cut], 2), flip(by_x[:, cut:], 4)

    def listed(near, by_x, by_y, first, second, cut):
        places = ((near, 0, 0), (by_x, 1, 0), (by_y, 2, 0), (first, 3, 0), (second, 3, cut))
        return with_core(places)

    def with_core(places):
        out = []
        for array, rel, offset in places:
            out.append((array, 2 * rel, offset))
            out.append((flip(array, 1), 2 * rel + 1, offset))
        return out

    planes = [[g + c + i for i in (0, 2, 4, 6)] for g in range(0, lanes, GROUP) for c in (0, 1)]

    def swap_plane(values):
        return lax.all_to_all(values, "dp", 0, 0, tiled=True, axis_index_groups=planes)

    def sum_groups(total):
        step = GROUP
        while step < lanes:
            total = total + flip(total, step)
            step *= 2
        return total

    def partial_sums(mine, got, *ready):
        got = after(got, *ready)
        return [mine[rel] + got[rel] for rel in range(4)]

    def exchange(parts):
        return [flip(parts[rel], 2 * rel) for rel in (1, 2, 3)]

    def total_of(first, rest, *ready):
        rest = after(rest, *ready)
        return sum_groups(first + rest[0] + rest[1] + rest[2])

    def finish(arrays, *ready):
        out = []
        for array in after(arrays, *ready):
            out += [array, flip(array, 1)]
        return out

    def local(
        tokens,
        doc_lengths,
        w_query,
        b_query,
        w_key,
        w_value,
        b_value,
        w_output,
        b_output,
        gain_attn,
        shift_attn,
        w_expand,
        b_expand,
        w_reduce,
        b_reduce,
        gain_ffn,
        shift_ffn,
        cotangent,
    ):
        row_count, length, width = tokens.shape
        heads = w_query.shape[1] // HD
        hidden = w_expand.shape[1]
        count = row_count * length
        inside = lax.axis_index("dp") % GROUP
        me = lax.axis_index("mp")
        ends = jnp.cumsum(doc_lengths, axis=-1)
        longest = jnp.max(doc_lengths, axis=-1, keepdims=True)
        offset = jnp.max(jnp.where(doc_lengths == longest, ends - doc_lengths, 0), axis=-1)
        place = jnp.stack([inside ^ i for i in range(GROUP)] + [me])
        place = jnp.concatenate([place, offset]).astype(jnp.int32)

        by_head = lambda w: w.T.reshape(heads, HD, width)
        own_heads = jnp.concatenate([by_head(w_query), by_head(w_key), by_head(w_value)], axis=1)
        own_heads = own_heads.reshape(3 * heads * HD, width)
        blank = jnp.zeros((width - 2 * heads * HD,), BF16)
        own_bias = jnp.stack(
            [jnp.concatenate([b_query, b_value, blank]), b_expand]
            + [jnp.zeros((width,), BF16)] * 6
        ).astype(F32)

        def piece_of(array):
            size = array.shape[0] // GROUP
            return lax.dynamic_slice_in_dim(array, inside * size, size, 0).astype(F32)

        piece = piece_of(own_heads)
        near = from_peers(jnp.concatenate([piece, own_bias]))

        def columns(rows):
            parts = rows[:, 0, : 2 * heads * HD].reshape(-1, 2, heads, HD)
            blank = jnp.zeros((rows.shape[0], heads, HD), F32)
            return jnp.concatenate([parts[:, 0], blank, parts[:, 1]], axis=-1)[..., None]

        position = (jnp.arange(length, dtype=jnp.int32)[None] + offset[:, None]) % length
        segment = jnp.sum((position[:, :, None] >= ends[:, None, :]).astype(jnp.int32), axis=-1)
        segment = segment.reshape(1, count)
        docs = doc_lengths.shape[1]
        label = jnp.arange(EXTRA, dtype=jnp.int32)[:, None]
        is_doc = label < docs
        qf = jnp.where(is_doc & (segment == label), 1.0, 0.0).astype(BF16)
        kf = jnp.where(
            is_doc,
            jnp.where(segment == label, 0.0, MASK),
            jnp.where(label < docs + 3, 1.0, 0.0),
        ).astype(BF16)
        inputs, cot = shift(
            place, length, tokens.reshape(count, width), cotangent.reshape(count, width)
        )
        own = attend_own(
            length, peers, place, inputs, columns(own_bias[None])[0], qf, kf, own_heads
        )

        near = after(near, own)
        biases = near[:, -own_bias.shape[0] :]
        peer_columns = columns(biases)
        biases = jnp.concatenate([own_bias[None], biases])
        near = near[:, : -own_bias.shape[0]]
        cut = piece.shape[0] // 16 * 8
        share = jnp.concatenate([piece_of(w_expand), piece_of(w_output)])
        near_expand = swapped(share, near)
        sides = both(near)
        corners = corner(*sides, cut)
        pieces = listed(near, *sides, *corners, cut)
        near_reduce = swapped(piece_of(w_reduce), near_expand)
        sides_expand = both(after(near_expand, corners))
        weights, qkv, ctx, aug = attend_peers(
            length, peers, place, inputs, after(peer_columns, near_expand), qf, kf, pieces, own
        )

        sides_expand = after(sides_expand, ctx)
        cut = width // GROUP // 2
        corners = corner(*sides_expand, cut)
        pieces = listed(near_expand, *sides_expand, *corners, cut)
        far_reduce = [flip(near_reduce, bits) for bits in (2, 4, 6)]
        vectors = jnp.stack(
            [b_output, gain_attn, shift_attn, b_reduce, gain_ffn, shift_ffn]
            + [jnp.zeros((width,), BF16)] * 2
        ).astype(F32)
        residual, act, slope, all_expand, all_output = expand(
            place,
            inputs,
            ctx,
            after(biases, near_reduce),
            vectors,
            w_expand,
            w_output,
            pieces,
            peers,
        )
        far_reduce = after(far_reduce, residual)
        pieces = with_core([(array, rel, 0) for rel, array in enumerate([near_reduce] + far_reduce)])
        shifted, grad_two, all_reduce, mine, send, small_one = reduce(
            place, residual, cot, act, slope, vectors, w_reduce, pieces
        )
        got = flip(send, 1)
        output = unshift(place, length, shifted)
        chip = mine + after(got, output)
        early = swap_plane(chip)
        grad_one, dctx, dwo, small = back_to_context(
            place,
            residual,
            grad_two,
            slope,
            ctx,
            all_expand,
            all_reduce,
            all_output,
            after(vectors, chip),
        )
        total = sum_groups(jnp.sum(after(early, grad_one), axis=0))
        copies = jnp.broadcast_to(total[None], (4,) + total.shape)
        early = swap_plane(copies)

        dqkv, mine, send = attend_back_own(
            length, place, qkv, ctx, aug, dctx, after(kf, copies), inputs, dwo, small, small_one
        )
        got = flip(send, 1)
        dqkv = attend_back(length, peers, 1, 1, place, qkv, ctx, aug, dctx, kf, dqkv)
        parts = partial_sums(mine, got, dqkv)
        rest = exchange(parts)
        dqkv = attend_back(
            length, peers, 2, peers - 2, place, qkv, ctx, aug, dctx, after(kf, parts), dqkv
        )
        total = total_of(parts[0], rest, dqkv)
        early = after(early, total)
        second = [total] + exchange([None] + [total] * 3)
        grad_tokens = input_grads(place, length, after(grad_one, total), dqkv, weights)
        second = finish(second, grad_tokens)
        dwe, dwr = spread(place, early, flip(early, 1), [width // GROUP, hidden // GROUP])
        dq, dk, dv, dwo, small_two = spread_late(place, second, heads)
        sums = lambda i: small_two[3 : 3 + heads, i * HD : (i + 1) * HD].reshape(heads * HD)
        shape = (row_count, length, width)
        return (
            output.reshape(shape),
            grad_tokens.reshape(shape),
            dq.T,
            sums(0),
            dk.T,
            dv.T,
            sums(2),
            dwo,
            small_two[0],
            small_two[1],
            small_two[2],
            dwe,
            small_two[11],
            dwr,
            small_two[8],
            small_two[9],
            small_two[10],
        )

    rows, split = P("dp", None, None), P(None, "mp")
    return jax.shard_map(
        local,
        mesh=mesh,
        in_specs=(
            rows,
            P("dp", None),
            split,
            P("mp"),
            split,
            split,
            P("mp"),
            P("mp", None),
            P(),
            P(),
            P(),
            split,
            P("mp"),
            P("mp", None),
            P(),
            P(),
            P(),
            rows,
        ),
        out_specs=(
            rows,
            rows,
            split,
            P("mp"),
            split,
            split,
            P("mp"),
            P("mp", None),
            P(),
            P(),
            P(),
            split,
            P("mp"),
            P("mp", None),
            P(),
            P(),
            P(),
        ),
        check_vma=False,
    )
```

time: 401 us -> 363 us (0.905); the launches traced: 400 us -> 357 us
  Pallas kernels: 235 us -> 207 us
  between operations: 14.8 us -> 1.57 us
  starting transfers between devices: 43.1 us -> 48.8 us
  waiting for transfers between devices: 70.9 us -> 65.6 us
    pallas_call x12, Pallas kernels: 226 us -> 202 us  [the longest x1 37.7 us: reduce(): pl.pallas_call(lambda *refs: reduce_kernel(spots, *refs), grid_spec=pltpu...]
    all_to_all x2 -> x4, starting transfers between devices: 7.52 us -> 16.2 us  [the longest x2 8.26 us: swapped(): got = lax.all_to_all(after(copies, *ready), 'mp', 0, 0, tiled=True)]
    ppermute x3, waiting for transfers between devices: 7.94 us -> 0.01 us  [from_peers(): return jnp.stack([lax.ppermute(piece, 'mp', perm) for perm in rotations])]
    all_to_all x2 -> x4, waiting for transfers between devices: 0.01 us -> 4.64 us  [the longest x2 4.64 us: swapped(): got = lax.all_to_all(after(copies, *ready), 'mp', 0, 0, tiled=True)]
    pallas_call x2 -> x1, Pallas kernels: 9.62 us -> 5.51 us  [spread(): pl.pallas_call(lambda *refs: spread_kernel(sizes, *refs), grid_spec=pltpu...]
    ppermute x47 -> x38, starting transfers between devices: 29.4 us -> 26.5 us  [flip(): return lax.ppermute(values, 'dp', [(i, i ^ bits) for i in range(lanes)])]
    ppermute x47 -> x38, waiting for transfers between devices: 62.9 us -> 61 us  [flip(): return lax.ppermute(values, 'dp', [(i, i ^ bits) for i in range(lanes)])]
    add x4 -> x3, other arithmetic: 8.16 us -> 7.27 us  [the longest x1 3.48 us: local(): chip = mine + after(got, output)]
  transfers between devices with their start and end apart: 53 -> 45, of which waited for: 17 -> 15; matrix products, arithmetic and copies ran while one was open for 7% -> 6% of each run, Pallas kernels for 41% -> 43%
where the time goes in v3:
time: 363 us; the launch traced here: 357 us
  Pallas kernels  207 us (57%)
  waiting for transfers between devices  65.6 us (18%)
  starting transfers between devices  48.8 us (13%)
  local copies, waits for them, and re-layouts  19.3 us (5%)
  other arithmetic  15 us (4%)
    ppermute x38, waiting for transfers between devices, flip(): return lax.ppermute(values, 'dp', [(i, i ^ bits) for i in range(lanes)])  61 us
    pallas_call x1, Pallas kernels, reduce(): pl.pallas_call(lambda *refs: reduce_kernel(spots, *refs), grid_spec=pltpu...  37.7 us
    pallas_call x1, Pallas kernels, back_to_context(): pl.pallas_call(return_kernel, grid_spec=pltpu.PrefetchScalarGridSpec(num_...  33.6 us
    pallas_call x1, Pallas kernels, expand(): pl.pallas_call(lambda *refs: expand_kernel(spots, *refs), grid_spec=pltpu...  31.9 us
    ppermute x38, starting transfers between devices, flip(): return lax.ppermute(values, 'dp', [(i, i ^ bits) for i in range(lanes)])  26.5 us
    pallas_call x1, Pallas kernels, attend_peers(): pl.pallas_call(lambda *refs: attend_peers_kernel(spots, *refs), grid_spec...  22.7 us
    pallas_call x2, Pallas kernels, attend_back(): pl.pallas_call(attend_back_kernel, grid_spec=pltpu.PrefetchScalarGridSpec...  20.9 us
    pallas_call x1, Pallas kernels, input_grads(): pl.pallas_call(input_grads_kernel, grid_spec=pltpu.PrefetchScalarGridSpec...  16.2 us
  transfers between devices with their start and end apart: 45, of which 15 were waited for; matrix products, arithmetic and copies ran while one was open for 6% of the time, Pallas kernels for 43%

profile of v3, /device:TPU:0, one launch (start us, length us, event | category | flops | bytes accessed | tf_op | source)
XLA Modules:
  0.0 357.5 jit_solution(16275155923777844256)
XLA Ops:
  3.5 5.1 %collective-permute-start.2 = (f32[80,768]{1,0:T(8,128)S(1)}, f32[80,768]{1,0:T(8,128)S(1)}, u32[]{:S(2)}, u32[]{:S(2)}) collective-permute-start(f32[80,768]{1,0:T(8,128)S(1)} %concatenate.48), channel_id=1, source_target_pairs={{0,3},{1,0},{2,1},{3,2},{4,7},{5,4},{6,5},{7,6},{8,11},{9,8},{10,9... | collective-permute-start | bytes 737288 | tf_op jit(solution)/shard_map/ppermute | solution.py:834
  13.7 7.7 %shift.1 = (bf16[2048,768]{1,0:T(8,128)(2,1)}, bf16[2048,768]{1,0:T(8,128)(2,1)}) custom-call(s32[13]{0:T(128)} %concatenate.44.place_ref.refs_0_, bf16[2048,768]{1,0:T(8,128)(2,1)} %bitcast.63, bf16[2048,768]{1,0:T(8,128)(2,1)} %bitcast.64), custom_call_target="tpu_custom_call" | custom-call | flops 3221225472 | bytes 12000000 | tf_op jit(solution)/shard_map/shift/pallas_call | solution.py:93
  21.4 8.7 %attend_own.1 = (bf16[2304,768]{1,0:T(8,128)(2,1)}, bf16[12,192,2048]{2,1,0:T(8,128)(2,1)}, bf16[12,64,2048]{2,1,0:T(8,128)(2,1)}, bf16[12,16,2048]{2,1,0:T(8,128)(2,1)}) custom-call(s32[13]{0:T(128)} %concatenate.44.place_ref.refs_0_, bf16[2048,768]{1,0:T(8,128)(2,1)} %get-tuple-element.78.x_ref.refs_1_.refs_0_, ...), custom_call_target="tpu_custom_call" | custom-call | flops 5033164800 | bytes 12000000 | tf_op jit(solution)/shard_map/attend_own/pallas_call | solution.py:185
  34.1 4.1 %all-to-all-start = ((f32[4,120,768]{2,1,0:T(8,128)}), f32[4,120,768]{2,1,0:T(8,128)S(1)}, u32[]{:S(2)}, u32[]{:S(2)}) async-start(f32[4,120,768]{2,1,0:T(8,128)} %broadcast_in_dim.87), calls=%async_computation | async-start | bytes 2949120 | tf_op jit(solution)/shard_map/all_to_all | solution.py:838
  41.2 13.0 %collective-permute-done.4.refs_7_ = f32[3,72,768]{2,1,0:T(8,128)S(1)} collective-permute-done((f32[3,72,768]{2,1,0:T(8,128)}, f32[3,72,768]{2,1,0:T(8,128)S(1)}, u32[]{:S(2)}, u32[]{:S(2)}) %collective-permute-start.4) | collective-permute-done | bytes 663584 | tf_op jit(solution)/shard_map/ppermute | solution.py:831
  60.1 7.3 %collective-permute-done.8.refs_11_ = f32[3,32,768]{2,1,0:T(8,128)S(1)} collective-permute-done((f32[3,32,768]{2,1,0:T(8,128)S(1)}, f32[3,32,768]{2,1,0:T(8,128)S(1)}, u32[]{:S(2)}, u32[]{:S(2)}) %collective-permute-start.8) | collective-permute-done | bytes 294944 | tf_op jit(solution)/shard_map/ppermute | solution.py:831
  67.9 4.6 %all-to-all-done = f32[4,120,768]{2,1,0:T(8,128)S(1)} async-done(((f32[4,120,768]{2,1,0:T(8,128)}), f32[4,120,768]{2,1,0:T(8,128)S(1)}, u32[]{:S(2)}, u32[]{:S(2)}) %all-to-all-start) | async-done | bytes 1474592 | tf_op jit(solution)/shard_map/all_to_all | solution.py:838
  74.8 4.2 %all-to-all-start.1 = ((f32[4,96,768]{2,1,0:T(8,128)}), f32[4,96,768]{2,1,0:T(8,128)S(1)}, u32[]{:S(2)}, u32[]{:S(2)}) async-start(f32[4,96,768]{2,1,0:T(8,128)} %broadcast_in_dim.88), calls=%async_computation.1 | async-start | bytes 2359296 | tf_op jit(solution)/shard_map/all_to_all | solution.py:838
  83.4 22.7 %attend_peers.1 = (bf16[2304,768]{1,0:T(8,128)(2,1)}, bf16[12,192,2048]{2,1,0:T(8,128)(2,1)}, bf16[12,64,2048]{2,1,0:T(8,128)(2,1)}, bf16[12,16,2048]{2,1,0:T(8,128)(2,1)}) custom-call(s32[13]{0:T(128)} %concatenate.44.place_ref.refs_0_, ...), custom_call_target="tpu_custom_call", output_to_operand_aliasing={{0}: (15, {}), {1}: (16, {}), {2}: (17, {}), {3}: (18, {})} | custom-call | flops 15099494400 | bytes 30000000 | tf_op jit(solution)/shard_map/attend_peers/pallas_call | solution.py:231
  111.9 11.1 %collective-permute-done.19.refs_15_ = f32[3,72,768]{2,1,0:T(8,128)} collective-permute-done((f32[3,72,768]{2,1,0:T(8,128)S(1)}, f32[3,72,768]{2,1,0:T(8,128)}, u32[]{:S(2)}, u32[]{:S(2)}) %collective-permute-start.19) | collective-permute-done | bytes 663584 | tf_op jit(solution)/shard_map/ppermute | solution.py:831
  128.8 31.9 %expand.1 = (f32[2048,768]{1,0:T(8,128)}, bf16[4,2048,768]{2,1,0:T(8,128)(2,1)}, bf16[4,2048,768]{2,1,0:T(8,128)(2,1)}, bf16[4,768,768]{2,1,0:T(8,128)(2,1)}, bf16[768,768]{1,0:T(8,128)(2,1)}) custom-call(s32[13]{0:T(128)} %concatenate.44.place_ref.refs_0_, bf16[2048,768]{1,0:T(8,128)(2,1)} %get-tuple-element.78.x_ref.refs_1_.refs_0_, ...), custom_call_target="tpu_custom_call" | custom-call | flops 12079595520 | bytes 40000000 | tf_op jit(solution)/shard_map/expand/pallas_call | solution.py:491
  160.7 6.1 %collective-permute-done.23.refs_11_ = f32[3,96,768]{2,1,0:T(8,128)S(1)} collective-permute-done((f32[3,96,768]{2,1,0:T(8,128)S(1)}, f32[3,96,768]{2,1,0:T(8,128)S(1)}, u32[]{:S(2)}, u32[]{:S(2)}) %collective-permute-start.23) | collective-permute-done | bytes 884768 | tf_op jit(solution)/shard_map/ppermute | solution.py:831
  172.7 37.7 %reduce.19 = (bf16[2048,768]{1,0:T(8,128)(2,1)}, f32[2048,768]{1,0:T(8,128)}, bf16[4,768,768]{2,1,0:T(8,128)(2,1)}, f32[4,192,768]{2,1,0:T(8,128)}, f32[4,192,768]{2,1,0:T(8,128)}, /*index=5*/f32[8,768]{1,0:T(8,128)}) custom-call(s32[13]{0:T(128)} %concatenate.44.place_ref.refs_0_, f32[2048,768]{1,0:T(8,128)} %get-tuple-element.92.refs_1_.sum_ref, ...), custom_call_target="tpu_custom_call" | custom-call | flops 16911433728 | bytes 40000000 | tf_op jit(solution)/shard_map/reduce/pallas_call | solution.py:604
  210.7 6.2 %unshift.1 = bf16[2048,768]{1,0:T(8,128)(2,1)} custom-call(s32[13]{0:T(128)} %concatenate.44.place_ref.refs_0_, bf16[2048,768]{1,0:T(8,128)(2,1)} %get-tuple-element.99.in_ref), custom_call_target="tpu_custom_call" | custom-call | flops 1610612736 | bytes 6000000 | tf_op jit(solution)/shard_map/unshift/pallas_call | solution.py:117
  224.2 33.6 %back_to_context.1 = (f32[2048,768]{1,0:T(8,128)}, bf16[12,64,2048]{2,1,0:T(8,128)(2,1)}, f32[192,768]{1,0:T(8,128)}, f32[8,768]{1,0:T(8,128)}) custom-call(s32[13]{0:T(128)} %concatenate.44.place_ref.refs_0_, f32[2048,768]{1,0:T(8,128)} %get-tuple-element.92.refs_1_.sum_ref, f32[2048,768]{1,0:T(8,128)} %get-tuple-element.100.g2_ref, ...), custom_call_target="tpu_custom_call" | custom-call | flops 21743271936 | bytes 40000000 | tf_op jit(solution)/shard_map/back_to_context/pallas_call | solution.py:690
  259.6 11.8 %attend_back_own.1 = (bf16[12,192,2048]{2,1,0:T(8,128)(2,1)}, f32[4,112,768]{2,1,0:T(8,128)}, f32[4,112,768]{2,1,0:T(8,128)}) custom-call(s32[13]{0:T(128)} %concatenate.44.place_ref.refs_0_, bf16[12,192,2048]{2,1,0:T(8,128)(2,1)} %get-tuple-element.109.qkv_ref, bf16[12,64,2048]{2,1,0:T(8,128)(2,1)} %get-tuple-element.86.refs_2_.ctx_ref, ...), custom_call_target="tpu_custom_call" | custom-call | flops 5838471168 | bytes 12000000 | tf_op jit(solution)/shard_map/attend_back_own/pallas_call | solution.py:350
  271.8 4.1 %all-to-all-start.3 = ((f32[4,192,768]{2,1,0:T(8,128)}), f32[4,192,768]{2,1,0:T(8,128)S(1)}, u32[]{:S(2)}, u32[]{:S(2)}) async-start(f32[4,192,768]{2,1,0:T(8,128)} %broadcast_in_dim.89), calls=%async_computation.3 | async-start | bytes 4718592 | tf_op jit(solution)/shard_map/all_to_all | solution.py:867
  276.0 7.9 %attend_back.2.old_ref = bf16[12,192,2048]{2,1,0:T(8,128)(2,1)} custom-call(s32[13]{0:T(128)} %concatenate.44.place_ref.refs_0_, bf16[12,192,2048]{2,1,0:T(8,128)(2,1)} %get-tuple-element.109.qkv_ref, bf16[12,64,2048]{2,1,0:T(8,128)(2,1)} %get-tuple-element.86.refs_2_.ctx_ref, ...), custom_call_target="tpu_custom_call", output_to_operand_aliasing={{}: (6, {})} | custom-call | flops 4026531840 | bytes 12000000 | tf_op jit(solution)/shard_map/attend_back/pallas_call | solution.py:389
  290.0 13.1 %attend_back.3.grad_ref = bf16[12,192,2048]{2,1,0:T(8,128)(2,1)} custom-call(s32[13]{0:T(128)} %concatenate.44.place_ref.refs_0_, bf16[12,192,2048]{2,1,0:T(8,128)(2,1)} %get-tuple-element.109.qkv_ref, bf16[12,64,2048]{2,1,0:T(8,128)(2,1)} %get-tuple-element.86.refs_2_.ctx_ref, ...), custom_call_target="tpu_custom_call", output_to_operand_aliasing={{}: (6, {})} | custom-call | flops 8053063680 | bytes 12000000 | tf_op jit(solution)/shard_map/attend_back/pallas_call | solution.py:389
  303.1 10.2 %collective-permute-done.32 = f32[112,768]{1,0:T(8,128)S(1)} collective-permute-done((f32[112,768]{1,0:T(8,128)}, f32[112,768]{1,0:T(8,128)S(1)}, u32[]{:S(2)}, u32[]{:S(2)}) %collective-permute-start.32) | collective-permute-done | bytes 344096 | tf_op jit(solution)/shard_map/ppermute | solution.py:831
  313.3 5.6 %collective-permute-done.31 = f32[112,768]{1,0:T(8,128)S(1)} collective-permute-done((f32[112,768]{1,0:T(8,128)}, f32[112,768]{1,0:T(8,128)S(1)}, u32[]{:S(2)}, u32[]{:S(2)}) %collective-permute-start.31) | collective-permute-done | bytes 344096 | tf_op jit(solution)/shard_map/ppermute | solution.py:831
  323.9 16.2 %input_grads.1 = bf16[2048,768]{1,0:T(8,128)(2,1)} custom-call(s32[13]{0:T(128)} %concatenate.44.place_ref.refs_0_, f32[2048,768]{1,0:T(8,128)} %get-tuple-element.125.g1_ref, bf16[12,192,2048]{2,1,0:T(8,128)(2,1)} %attend_back.3.grad_ref, bf16[2304,768]{1,0:T(8,128)(2,1)} %get-tuple-element.126.w_ref), custom_call_target="tpu_custom_call" | custom-call | flops 8858370048 | bytes 20000000 | tf_op jit(solution)/shard_map/input_grads/pallas_call | solution.py:802
  344.2 4.0 %spread_late.1 = (f32[192,768]{1,0:T(8,128)}, f32[192,768]{1,0:T(8,128)}, f32[192,768]{1,0:T(8,128)}, f32[192,768]{1,0:T(8,128)}, f32[16,768]{1,0:T(8,128)}) custom-call(s32[13]{0:T(128)} %concatenate.44.place_ref.refs_0_, f32[112,768]{1,0:T(8,128)} %copy-done.2, f32[112,768]{1,0:T(8,128)} %copy-done.9, f32[112,768]{1,0:T(8,128)} %copy-done.8, ...), custom_call_target="tpu_custom_call" | custom-call | bytes 5505024 | tf_op jit(solution)/shard_map/spread_late/pallas_call | solution.py:775
  351.7 5.5 %spread.1 = (f32[768,768]{1,0:T(8,128)}, f32[768,768]{1,0:T(8,128)}) custom-call(s32[13]{0:T(128)} %concatenate.44.place_ref.refs_0_, f32[4,192,768]{2,1,0:T(8,128)} %copy-done, f32[4,192,768]{2,1,0:T(8,128)} %collective-permute-done.40.refs_2_), custom_call_target="tpu_custom_call" | custom-call | bytes 9437184 | tf_op jit(solution)/shard_map/spread/pallas_call | solution.py:737
  (212 shorter events, 73.4 us)
Async XLA Ops:
  3.5 28.4 %collective-permute-start.2 = (f32[80,768]{1,0:T(8,128)S(1)}, f32[80,768]{1,0:T(8,128)S(1)}, u32[]{:S(2)}, u32[]{:S(2)}) collective-permute-start(f32[80,768]{1,0:T(8,128)S(1)} %concatenate.48), channel_id=1, source_target_pairs={{0,3},{1,0},{2,1},{3,2},{4,7},{5,4},{6,5},{7,6},{8,11},{9,8},{10,9... | collective-permute-start | bytes 737288 | tf_op jit(solution)/shard_map/ppermute | solution.py:834
  8.6 23.3 %collective-permute-start.1 = (f32[80,768]{1,0:T(8,128)S(1)}, f32[80,768]{1,0:T(8,128)S(1)}, u32[]{:S(2)}, u32[]{:S(2)}) collective-permute-start(f32[80,768]{1,0:T(8,128)S(1)} %concatenate.48), channel_id=1, source_target_pairs={{0,2},{1,3},{2,0},{3,1},{4,6},{5,7},{6,4},{7,5},{8,10},{9,11},{10,... | collective-permute-start | bytes 737288 | tf_op jit(solution)/shard_map/ppermute | solution.py:834
  8.6 23.4 %collective-permute-start = (f32[80,768]{1,0:T(8,128)S(1)}, f32[80,768]{1,0:T(8,128)S(1)}, u32[]{:S(2)}, u32[]{:S(2)}) collective-permute-start(f32[80,768]{1,0:T(8,128)S(1)} %concatenate.48), channel_id=1, source_target_pairs={{0,1},{1,2},{2,3},{3,0},{4,5},{5,6},{6,7},{7,4},{8,9},{9,10},{10,1... | collective-permute-start | bytes 737288 | tf_op jit(solution)/shard_map/ppermute | solution.py:834
  34.1 38.4 %all-to-all-start = ((f32[4,120,768]{2,1,0:T(8,128)}), f32[4,120,768]{2,1,0:T(8,128)S(1)}, u32[]{:S(2)}, u32[]{:S(2)}) async-start(f32[4,120,768]{2,1,0:T(8,128)} %broadcast_in_dim.87), calls=%async_computation | async-start | bytes 2949120 | tf_op jit(solution)/shard_map/all_to_all | solution.py:838
  56.8 23.5 %collective-permute-start.3 = (f32[3,72,768]{2,1,0:T(8,128)}, f32[3,72,768]{2,1,0:T(8,128)}, u32[]{:S(2)}, u32[]{:S(2)}) collective-permute-start(f32[3,72,768]{2,1,0:T(8,128)} %slice.94.refs_5_), channel_id=1, source_target_pairs={{0,4},{4,0},{8,12},{12,8},{16,20},{20,16},{24,28},{28,24},{1,5},{5... | collective-permute-start | bytes 1990664 | tf_op jit(solution)/shard_map/ppermute | solution.py:831
  59.5 23.9 %collective-permute-start.7 = (f32[3,72,768]{2,1,0:T(8,128)}, f32[3,72,768]{2,1,0:T(8,128)}, u32[]{:S(2)}, u32[]{:S(2)}) collective-permute-start(f32[3,72,768]{2,1,0:T(8,128)} %collective-permute-done.6.refs_9_), channel_id=1, source_target_pairs={{0,4},{4,0},{8,12},{12,8},{16,20},{20,16},{24,28},{28,24},{1,5},{5... | collective-permute-start | bytes 1990664 | tf_op jit(solution)/shard_map/ppermute | solution.py:831
  59.8 23.7 %collective-permute-start.5 = (f32[3,72,768]{2,1,0:T(8,128)}, f32[3,72,768]{2,1,0:T(8,128)}, u32[]{:S(2)}, u32[]{:S(2)}) collective-permute-start(f32[3,72,768]{2,1,0:T(8,128)} %copy-done.12), channel_id=1, source_target_pairs={{0,4},{4,0},{8,12},{12,8},{16,20},{20,16},{24,28},{28,24},{1,5},{5... | collective-permute-start | bytes 1990664 | tf_op jit(solution)/shard_map/ppermute | solution.py:831
  74.8 50.2 %all-to-all-start.1 = ((f32[4,96,768]{2,1,0:T(8,128)}), f32[4,96,768]{2,1,0:T(8,128)S(1)}, u32[]{:S(2)}, u32[]{:S(2)}) async-start(f32[4,96,768]{2,1,0:T(8,128)} %broadcast_in_dim.88), calls=%async_computation.1 | async-start | bytes 2359296 | tf_op jit(solution)/shard_map/all_to_all | solution.py:838
  80.3 25.8 %collective-permute-start.14 = (f32[3,120,768]{2,1,0:T(8,128)S(1)}, f32[3,120,768]{2,1,0:T(8,128)}, u32[]{:S(2)}, u32[]{:S(2)}) collective-permute-start(f32[3,120,768]{2,1,0:T(8,128)S(1)} %copy-done.4), channel_id=1, source_target_pairs={{0,16},{4,20},{8,24},{12,28},{16,0},{20,4},{24,8},{28,12},{1,17},{... | collective-permute-start | bytes 3317768 | tf_op jit(solution)/shard_map/ppermute | solution.py:831
  81.9 25.2 %collective-permute-start.13 = (f32[3,120,768]{2,1,0:T(8,128)S(1)}, f32[3,120,768]{2,1,0:T(8,128)}, u32[]{:S(2)}, u32[]{:S(2)}) collective-permute-start(f32[3,120,768]{2,1,0:T(8,128)S(1)} %copy-done.4), channel_id=1, source_target_pairs={{0,8},{4,12},{8,0},{12,4},{16,24},{20,28},{24,16},{28,20},{1,9},{5... | collective-permute-start | bytes 3317768 | tf_op jit(solution)/shard_map/ppermute | solution.py:831
  108.8 19.4 %collective-permute-start.15 = (f32[3,120,768]{2,1,0:T(8,128)}, f32[3,120,768]{2,1,0:T(8,128)}, u32[]{:S(2)}, u32[]{:S(2)}) collective-permute-start(f32[3,120,768]{2,1,0:T(8,128)} %collective-permute-done.13.refs_9_), channel_id=1, source_target_pairs={{0,4},{4,0},{8,12},{12,8},{16,20},{20,16},{24,28},{28,24},{1,5},{5... | collective-permute-start | bytes 3317768 | tf_op jit(solution)/shard_map/ppermute | solution.py:831
  109.3 19.4 %collective-permute-start.16 = (f32[3,120,768]{2,1,0:T(8,128)}, f32[3,120,768]{2,1,0:T(8,128)}, u32[]{:S(2)}, u32[]{:S(2)}) collective-permute-start(f32[3,120,768]{2,1,0:T(8,128)} %collective-permute-done.14.refs_11_), channel_id=1, source_target_pairs={{0,4},{4,0},{8,12},{12,8},{16,20},{20,16},{24,28},{28,24},{1,5},{5... | collective-permute-start | bytes 3317768 | tf_op jit(solution)/shard_map/ppermute | solution.py:831
  125.2 35.5 %collective-permute-start.24 = (f32[3,96,768]{2,1,0:T(8,128)S(1)}, f32[3,96,768]{2,1,0:T(8,128)S(1)}, u32[]{:S(2)}, u32[]{:S(2)}) collective-permute-start(f32[3,96,768]{2,1,0:T(8,128)S(1)} %pad_maximum_fusion.2.refs_7_), channel_id=1, source_target_pairs={{0,24},{4,28},{8,16},{12,20},{16,8},{20,12},{24,0},{28,4},{1,25},{... | collective-permute-start | bytes 2654216 | tf_op jit(solution)/shard_map/ppermute | solution.py:831
  127.2 39.6 %collective-permute-start.23 = (f32[3,96,768]{2,1,0:T(8,128)S(1)}, f32[3,96,768]{2,1,0:T(8,128)S(1)}, u32[]{:S(2)}, u32[]{:S(2)}) collective-permute-start(f32[3,96,768]{2,1,0:T(8,128)S(1)} %pad_maximum_fusion.2.refs_7_), channel_id=1, source_target_pairs={{0,16},{4,20},{8,24},{12,28},{16,0},{20,4},{24,8},{28,12},{1,17},{... | collective-permute-start | bytes 2654216 | tf_op jit(solution)/shard_map/ppermute | solution.py:831
  128.2 38.5 %collective-permute-start.22 = (f32[3,96,768]{2,1,0:T(8,128)S(1)}, f32[3,96,768]{2,1,0:T(8,128)S(1)}, u32[]{:S(2)}, u32[]{:S(2)}) collective-permute-start(f32[3,96,768]{2,1,0:T(8,128)S(1)} %pad_maximum_fusion.2.refs_7_), channel_id=1, source_target_pairs={{0,8},{4,12},{8,0},{12,4},{16,24},{20,28},{24,16},{28,20},{1,9},{5... | collective-permute-start | bytes 2654216 | tf_op jit(solution)/shard_map/ppermute | solution.py:831
  128.8 38.6 %collective-permute-start.21 = (f32[3,96,768]{2,1,0:T(8,128)S(1)}, f32[3,96,768]{2,1,0:T(8,128)}, u32[]{:S(2)}, u32[]{:S(2)}) collective-permute-start(f32[3,96,768]{2,1,0:T(8,128)S(1)} %pad_maximum_fusion.2.refs_7_), channel_id=1, source_target_pairs={{0,4},{4,0},{8,12},{12,8},{16,20},{20,16},{24,28},{28,24},{1,5},{5... | collective-permute-start | bytes 2654216 | tf_op jit(solution)/shard_map/ppermute | solution.py:831
  220.4 37.5 %all-to-all-start.2 = ((f32[4,192,768]{2,1,0:T(8,128)}), f32[4,192,768]{2,1,0:T(8,128)S(1)}, u32[]{:S(2)}, u32[]{:S(2)}) async-start(f32[4,192,768]{2,1,0:T(8,128)} %add.115), calls=%async_computation.2 | async-start | bytes 4718592 | tf_op jit(solution)/shard_map/all_to_all | solution.py:867
  271.8 48.4 %all-to-all-start.3 = ((f32[4,192,768]{2,1,0:T(8,128)}), f32[4,192,768]{2,1,0:T(8,128)S(1)}, u32[]{:S(2)}, u32[]{:S(2)}) async-start(f32[4,192,768]{2,1,0:T(8,128)} %broadcast_in_dim.89), calls=%async_computation.3 | async-start | bytes 4718592 | tf_op jit(solution)/shard_map/all_to_all | solution.py:867
  286.6 26.8 %collective-permute-start.32 = (f32[112,768]{1,0:T(8,128)}, f32[112,768]{1,0:T(8,128)S(1)}, u32[]{:S(2)}, u32[]{:S(2)}) collective-permute-start(f32[112,768]{1,0:T(8,128)} %get-tuple-element.147), channel_id=1, source_target_pairs={{0,24},{4,28},{8,16},{12,20},{16,8},{20,12},{24,0},{28,4},{1,25},{... | collective-permute-start | bytes 1032200 | tf_op jit(solution)/shard_map/ppermute | solution.py:831
  289.5 29.5 %collective-permute-start.31 = (f32[112,768]{1,0:T(8,128)}, f32[112,768]{1,0:T(8,128)S(1)}, u32[]{:S(2)}, u32[]{:S(2)}) collective-permute-start(f32[112,768]{1,0:T(8,128)} %get-tuple-element.148), channel_id=1, source_target_pairs={{0,16},{4,20},{8,24},{12,28},{16,0},{20,4},{24,8},{28,12},{1,17},{... | collective-permute-start | bytes 1032200 | tf_op jit(solution)/shard_map/ppermute | solution.py:831
  290.0 29.1 %collective-permute-start.30 = (f32[112,768]{1,0:T(8,128)S(1)}, f32[112,768]{1,0:T(8,128)}, u32[]{:S(2)}, u32[]{:S(2)}) collective-permute-start(f32[112,768]{1,0:T(8,128)S(1)} %get-tuple-element.149), channel_id=1, source_target_pairs={{0,8},{4,12},{8,0},{12,4},{16,24},{20,28},{24,16},{28,20},{1,9},{5... | collective-permute-start | bytes 1032200 | tf_op jit(solution)/shard_map/ppermute | solution.py:831
  320.3 31.4 %collective-permute-start.40 = (f32[4,192,768]{2,1,0:T(8,128)S(1)}, f32[4,192,768]{2,1,0:T(8,128)}, u32[]{:S(2)}, u32[]{:S(2)}) collective-permute-start(f32[4,192,768]{2,1,0:T(8,128)S(1)} %all-to-all-done.3.refs_1_), channel_id=1, source_target_pairs={{0,4},{4,0},{8,12},{12,8},{16,20},{20,16},{24,28},{28,24},{1,5},{5... | collective-permute-start | bytes 7077896 | tf_op jit(solution)/shard_map/ppermute | solution.py:831
  320.3 19.8 %collective-permute-start.35 = (f32[112,768]{1,0:T(8,128)S(1)}, f32[112,768]{1,0:T(8,128)S(1)}, u32[]{:S(2)}, u32[]{:S(2)}) collective-permute-start(f32[112,768]{1,0:T(8,128)S(1)} %add_add_fusion.refs_1_), channel_id=1, source_target_pairs={{0,24},{4,28},{8,16},{12,20},{16,8},{20,12},{24,0},{28,4},{1,25},{... | collective-permute-start | bytes 1032200 | tf_op jit(solution)/shard_map/ppermute | solution.py:831
  321.8 18.3 %collective-permute-start.34 = (f32[112,768]{1,0:T(8,128)S(1)}, f32[112,768]{1,0:T(8,128)S(1)}, u32[]{:S(2)}, u32[]{:S(2)}) collective-permute-start(f32[112,768]{1,0:T(8,128)S(1)} %add_add_fusion.refs_1_), channel_id=1, source_target_pairs={{0,16},{4,20},{8,24},{12,28},{16,0},{20,4},{24,8},{28,12},{1,17},{... | collective-permute-start | bytes 1032200 | tf_op jit(solution)/shard_map/ppermute | solution.py:831
  (50 other events, 638.2 us)
